TPU v7x, 32 devices: a whole 2x2x4 slice. The times are simulated.
32 devices in a mesh: groups: 2 (over x), tensor: 4 (over y, core), dp: 4 (over z).
Axes of the slice: x: 2, y: 2, z: 4, core: 2. Of those that a mesh axis runs over, the one named last changes fastest.
Arguments:
- hidden_in: bfloat16 [1024, 8192], P(('groups', 'dp'), 'tensor'), parts along dimension 0, may hold values from -6 to 6
- out_grad: bfloat16 [1024, 8192], P(('groups', 'dp'), 'tensor'), parts along dimension 0, may hold values from -6 to 6
- w_gate_up: bfloat16 [2, 28672, 8192], P(None, ('tensor', 'dp')), may hold values from -0.0625 to 0.0625
- w_down: bfloat16 [28672, 8192], P(('tensor', 'dp')), may hold values from -0.03125 to 0.03125
- feat_proj: bfloat16 [8192, 192], P('tensor'), may hold values from -0.0625 to 0.0625
- unit_proj: bfloat16 [28672, 192], P(('tensor', 'dp')), may hold values from -0.03125 to 0.03125
- precond: float32 [3, 4096, 4096], P(None, ('tensor', 'dp')), may hold values from -20 to 20
Outputs:
- precond_grad: float32 [3, 8, 4096], P(None, 'groups', ('tensor', 'dp')), parts along dimension 1
There are 2 independent parts, one for each index of `groups`. A program takes and returns all parts, laid end to end along the dimension named above; an argument that names none is the same for every part. Nothing has to cross between parts.
All inputs are finite; a program needn't handle non-finite values.
Results may differ from a plain program's by a relative error of at most 0.0029.
Values may be sent and summed in bfloat16 or wider, within the bound.
No kernel may reach another device: no remote copies, remote signals or barrier semaphores. Data moves between devices by JAX's collectives and lax.ppermute only.
A program may use at most 256 MiB of HBM per device.

v0:
```python
import jax
import jax.numpy as jnp
from jax import lax
from jax.sharding import PartitionSpec as P

K = 64
SEQ = 128


contract_last = (((1,), (1,)), ((), ()))


def project_pair(rows_in, rows_out, columns):
    return jnp.concatenate(
        [
            jnp.dot(rows_in, columns[:, : 2 * K], preferred_element_type=jnp.float32),
            jnp.dot(rows_out, columns[:, 2 * K :], preferred_element_type=jnp.float32),
        ],
        axis=1,
    )


def form_sketch(in_side, out_side):
    seq_count = in_side.shape[0] // SEQ
    left_rows = in_side.reshape(seq_count, SEQ, 3, K)
    right_rows = out_side.reshape(seq_count, SEQ, 3, K)
    sketch = jnp.einsum("stwi,stwj->wsij", left_rows, right_rows, precision=lax.Precision.HIGHEST)
    sketch = sketch * SEQ ** (-0.5)
    return sketch.reshape(3, seq_count, K * K)


def local(hidden_in, out_grad, w_gate_up, w_down, feat_proj, unit_proj, precond):
    unit_width = w_down.shape[0]
    model_width = w_down.shape[1]
    w_both = w_gate_up.reshape(2 * unit_width, model_width)
    paired = jnp.stack([hidden_in, out_grad])
    tokens = hidden_in.shape[0] * lax.axis_size("dp")
    columns = lax.all_gather(feat_proj, "tensor", axis=0, tiled=True)
    feat_side = None
    rows_all = lax.all_gather(paired, "dp", axis=1, tiled=True)
    initial = [
        jnp.zeros((tokens, 2 * unit_width), jnp.float32),
        jnp.zeros((tokens, unit_width), jnp.float32),
    ]
    initial.append(jnp.zeros((tokens, 3 * K), jnp.float32))
    pieces = lax.all_gather(rows_all, "tensor", axis=2, tiled=True)
    result = [
        lax.dot_general(pieces[0], w_both, contract_last, preferred_element_type=jnp.float32),
        lax.dot_general(pieces[1], w_down, contract_last, preferred_element_type=jnp.float32),
    ]
    result.append(project_pair(pieces[0], pieces[1], columns))
    folded = tuple(result)
    pre_act = folded[0]
    hid_grad = folded[1]
    feat_side = folded[2]
    gate_pre = pre_act[:, :unit_width]
    up_pre = pre_act[:, unit_width:]
    gate_sig = jax.nn.sigmoid(gate_pre)
    silu_gate = gate_pre * gate_sig
    hidden = (silu_gate * up_pre).astype(jnp.bfloat16)
    gate_grad = (hid_grad * up_pre * gate_sig * (1.0 + gate_pre * (1.0 - gate_sig))).astype(
        jnp.bfloat16
    )
    up_grad = (hid_grad * silu_gate).astype(jnp.bfloat16)
    unit_part = jnp.concatenate(
        [
            jnp.dot(gate_grad, unit_proj[:, :K], preferred_element_type=jnp.float32),
            jnp.dot(up_grad, unit_proj[:, K : 2 * K], preferred_element_type=jnp.float32),
            jnp.dot(hidden, unit_proj[:, 2 * K :], preferred_element_type=jnp.float32),
        ],
        axis=1,
    )
    unit_side = lax.psum(unit_part, ("tensor", "dp"))
    in_side = jnp.concatenate([feat_side[:, : 2 * K], unit_side[:, 2 * K :]], axis=1)
    out_side = jnp.concatenate([unit_side[:, : 2 * K], feat_side[:, 2 * K :]], axis=1)
    sketch = form_sketch(in_side, out_side)
    return jnp.einsum("wrc,wsc->wsr", precond, sketch, precision=lax.Precision.HIGHEST)


def solution(mesh):
    in_specs = (
        P(("groups", "dp"), "tensor"),
        P(("groups", "dp"), "tensor"),
        P(None, ("tensor", "dp"), None),
        P(("tensor", "dp"), None),
        P("tensor", None),
        P(("tensor", "dp"), None),
        P(None, ("tensor", "dp"), None),
    )
    out_specs = P(None, "groups", ("tensor", "dp"))
    return jax.shard_map(local, mesh=mesh, in_specs=in_specs, out_specs=out_specs, check_vma=False)
```

profile of v0, /device:TPU:0, one launch (start us, length us, event | category | flops | bytes accessed | tf_op | source)
XLA Modules:
  0.0 386.8 jit_solution(336281864798562320)
XLA Ops:
  6.5 0.0 all-gather.4.cloned.1.call-start
  6.5 2.3 pad_maximum_fusion
  8.8 0.0 all-gather.4.cloned.1.call-update
  8.8 0.0 all-gather.6.cloned.1.call-start
  8.9 83.6 %all-gather.4.cloned.1.call-done = bf16[2,512,2048]{2,1,0:T(8,128)(2,1)} async-done(((bf16[2,128,2048]{2,1,0:T(8,128)(2,1)}), bf16[2,512,2048]{2,1,0:T(8,128)(2,1)}) %all-gather.4.cloned.1.call-update) | async-done | bytes 4194320 | tf_op jit(solution)/shard_map/all_gather | solution.py:40
  92.4 0.0 all-gather.6.cloned.1.call-update
  92.5 0.0 all-gather.8.cloned.1.call-start
  92.5 0.7 all-gather.8.cloned.1.call-update
  93.2 0.0 all-reduce.2.cloned.1.call-start
  93.3 105.2 %all-gather.6.cloned.1.call-done = bf16[2,512,8192]{2,1,0:T(8,128)(2,1)} async-done(((bf16[2,512,2048]{2,1,0:T(8,128)(2,1)}), bf16[2,512,8192]{2,1,0:T(8,128)(2,1)}) %all-gather.6.cloned.1.call-update) | async-done | bytes 16777232 | tf_op jit(solution)/shard_map/all_gather | solution.py:46
  198.5 0.0 copy-start
  198.5 38.6 %fusion = f32[512,3584]{1,0:T(8,128)} fusion(bf16[3584,8192]{1,0:T(8,128)(2,1)} %bitcast.23, bf16[2,512,8192]{2,1,0:T(8,128)(2,1)} %all-gather.6.cloned.1.call-done), kind=kOutput, calls=%fused_computation.2 | convolution fusion | flops 30064771072 | bytes 74448896 | tf_op jit(solution)/shard_map/dot_general | solution.py:48
  237.1 0.0 copy-done
  237.1 4.3 %fusion.7 = f32[512,64]{0,1:T(8,128)S(1)} fusion(f32[512,3584]{1,0:T(8,128)} %fusion, bf16[1792,192]{0,1:T(8,128)(2,1)S(1)} %copy-done), kind=kOutput, calls=%fused_computation.13 | convolution fusion | flops 122945536 | bytes 7700480 | tf_op jit(solution)/shard_map/dot_general | solution.py:69
  241.3 22.9 %fusion.3 = f32[512,1792]{1,0:T(8,128)} fusion(bf16[1792,8192]{1,0:T(8,128)(2,1)} %param.10, bf16[2,512,8192]{2,1,0:T(8,128)(2,1)} %all-gather.6.cloned.1.call-done), kind=kOutput, calls=%fused_computation.5 | convolution fusion | flops 15032385536 | bytes 41418752 | tf_op jit(solution)/shard_map/dot_general | solution.py:49
  264.3 0.0 copy-start.1
  264.3 0.0 copy-start.2
  264.3 4.4 %fusion.6 = f32[512,64]{0,1:T(8,128)S(1)} fusion(f32[512,1792]{1,0:T(8,128)} %fusion.3, f32[512,3584]{1,0:T(8,128)} %fusion, bf16[1792,192]{0,1:T(8,128)(2,1)S(1)} %copy-done), kind=kOutput, calls=%fused_computation.12 | convolution fusion | flops 122945536 | bytes 7700480 | tf_op jit(solution)/shard_map/dot_general | solution.py:68
  268.7 0.8 copy-done.1
  269.5 1.0 copy-done.2
  270.5 1.6 fusion.8
  272.1 0.8 pad_maximum_fusion.1
  272.9 0.0 all-reduce.2.cloned.1.call-update
  272.9 0.0 all-gather.8.cloned.1.call-done
  272.9 6.9 %fusion.1 = f32[512,128]{0,1:T(8,128)S(1)} fusion(bf16[2,512,8192]{2,1,0:T(8,128)(2,1)} %all-gather.6.cloned.1.call-done, bf16[8192,192]{0,1:T(8,128)(2,1)} %all-gather.8.cloned.1.call-done), kind=kOutput, calls=%fused_computation.3 | convolution fusion | flops 1073741824 | bytes 10747904 | tf_op jit(solution)/shard_map/dot_general | solution.py:16
  279.8 6.3 %fusion.2 = f32[512,64]{0,1:T(8,128)S(1)} fusion(bf16[2,512,8192]{2,1,0:T(8,128)(2,1)} %all-gather.6.cloned.1.call-done, bf16[8192,192]{0,1:T(8,128)(2,1)} %all-gather.8.cloned.1.call-done), kind=kOutput, calls=%fused_computation.4 | convolution fusion | flops 536870912 | bytes 9568256 | tf_op jit(solution)/shard_map/dot_general | solution.py:17
  286.1 77.3 %all-reduce.2.cloned.1.call-done = f32[512,192]{0,1:T(8,128)} async-done(((f32[512,192]{0,1:T(8,128)}), f32[512,192]{0,1:T(8,128)}) %all-reduce.2.cloned.1.call-update) | async-done | bytes 393232 | tf_op jit(solution)/shard_map/psum | solution.py:73
  363.4 0.9 slice.51
  364.4 0.1 reshape.13
  364.5 1.0 slice.52
  365.5 0.1 reshape.14
  365.7 0.8 convolution_multiply_fusion
  366.4 0.2 reshape.15
  366.6 13.6 %fusion.20 = f32[3,4,256]{2,1,0:T(4,128)} fusion(f32[3,4,4096]{2,1,0:T(4,128)S(1)} %reshape.15, f32[3,256,4096]{2,1,0:T(8,128)} %param.13), kind=kOutput, calls=%fused_computation.29 | convolution fusion | flops 150994944 | bytes 12791808 | tf_op jit(solution)/shard_map/wrc,wsc->wsr/dot_general | solution.py:77
  (2 shorter events, 0.1 us)
Async XLA Ops:
  6.5 85.9 %all-gather.4.cloned.1.call-start = ((), (), s32[]{:S(2)}) async-start(), calls=%async_computation | async-start | bytes 5242880 | tf_op jit(solution)/shard_map/all_gather | solution.py:40
  8.8 189.7 %all-gather.6.cloned.1.call-start = ((), (), s32[]{:S(2)}) async-start(), calls=%async_computation.1 | async-start | bytes 20971520 | tf_op jit(solution)/shard_map/all_gather | solution.py:46
  92.5 180.4 %all-gather.8.cloned.1.call-start = ((), (), s32[]{:S(2)}) async-start(), calls=%async_computation.2 | async-start | bytes 3932160 | tf_op jit(solution)/shard_map/all_gather | solution.py:38
  93.2 270.2 %all-reduce.2.cloned.1.call-start = ((), (), s32[]{:S(2)}) async-start(), calls=%async_computation.3 | async-start | bytes 786432 | tf_op jit(solution)/shard_map/psum | solution.py:73
  198.5 38.6 %copy-start = (bf16[1792,192]{0,1:T(8,128)(2,1)S(1)}, bf16[1792,192]{0,1:T(8,128)(2,1)}, u32[]{:S(2)}) copy-start(bf16[1792,192]{0,1:T(8,128)(2,1)} %param.12) | copy-start | bytes 2064388
  264.3 5.2 %copy-start.1 = (f32[512,3584]{1,0:T(8,128)S(1)}, f32[512,3584]{1,0:T(8,128)}, u32[]{:S(2)}) copy-start(f32[512,3584]{1,0:T(8,128)} %fusion) | copy-start | bytes 22020100
  264.3 6.3 %copy-start.2 = (f32[512,1792]{1,0:T(8,128)S(1)}, f32[512,1792]{1,0:T(8,128)}, u32[]{:S(2)}) copy-start(f32[512,1792]{1,0:T(8,128)} %fusion.3) | copy-start | bytes 11010052
Sparse Core Ops, SparseCore 0:
  9.0 83.4 all-gather.3
  94.0 104.4 all-gather.5
  200.1 28.5 all-gather.7
  273.0 90.3 all-reduce.1
where the time goes:
time: 387 us
  waiting for transfers between devices  267 us (69%)
  matrix products  99.3 us (26%)
  between operations  13.2 us (3%)
  local copies, waits for them, and re-layouts  4.2 us (1%)
    all_gather x1, waiting for transfers between devices, local(): pieces = lax.all_gather(rows_all, 'tensor', axis=2, tiled=True)  105 us
    all_gather x1, waiting for transfers between devices, local(): rows_all = lax.all_gather(paired, 'dp', axis=1, tiled=True)  83.6 us
    psum x1, waiting for transfers between devices, local(): unit_side = lax.psum(unit_part, ('tensor', 'dp'))  77.3 us
    dot_general x1, matrix products, local(): lax.dot_general(pieces[0], w_both, contract_last, preferred_element_type=...  38.6 us
    dot_general x1, matrix products, local(): lax.dot_general(pieces[1], w_down, contract_last, preferred_element_type=...  22.9 us
    dot_general x1, matrix products, local(): jnp.einsum('wrc,wsc->wsr', precond, sketch, precision=lax.Precision.HIGHEST)  13.6 us
  transfers between devices with their start and end apart: 4, of which 3 were waited for; matrix products, arithmetic and copies ran while one was open for 22% of the time, Pallas kernels for 0%

commit v1 on v0

v1 whole, which is shorter than its diff:
```python
import functools

import jax
import jax.numpy as jnp
from jax import lax
from jax.experimental import pallas as pl
from jax.experimental.pallas import tpu as pltpu
from jax.sharding import PartitionSpec as P

K = 64
SEQ = 128
BOTH = ("tensor", "dp")
NT = (((1,), (1,)), ((), ()))
MIB = 1 << 20


def project_pair(rows_in, rows_out, columns):
    return jnp.concatenate(
        [
            jnp.dot(rows_in, columns[:, : 2 * K], preferred_element_type=jnp.float32),
            jnp.dot(rows_out, columns[:, 2 * K :], preferred_element_type=jnp.float32),
        ],
        axis=1,
    )


def form_sketch(in_side, out_side):
    seq_count = in_side.shape[0] // SEQ
    left_rows = in_side.reshape(seq_count, SEQ, 3, K)
    right_rows = out_side.reshape(seq_count, SEQ, 3, K)
    sketch = jnp.einsum("stwi,stwj->wsij", left_rows, right_rows, precision=lax.Precision.HIGHEST)
    sketch = sketch * SEQ ** (-0.5)
    return sketch.reshape(3, seq_count, K * K)


def activations(gate_pre, up_pre, hid_grad):
    gate_sig = jax.nn.sigmoid(gate_pre)
    silu_gate = gate_pre * gate_sig
    hidden = (silu_gate * up_pre).astype(jnp.bfloat16)
    gate_grad = (hid_grad * up_pre * gate_sig * (1.0 + gate_pre * (1.0 - gate_sig))).astype(
        jnp.bfloat16
    )
    up_grad = (hid_grad * silu_gate).astype(jnp.bfloat16)
    return gate_grad, up_grad, hidden


def local_plain(hidden_in, out_grad, w_gate_up, w_down, feat_proj, unit_proj, precond):
    unit_width, model_width = w_down.shape
    w_both = w_gate_up.reshape(2 * unit_width, model_width)
    paired = jnp.stack([hidden_in, out_grad])
    columns = lax.all_gather(feat_proj, "tensor", axis=0, tiled=True)
    rows_all = lax.all_gather(paired, "dp", axis=1, tiled=True)
    pieces = lax.all_gather(rows_all, "tensor", axis=2, tiled=True)
    pre_act = lax.dot_general(pieces[0], w_both, NT, preferred_element_type=jnp.float32)
    hid_grad = lax.dot_general(pieces[1], w_down, NT, preferred_element_type=jnp.float32)
    feat_side = project_pair(pieces[0], pieces[1], columns)
    sides = activations(pre_act[:, :unit_width], pre_act[:, unit_width:], hid_grad)
    unit_part = jnp.concatenate(
        [
            jnp.dot(side, unit_proj[:, n * K : (n + 1) * K], preferred_element_type=jnp.float32)
            for n, side in enumerate(sides)
        ],
        axis=1,
    )
    unit_side = lax.psum(unit_part, BOTH)
    in_side = jnp.concatenate([feat_side[:, : 2 * K], unit_side[:, 2 * K :]], axis=1)
    out_side = jnp.concatenate([unit_side[:, : 2 * K], feat_side[:, 2 * K :]], axis=1)
    sketch = form_sketch(in_side, out_side)
    return jnp.einsum("wrc,wsc->wsr", precond, sketch, precision=lax.Precision.HIGHEST)


TENSOR = 4
ROWS = 4


def swap_with(flip):
    return [(t * ROWS + z, (t ^ flip) * ROWS + z) for t in range(TENSOR) for z in range(ROWS)]


def shift_rows(step, wrap=True):
    return [
        (t * ROWS + z, t * ROWS + (z + step) % ROWS)
        for t in range(TENSOR)
        for z in range(ROWS)
        if wrap or 0 <= z + step < ROWS
    ]


def send(value, pairs):
    return lax.ppermute(value, BOTH, pairs)


FORWARD = [(t * ROWS + a, t * ROWS + b) for t in range(TENSOR) for a, b in ((2, 3), (1, 0))]


def gather_rows(own):
    row = lax.axis_index("dp")
    from_1 = send(own, shift_rows(1, False))
    from_2 = send(own, shift_rows(2))
    from_3 = send(own, shift_rows(-1, False))
    end = send(from_2, FORWARD)
    from_1 = jnp.where(row == 0, end, from_1)
    from_3 = jnp.where(row == ROWS - 1, end, from_3)
    return jnp.concatenate([from_1, from_2, from_3], axis=1)


def matmul_kernel(blocks, tokens, first, last, *refs):
    count = len(blocks)
    refs = list(refs)
    where_ref = refs.pop(0)
    arrays = [(refs.pop(0), refs.pop(0)) for _ in range(count)]
    gate_up = [refs.pop(0) for _ in range(count)]
    down = [refs.pop(0) for _ in range(count)]
    acc_in = None if first else refs.pop(0)
    if last:
        proj_ref = refs.pop(0)
        mine_ref, theirs_ref = refs.pop(0), refs.pop(0)
    else:
        acc_out = refs.pop(0)
    rows = [refs.pop(0) for _ in range(count)]
    sems = refs.pop(0)
    step = pl.program_id(0)

    @pl.when(step == 0)
    def _():
        copies = []
        for n, (block, (own, rest)) in enumerate(zip(blocks, arrays)):
            _, offset, width, lead = block
            split = own.shape[1]
            copies.append(
                pltpu.make_async_copy(
                    own.at[:, :, pl.ds(offset, width)], rows[n].at[:, pl.ds(0, split), :], sems.at[2 * n]
                )
            )
            copies.append(
                pltpu.make_async_copy(
                    rest.at[pl.ds(lead, 2)],
                    rows[n].at[:, pl.ds(split, tokens - split), :],
                    sems.at[2 * n + 1],
                )
            )
        for copy in copies:
            copy.start()
        for copy in copies:
            copy.wait()
        if last:
            ut_ref = refs[0]
            ut_ref[...] = jnp.zeros_like(ut_ref)

    def total(which):
        value = None if first else acc_in[0, which]
        for n in range(count):
            weight = down[n][...] if which == 2 else gate_up[n][which]
            part = lax.dot_general(
                rows[n][1 if which == 2 else 0], weight, NT, preferred_element_type=jnp.float32
            )
            value = part if value is None else value + part
        return value

    if not last:
        for which in range(3):
            acc_out[0, which] = total(which)
        return
    ut_ref = refs[0]
    sides = activations(total(0), total(1), total(2))
    for n, side in enumerate(sides):
        ut_ref[pl.ds(n * K, K), :] += lax.dot_general(
            proj_ref[pl.ds(n * K, K), :], side, NT, preferred_element_type=jnp.float32
        )

    @pl.when(step == pl.num_programs(0) - 1)
    def _():
        half = mine_ref.shape[0]
        core = lax.rem(where_ref[0], 2)
        mine_ref[...] = ut_ref[pl.ds(pl.multiple_of(core * half, 8), half), :]
        theirs_ref[...] = ut_ref[pl.ds(pl.multiple_of((1 - core) * half, 8), half), :]


def matmul_step(where, blocks, arrays, w_gate_up, w_down, acc, unit_proj_t=None):
    first, last = acc is None, unit_proj_t is not None
    unit_width, model_width = w_down.shape
    own_width = model_width // TENSOR
    tokens = arrays[0][0].shape[1] + arrays[0][1].shape[1]
    tile = 256
    tiles = unit_width // tile

    def at(owner, offset, width):
        per = own_width // width
        return lambda i, at_ref: at_ref[owner] * per + offset // width

    in_specs = [pl.BlockSpec(memory_space=pl.ANY)] * (2 * len(blocks))
    operands = [a for pair in arrays for a in pair]
    for owner, offset, width, _ in blocks:
        column = at(owner, offset, width)
        in_specs.append(pl.BlockSpec((2, tile, width), lambda i, r, c=column: (0, i, c(i, r))))
        operands.append(w_gate_up)
    for owner, offset, width, _ in blocks:
        column = at(owner, offset, width)
        in_specs.append(pl.BlockSpec((tile, width), lambda i, r, c=column: (i, c(i, r))))
        operands.append(w_down)
    acc_spec = pl.BlockSpec((1, 3, tokens, tile), lambda i, r: (i, 0, 0, 0))
    acc_shape = jax.ShapeDtypeStruct((tiles, 3, tokens, tile), jnp.float32)
    aliases = {}
    if not first:
        if not last:
            aliases = {1 + len(operands): 0}
        in_specs.append(acc_spec)
        operands.append(acc)
    scratch = [pltpu.VMEM((2, tokens, width), jnp.bfloat16) for _, _, width, _ in blocks]
    scratch.append(pltpu.SemaphoreType.DMA((2 * len(blocks),)))
    if last:
        in_specs.append(pl.BlockSpec((3 * K, tile), lambda i, r: (0, i)))
        operands.append(unit_proj_t)
        half = jax.ShapeDtypeStruct((3 * K // 2, tokens), jnp.float32)
        out_shape = (half, half)
        out_specs = (pl.BlockSpec(half.shape, lambda i, r: (0, 0)),) * 2
        scratch.append(pltpu.VMEM((3 * K, tokens), jnp.float32))
    else:
        out_shape, out_specs = acc_shape, acc_spec
    depth = sum(width for _, _, width, _ in blocks)
    return pl.pallas_call(
        functools.partial(matmul_kernel, blocks, tokens, first, last),
        out_shape=out_shape,
        grid_spec=pltpu.PrefetchScalarGridSpec(
            num_scalar_prefetch=1,
            grid=(tiles,),
            in_specs=in_specs,
            out_specs=out_specs,
            scratch_shapes=scratch,
        ),
        input_output_aliases=aliases,
        compiler_params=pltpu.CompilerParams(vmem_limit_bytes=44 * MIB),
        cost_estimate=pl.CostEstimate(
            flops=2 * tokens * 3 * unit_width * depth,
            bytes_accessed=3 * unit_width * depth * 2 + 4 * depth * tokens,
            transcendentals=0,
        ),
        name="matmul",
    )(where, *operands)


def sketch_kernel(where_ref, feat_ref, mine_ref, other_ref, out_ref, unit_ref):
    half = mine_ref.shape[0]
    core = lax.rem(where_ref[0], 2)
    unit_ref[pl.ds(pl.multiple_of(core * half, 8), half), :] = mine_ref[...]
    unit_ref[pl.ds(pl.multiple_of((1 - core) * half, 8), half), :] = other_ref[...]
    for w in range(3):
        in_ref, side_ref = (feat_ref, unit_ref) if w < 2 else (unit_ref, feat_ref)
        right = side_ref[pl.ds(w * K, K), :]
        parts = [
            lax.dot_general(
                in_ref[pl.ds(w * K + odd, K // 2, stride=2), :],
                right,
                NT,
                precision=lax.Precision.HIGHEST,
                preferred_element_type=jnp.float32,
            )
            for odd in range(2)
        ]
        out_ref[w] = jnp.concatenate(parts, axis=1) * SEQ ** (-0.5)


def sketch_own(where, feat_t, mine, other):
    whole = pl.BlockSpec(memory_space=pltpu.VMEM)
    return pl.pallas_call(
        sketch_kernel,
        out_shape=jax.ShapeDtypeStruct((3, K // 2, 2 * K), jnp.float32),
        in_specs=[pl.BlockSpec(memory_space=pltpu.SMEM), whole, whole, whole],
        out_specs=whole,
        scratch_shapes=[pltpu.VMEM((3 * K, SEQ), jnp.float32)],
        name="sketch",
    )(where, feat_t, mine, other)


def precond_kernel(row_ref, p_ref, *refs):
    sketches, out_ref, sums = refs[:ROWS], refs[ROWS], refs[ROWS + 1]
    height = p_ref.shape[1]
    lanes = 2 * K
    group = 32
    ones = jnp.ones((8, lanes), jnp.float32)

    @pl.loop(0, height // group)
    def _(g):
        at = pl.ds(pl.multiple_of(g * group, group), group)
        totals = [jnp.zeros((group, lanes), jnp.float32) for _ in range(ROWS)]
        for q in range(K // 2):
            part = p_ref[0, at, pl.ds(q * lanes, lanes)]
            for n in range(ROWS):
                totals[n] = totals[n] + part * sketches[n][0, pl.ds(q, 1), :]
        for n in range(ROWS):
            sums[n, at, :] = totals[n]

    for n in range(ROWS):
        seq = lax.rem(row_ref[0] - n + ROWS, ROWS)
        line = lax.dot_general(
            ones,
            sums[n],
            NT,
            precision=lax.Precision.HIGHEST,
            preferred_element_type=jnp.float32,
        )
        out_ref[0, pl.ds(seq, 1), :] = line[:1]


def apply_precond(row, precond, sketches):
    height, order = precond.shape[1:]
    piece = pl.BlockSpec((1, K // 2, 2 * K), lambda w, r: (w, 0, 0))
    return pl.pallas_call(
        precond_kernel,
        out_shape=jax.ShapeDtypeStruct((3, ROWS, height), jnp.float32),
        grid_spec=pltpu.PrefetchScalarGridSpec(
            num_scalar_prefetch=1,
            grid=(3,),
            in_specs=[pl.BlockSpec((1, height, order), lambda w, r: (w, 0, 0))] + [piece] * ROWS,
            out_specs=pl.BlockSpec((1, ROWS, height), lambda w, r: (w, 0, 0)),
            scratch_shapes=[pltpu.VMEM((ROWS, height, 2 * K), jnp.float32)],
        ),
        compiler_params=pltpu.CompilerParams(vmem_limit_bytes=24 * MIB),
        name="precond",
    )(row, precond, *sketches)


CHUNKS = (1024, 512, 256)
A, C, Y, D = range(4)


def local_split(hidden_in, out_grad, w_gate_up, w_down, feat_proj, unit_proj, precond):
    tensor, row = lax.axis_index("tensor"), lax.axis_index("dp")
    where = jnp.stack([tensor, tensor ^ 1, tensor ^ 2, tensor ^ 3]).astype(jnp.int32)
    own = jnp.stack([hidden_in, out_grad])
    width = own.shape[2]
    other_y = send(own, swap_with(2))
    other_core = send(own, swap_with(1))
    other_both = send(other_y, swap_with(1))
    unit_proj_t = unit_proj.T

    feat_t = jnp.concatenate(
        [
            lax.dot_general(
                feat_proj[:, : 2 * K], hidden_in, (((0,), (1,)), ((), ())), preferred_element_type=jnp.float32
            ),
            lax.dot_general(
                feat_proj[:, 2 * K :], out_grad, (((0,), (1,)), ((), ())), preferred_element_type=jnp.float32
            ),
        ],
        axis=0,
    )
    feat_t = feat_t + send(feat_t, swap_with(1))
    feat_t = feat_t + send(feat_t, swap_with(2))

    acc = None
    waiting = ([], [])
    offset = 0
    for size in CHUNKS:
        rest = gather_rows(own[:, :, offset : offset + size])
        rest_core = send(rest, swap_with(1))
        rest_y = send(rest, swap_with(2))
        rest_both = send(rest_y, swap_with(1))
        blocks = waiting[0] + [(A, offset, size, 0), (C, offset, size, 0)]
        arrays = waiting[1] + [(own, rest), (other_core, rest_core)]
        acc = matmul_step(where, blocks, arrays, w_gate_up, w_down, acc)
        waiting = (
            [(Y, offset, size, 0), (D, offset, size, 0)],
            [(other_y, rest_y), (other_both, rest_both)],
        )
        offset += size
    acc = matmul_step(where, *waiting, w_gate_up, w_down, acc)
    size = width - offset
    both = jnp.concatenate([own[:, :, offset:], other_y[:, :, offset:]], axis=0)
    rest = gather_rows(both)
    rest_core = send(rest, swap_with(1))
    blocks = [(A, offset, size, 0), (Y, offset, size, 2), (C, offset, size, 0), (D, offset, size, 2)]
    arrays = [(own, rest), (other_y, rest), (other_core, rest_core), (other_both, rest_core)]
    mine, theirs = matmul_step(where, blocks, arrays, w_gate_up, w_down, acc, unit_proj_t)

    mine = mine + send(theirs, swap_with(1))
    part = mine[:, :SEQ]
    for n in range(1, ROWS):
        part = part + send(mine[:, n * SEQ : (n + 1) * SEQ], shift_rows(-n))
    part = part + send(part, swap_with(2))
    other = send(part, swap_with(1))
    sketch = sketch_own(where, feat_t, part, other)
    sketches = [sketch] + [send(sketch, shift_rows(n)) for n in range(1, ROWS)]
    return apply_precond(row.astype(jnp.int32).reshape(1), precond, sketches)


def local(hidden_in, out_grad, w_gate_up, w_down, feat_proj, unit_proj, precond):
    fits = (
        lax.axis_size("tensor") == TENSOR
        and lax.axis_size("dp") == ROWS
        and hidden_in.shape[0] == SEQ
        and w_down.shape[0] % 256 == 0
        and hidden_in.shape[1] == 2048
    )
    step = local_split if fits else local_plain
    return step(hidden_in, out_grad, w_gate_up, w_down, feat_proj, unit_proj, precond)


def solution(mesh):
    in_specs = (
        P(("groups", "dp"), "tensor"),
        P(("groups", "dp"), "tensor"),
        P(None, ("tensor", "dp"), None),
        P(("tensor", "dp"), None),
        P("tensor", None),
        P(("tensor", "dp"), None),
        P(None, ("tensor", "dp"), None),
    )
    out_specs = P(None, "groups", ("tensor", "dp"))
    return jax.shard_map(local, mesh=mesh, in_specs=in_specs, out_specs=out_specs, check_vma=False)
```

time: 387 us -> 261 us (0.67)
  waiting for transfers between devices: 267 us -> 83.9 us
  Pallas kernels: 0 us -> 110 us
  matrix products: 99.3 us -> 2.23 us
  starting transfers between devices: 0.12 us -> 47 us
  between operations: 13.2 us -> 0.44 us
  other arithmetic: 3.1 us -> 10.6 us
    all_gather x3 -> x0, waiting for transfers between devices: 189 us -> none  [the longest x1 105 us: local(): pieces = lax.all_gather(rows_all, 'tensor', axis=2, tiled=True)]
    pallas_call x0 -> x7, Pallas kernels: none -> 110 us  [the longest x5 101 us: matmul_step(): pl.pallas_call(functools.partial(matmul_kernel, blocks, tokens, first, la...]
    dot_general x9 -> x2, matrix products: 99.3 us -> 2.23 us  [the longest x1 1.25 us: local_split(): lax.dot_general(feat_proj[:, 2 * K:], out_grad, (((0,), (1,)), ((), ())),...]
    ppermute x0 -> x40, waiting for transfers between devices: none -> 83.9 us  [send(): return lax.ppermute(value, BOTH, pairs)]
    psum x1 -> x0, waiting for transfers between devices: 77.3 us -> none  [local(): unit_side = lax.psum(unit_part, ('tensor', 'dp'))]
    ppermute x0 -> x40, starting transfers between devices: none -> 47 us  [send(): return lax.ppermute(value, BOTH, pairs)]
    unnamed x6 -> x22, local copies, waits for them, and re-layouts: 1.86 us -> 6.03 us
  transfers between devices with their start and end apart: 4 -> 40, of which waited for: 3 -> 15; matrix products, arithmetic and copies ran while one was open for 22% -> 4% of each run, Pallas kernels for 0% -> 32%
where the time goes in v1:
time: 261 us; the launch traced here: 260 us
  Pallas kernels  110 us (42%)
  waiting for transfers between devices  83.9 us (32%)
  starting transfers between devices  47 us (18%)
  other arithmetic  10.6 us (4%)
  local copies, waits for them, and re-layouts  6.06 us (2%)
    pallas_call x5, Pallas kernels, matmul_step(): pl.pallas_call(functools.partial(matmul_kernel, blocks, tokens, first, la...  101 us
    ppermute x40, waiting for transfers between devices, send(): return lax.ppermute(value, BOTH, pairs)  83.9 us
    ppermute x40, starting transfers between devices, send(): return lax.ppermute(value, BOTH, pairs)  47 us
    pallas_call x1, Pallas kernels, apply_precond(): pl.pallas_call(precond_kernel, out_shape=jax.ShapeDtypeStruct((3, ROWS, h...  6.4 us
    unnamed x22, local copies, waits for them, and re-layouts  6.03 us
  transfers between devices with their start and end apart: 40, of which 15 were waited for; matrix products, arithmetic and copies ran while one was open for 4% of the time, Pallas kernels for 32%

profile of v1, /device:TPU:0, one launch (start us, length us, event | category | flops | bytes accessed | tf_op | source)
XLA Modules:
  0.0 260.0 jit_solution(7477177505007842618)
XLA Ops:
  0.0 2.0 fusion
  2.0 4.0 %collective-permute-start.23 = (bf16[2,128,1024]{2,1,0:T(8,128)(2,1)}, bf16[2,128,1024]{2,1,0:T(8,128)(2,1)}, u32[]{:S(2)}, u32[]{:S(2)}) collective-permute-start(bf16[2,128,1024]{2,1,0:T(8,128)(2,1)} %fusion), channel_id=1, source_target_pairs={{0,2},{1,3},{2,0},{3,1},{4,6},{5,7},{6,4},{7,5},{8,10},{9,11},{10,... | collective-permute-start | bytes 1572872 | tf_op jit(solution)/shard_map/ppermute | solution.py:90
  6.0 4.3 %collective-permute-start.25 = (bf16[2,128,1024]{2,1,0:T(8,128)(2,1)}, bf16[2,128,1024]{2,1,0:T(8,128)(2,1)}, u32[]{:S(2)}, u32[]{:S(2)}) collective-permute-start(bf16[2,128,1024]{2,1,0:T(8,128)(2,1)} %fusion), channel_id=1, source_target_pairs={{0,1},{1,2},{2,3},{4,5},{5,6},{6,7},{8,9},{9,10},{10,11},{12,13},{... | collective-permute-start | bytes 1572872 | tf_op jit(solution)/shard_map/ppermute | solution.py:90
  10.3 1.3 collective-permute-start.26
  11.6 18.8 %collective-permute-done.23 = bf16[2,128,1024]{2,1,0:T(8,128)(2,1)} collective-permute-done((bf16[2,128,1024]{2,1,0:T(8,128)(2,1)}, bf16[2,128,1024]{2,1,0:T(8,128)(2,1)}, u32[]{:S(2)}, u32[]{:S(2)}) %collective-permute-start.23) | collective-permute-done | bytes 524320 | tf_op jit(solution)/shard_map/ppermute | solution.py:90
  30.4 1.3 collective-permute-start.24
  31.8 1.9 collective-permute-start.2
  33.7 3.7 %collective-permute-done.26 = bf16[2,128,1024]{2,1,0:T(8,128)(2,1)} collective-permute-done((bf16[2,128,1024]{2,1,0:T(8,128)(2,1)}, bf16[2,128,1024]{2,1,0:T(8,128)(2,1)}, u32[]{:S(2)}, u32[]{:S(2)}) %collective-permute-start.26) | collective-permute-done | bytes 524320 | tf_op jit(solution)/shard_map/ppermute | solution.py:90
  37.4 9.5 %collective-permute-done.24 = bf16[2,128,1024]{2,1,0:T(8,128)(2,1)} collective-permute-done((bf16[2,128,1024]{2,1,0:T(8,128)(2,1)}, bf16[2,128,1024]{2,1,0:T(8,128)(2,1)}, u32[]{:S(2)}, u32[]{:S(2)}) %collective-permute-start.24) | collective-permute-done | bytes 524320 | tf_op jit(solution)/shard_map/ppermute | solution.py:90
  46.9 1.3 broadcast_select_fusion.1
  48.2 2.3 pad_maximum_fusion.1.refs_2_
  50.5 1.6 collective-permute-start.27
  52.6 4.9 %collective-permute-start.12 = (bf16[2,128,256]{2,1,0:T(8,128)(2,1)S(1)}, bf16[2,128,256]{2,1,0:T(8,128)(2,1)}, u32[]{:S(2)}, u32[]{:S(2)}) collective-permute-start(bf16[2,128,256]{2,1,0:T(8,128)(2,1)S(1)} %get-tuple-element.9), channel_id=1, source_target_pairs={{0,1},{1,2},{2,3},{4,5},{5,6},{6,7},{8,9},{9,10},{10,11},{12,13},{... | collective-permute-start | bytes 393224 | tf_op jit(solution)/shard_map/ppermute | solution.py:90
  57.6 8.3 %collective-permute-done.10 = bf16[2,128,256]{2,1,0:T(8,128)(2,1)} collective-permute-done((bf16[2,128,256]{2,1,0:T(8,128)(2,1)S(1)}, bf16[2,128,256]{2,1,0:T(8,128)(2,1)}, u32[]{:S(2)}, u32[]{:S(2)}) %collective-permute-start.10) | collective-permute-done | bytes 131104 | tf_op jit(solution)/shard_map/ppermute | solution.py:90
  65.9 1.3 collective-permute-start.18
  67.2 1.3 collective-permute-start.13
  68.5 5.7 %collective-permute-done.13 = bf16[2,128,256]{2,1,0:T(8,128)(2,1)} collective-permute-done((bf16[2,128,256]{2,1,0:T(8,128)(2,1)S(1)}, bf16[2,128,256]{2,1,0:T(8,128)(2,1)}, u32[]{:S(2)}, u32[]{:S(2)}) %collective-permute-start.13) | collective-permute-done | bytes 131104 | tf_op jit(solution)/shard_map/ppermute | solution.py:90
  74.2 1.3 collective-permute-start.19
  75.5 1.3 collective-permute-start.17
  77.8 1.3 collective-permute-start.11
  79.3 6.1 %collective-permute-done.19 = bf16[2,128,512]{2,1,0:T(8,128)(2,1)} collective-permute-done((bf16[2,128,512]{2,1,0:T(8,128)(2,1)S(1)}, bf16[2,128,512]{2,1,0:T(8,128)(2,1)}, u32[]{:S(2)}, u32[]{:S(2)}) %collective-permute-start.19) | collective-permute-done | bytes 262176 | tf_op jit(solution)/shard_map/ppermute | solution.py:90
  85.4 5.3 %collective-permute-done.11 = bf16[2,128,256]{2,1,0:T(8,128)(2,1)S(1)} collective-permute-done((bf16[2,128,256]{2,1,0:T(8,128)(2,1)}, bf16[2,128,256]{2,1,0:T(8,128)(2,1)S(1)}, u32[]{:S(2)}, u32[]{:S(2)}) %collective-permute-start.11) | collective-permute-done | bytes 131104 | tf_op jit(solution)/shard_map/ppermute | solution.py:90
  90.7 4.0 %collective-permute-start.5 = (bf16[4,128,256]{2,1,0:T(8,128)(2,1)S(1)}, bf16[4,128,256]{2,1,0:T(8,128)(2,1)S(1)}, u32[]{:S(2)}, u32[]{:S(2)}) collective-permute-start(bf16[4,128,256]{2,1,0:T(8,128)(2,1)S(1)} %pad_maximum_fusion.5), channel_id=1, source_target_pairs={{0,1},{1,2},{2,3},{4,5},{5,6},{6,7},{8,9},{9,10},{10,11},{12,13},{... | collective-permute-start | bytes 786440 | tf_op jit(solution)/shard_map/ppermute | solution.py:90
  96.6 6.1 %collective-permute-done.3 = bf16[4,128,256]{2,1,0:T(8,128)(2,1)S(1)} collective-permute-done((bf16[4,128,256]{2,1,0:T(8,128)(2,1)S(1)}, bf16[4,128,256]{2,1,0:T(8,128)(2,1)S(1)}, u32[]{:S(2)}, u32[]{:S(2)}) %collective-permute-start.3) | collective-permute-done | bytes 262176 | tf_op jit(solution)/shard_map/ppermute | solution.py:90
  102.7 1.3 collective-permute-start.6
  104.0 1.3 collective-permute-start.4
  105.3 1.1 broadcast_select_fusion.3
  106.5 5.6 %collective-permute-done.6 = bf16[4,128,256]{2,1,0:T(8,128)(2,1)S(1)} collective-permute-done((bf16[4,128,256]{2,1,0:T(8,128)(2,1)S(1)}, bf16[4,128,256]{2,1,0:T(8,128)(2,1)S(1)}, u32[]{:S(2)}, u32[]{:S(2)}) %collective-permute-start.6) | collective-permute-done | bytes 262176 | tf_op jit(solution)/shard_map/ppermute | solution.py:90
  112.7 4.6 %collective-permute-done.4 = bf16[4,128,256]{2,1,0:T(8,128)(2,1)S(1)} collective-permute-done((bf16[4,128,256]{2,1,0:T(8,128)(2,1)S(1)}, bf16[4,128,256]{2,1,0:T(8,128)(2,1)S(1)}, u32[]{:S(2)}, u32[]{:S(2)}) %collective-permute-start.4) | collective-permute-done | bytes 262176 | tf_op jit(solution)/shard_map/ppermute | solution.py:90
  118.9 20.4 %matmul.5.refs_17_ = f32[7,3,512,256]{3,2,1,0:T(8,128)} custom-call(s32[4]{0:T(128)S(1)} %pad_add_fusion.refs_0_.where_ref, bf16[2,128,2048]{2,1,0:T(8,128)(2,1)S(1)} %pad_maximum_fusion.refs_1_.refs_5_, bf16[2,384,1024]{2,1,0:T(8,128)(2,1)} %pad_maximum_fusion.1.refs_2_, bf16[2,128,2048]{2,1,0:T(8,128)(2,1)S(1)} %collective-permute-done.7.refs_3_.refs_7_.refs_5_, ...), custom_call_target="tpu_custom_call" | custom-call | flops 11274289152 | bytes 26214400 | tf_op jit(solution)/shard_map/matmul/pallas_call | solution.py:221
  140.5 28.1 %matmul.6.refs_17_ = f32[7,3,512,256]{3,2,1,0:T(8,128)} custom-call(s32[4]{0:T(128)S(1)} %pad_add_fusion.refs_0_.where_ref, bf16[2,128,2048]{2,1,0:T(8,128)(2,1)S(1)} %collective-permute-done.2.refs_1_.refs_3_, bf16[2,384,1024]{2,1,0:T(8,128)(2,1)} %collective-permute-done.27.refs_2_, ...), custom_call_target="tpu_custom_call", output_to_operand_aliasing={{}: (17, {})} | custom-call | flops 16911433728 | bytes 39321600 | tf_op jit(solution)/shard_map/matmul/pallas_call | solution.py:221
  168.7 19.7 %matmul.7.refs_9_ = f32[7,3,512,256]{3,2,1,0:T(8,128)} custom-call(s32[4]{0:T(128)S(1)} %pad_add_fusion.refs_0_.where_ref, bf16[2,128,2048]{2,1,0:T(8,128)(2,1)S(1)} %collective-permute-done.2.refs_1_.refs_3_, bf16[2,384,512]{2,1,0:T(8,128)(2,1)S(1)} %collective-permute-done.20.refs_2_, ...), custom_call_target="tpu_custom_call", output_to_operand_aliasing={{}: (17, {})} | custom-call | flops 8455716864 | bytes 19660800 | tf_op jit(solution)/shard_map/matmul/pallas_call | solution.py:221
  188.4 15.5 %matmul.8.refs_17_ = f32[7,3,512,256]{3,2,1,0:T(8,128)} custom-call(s32[4]{0:T(128)S(1)} %pad_add_fusion.refs_0_.where_ref, bf16[2,128,2048]{2,1,0:T(8,128)(2,1)S(1)} %collective-permute-done.2.refs_1_.refs_3_, bf16[2,384,256]{2,1,0:T(8,128)(2,1)} %collective-permute-done.14.refs_2_, ...), custom_call_target="tpu_custom_call", output_to_operand_aliasing={{}: (9, {})} | custom-call | flops 2818572288 | bytes 6553600 | tf_op jit(solution)/shard_map/matmul/pallas_call | solution.py:221
  204.0 17.5 %matmul.9 = (f32[96,512]{1,0:T(8,128)S(1)}, f32[96,512]{1,0:T(8,128)S(1)}) custom-call(s32[4]{0:T(128)S(1)} %pad_add_fusion.refs_0_.where_ref, bf16[2,128,2048]{2,1,0:T(8,128)(2,1)S(1)} %pad_maximum_fusion.refs_1_.refs_5_, bf16[4,384,256]{2,1,0:T(8,128)(2,1)} %pad_maximum_fusion.2.refs_2_.refs_4_, ...), custom_call_target="tpu_custom_call" | custom-call | flops 5637144576 | bytes 13107200 | tf_op jit(solution)/shard_map/matmul/pallas_call | solution.py:221
  221.8 1.2 fusion.4
  223.5 2.8 %collective-permute-start.32 = (f32[96,128]{1,0:T(8,128)S(1)}, f32[96,128]{1,0:T(8,128)S(1)}, u32[]{:S(2)}, u32[]{:S(2)}) collective-permute-start(f32[96,128]{1,0:T(8,128)S(1)} %get-tuple-element.17), channel_id=1, source_target_pairs={{0,3},{1,0},{2,1},{3,2},{4,7},{5,4},{6,5},{7,6},{8,11},{9,8},{10,9... | collective-permute-start | bytes 147464 | tf_op jit(solution)/shard_map/ppermute | solution.py:90
  226.3 1.0 collective-permute-start.34
  227.3 1.2 collective-permute-start.1
  228.5 3.7 %collective-permute-done.33 = f32[96,128]{1,0:T(8,128)S(1)} collective-permute-done((f32[96,128]{1,0:T(8,128)S(1)}, f32[96,128]{1,0:T(8,128)S(1)}, u32[]{:S(2)}, u32[]{:S(2)}) %collective-permute-start.33) | collective-permute-done | bytes 49184 | tf_op jit(solution)/shard_map/ppermute | solution.py:90
  232.3 1.6 collective-permute-start.35
  233.9 2.6 collective-permute-done.35
  238.4 2.1 sketch.1.refs_0_
  240.5 2.3 collective-permute-start.38
  242.7 2.1 collective-permute-start.39
  244.8 2.2 collective-permute-done.37.refs_1_
  247.1 1.1 collective-permute-done.38.refs_2_
  248.2 4.6 %copy-done = f32[3,256,4096]{2,1,0:T(8,128)S(1)} copy-done((f32[3,256,4096]{2,1,0:T(8,128)S(1)}, f32[3,256,4096]{2,1,0:T(8,128)}, u32[]{:S(2)}) %copy-start) | copy-done | bytes 12582936
  253.5 6.4 %precond.1 = f32[3,4,256]{2,1,0:T(4,128)} custom-call(s32[1]{0:T(128)} %bitcast.row_ref, f32[3,256,4096]{2,1,0:T(8,128)S(1)} %copy-done, f32[3,32,128]{2,1,0:T(8,128)S(1)} %copy-done.2, f32[3,32,128]{2,1,0:T(8,128)S(1)} %collective-permute-done.37.refs_1_, f32[3,32,128]{2,1,0:T(8,128)S(1)} %collective-permute-done.38.refs_2_, ...), custom_call_target="tpu_custom_call" | custom-call | tf_op jit(solution)/shard_map/precond/pallas_call | solution.py:308
  (85 shorter events, 10.8 us)
Async XLA Ops:
  0.0 31.6 %copy-start.4 = (bf16[128,2048]{1,0:T(8,128)(2,1)S(1)}, bf16[128,2048]{1,0:T(8,128)(2,1)}, u32[]{:S(2)}) copy-start(bf16[128,2048]{1,0:T(8,128)(2,1)} %param.7) | copy-start | bytes 1572868
  0.0 31.7 %copy-start.5 = (bf16[128,2048]{1,0:T(8,128)(2,1)S(1)}, bf16[128,2048]{1,0:T(8,128)(2,1)}, u32[]{:S(2)}) copy-start(bf16[128,2048]{1,0:T(8,128)(2,1)} %param.8) | copy-start | bytes 1572868
  2.0 28.4 %collective-permute-start.23 = (bf16[2,128,1024]{2,1,0:T(8,128)(2,1)}, bf16[2,128,1024]{2,1,0:T(8,128)(2,1)}, u32[]{:S(2)}, u32[]{:S(2)}) collective-permute-start(bf16[2,128,1024]{2,1,0:T(8,128)(2,1)} %fusion), channel_id=1, source_target_pairs={{0,2},{1,3},{2,0},{3,1},{4,6},{5,7},{6,4},{7,5},{8,10},{9,11},{10,... | collective-permute-start | bytes 1572872 | tf_op jit(solution)/shard_map/ppermute | solution.py:90
  6.0 27.7 %collective-permute-start.25 = (bf16[2,128,1024]{2,1,0:T(8,128)(2,1)}, bf16[2,128,1024]{2,1,0:T(8,128)(2,1)}, u32[]{:S(2)}, u32[]{:S(2)}) collective-permute-start(bf16[2,128,1024]{2,1,0:T(8,128)(2,1)} %fusion), channel_id=1, source_target_pairs={{0,1},{1,2},{2,3},{4,5},{5,6},{6,7},{8,9},{9,10},{10,11},{12,13},{... | collective-permute-start | bytes 1572872 | tf_op jit(solution)/shard_map/ppermute | solution.py:90
  10.3 27.1 %collective-permute-start.26 = (bf16[2,128,1024]{2,1,0:T(8,128)(2,1)}, bf16[2,128,1024]{2,1,0:T(8,128)(2,1)}, u32[]{:S(2)}, u32[]{:S(2)}) collective-permute-start(bf16[2,128,1024]{2,1,0:T(8,128)(2,1)} %fusion), channel_id=1, source_target_pairs={{1,0},{2,1},{3,2},{5,4},{6,5},{7,6},{9,8},{10,9},{11,10},{13,12},{... | collective-permute-start | bytes 1572872 | tf_op jit(solution)/shard_map/ppermute | solution.py:90
  30.4 16.5 %collective-permute-start.24 = (bf16[2,128,1024]{2,1,0:T(8,128)(2,1)}, bf16[2,128,1024]{2,1,0:T(8,128)(2,1)}, u32[]{:S(2)}, u32[]{:S(2)}) collective-permute-start(bf16[2,128,1024]{2,1,0:T(8,128)(2,1)} %collective-permute-done.23), channel_id=1, source_target_pairs={{2,3},{1,0},{6,7},{5,4},{10,11},{9,8},{14,15},{13,12},{18,19},{17,... | collective-permute-start | bytes 1572872 | tf_op jit(solution)/shard_map/ppermute | solution.py:90
  31.8 46.1 %collective-permute-start.2 = (bf16[2,128,2048]{2,1,0:T(8,128)(2,1)S(1)}, bf16[2,128,2048]{2,1,0:T(8,128)(2,1)S(1)}, u32[]{:S(2)}, u32[]{:S(2)}) collective-permute-start(bf16[2,128,2048]{2,1,0:T(8,128)(2,1)S(1)} %pad_maximum_fusion.refs_1_.refs_5_), channel_id=1, source_target_pairs={{0,8},{1,9},{2,10},{3,11},{4,12},{5,13},{6,14},{7,15},{8,0},{9,1},... | collective-permute-start | bytes 3145736 | tf_op jit(solution)/shard_map/ppermute | solution.py:90
  50.5 26.4 %copy-start.7 = (bf16[2048,192]{0,1:T(8,128)(2,1)S(1)}, bf16[2048,192]{0,1:T(8,128)(2,1)}, u32[]{:S(2)}) copy-start(bf16[2048,192]{0,1:T(8,128)(2,1)} %param.11) | copy-start | bytes 2359300
  50.5 55.9 %collective-permute-start.27 = (bf16[2,384,1024]{2,1,0:T(8,128)(2,1)}, bf16[2,384,1024]{2,1,0:T(8,128)(2,1)}, u32[]{:S(2)}, u32[]{:S(2)}) collective-permute-start(bf16[2,384,1024]{2,1,0:T(8,128)(2,1)} %pad_maximum_fusion.1.refs_2_), channel_id=1, source_target_pairs={{0,8},{1,9},{2,10},{3,11},{4,12},{5,13},{6,14},{7,15},{8,0},{9,1},... | collective-permute-start | bytes 4718600 | tf_op jit(solution)/shard_map/ppermute | solution.py:90
  52.1 13.8 %collective-permute-start.10 = (bf16[2,128,256]{2,1,0:T(8,128)(2,1)S(1)}, bf16[2,128,256]{2,1,0:T(8,128)(2,1)}, u32[]{:S(2)}, u32[]{:S(2)}) collective-permute-start(bf16[2,128,256]{2,1,0:T(8,128)(2,1)S(1)} %get-tuple-element.9), channel_id=1, source_target_pairs={{0,2},{1,3},{2,0},{3,1},{4,6},{5,7},{6,4},{7,5},{8,10},{9,11},{10,... | collective-permute-start | bytes 393224 | tf_op jit(solution)/shard_map/ppermute | solution.py:90
  52.6 14.6 %collective-permute-start.12 = (bf16[2,128,256]{2,1,0:T(8,128)(2,1)S(1)}, bf16[2,128,256]{2,1,0:T(8,128)(2,1)}, u32[]{:S(2)}, u32[]{:S(2)}) collective-permute-start(bf16[2,128,256]{2,1,0:T(8,128)(2,1)S(1)} %get-tuple-element.9), channel_id=1, source_target_pairs={{0,1},{1,2},{2,3},{4,5},{5,6},{6,7},{8,9},{9,10},{10,11},{12,13},{... | collective-permute-start | bytes 393224 | tf_op jit(solution)/shard_map/ppermute | solution.py:90
  57.5 18.0 %collective-permute-start.16 = (bf16[2,128,512]{2,1,0:T(8,128)(2,1)S(1)}, bf16[2,128,512]{2,1,0:T(8,128)(2,1)S(1)}, u32[]{:S(2)}, u32[]{:S(2)}) collective-permute-start(bf16[2,128,512]{2,1,0:T(8,128)(2,1)S(1)} %fusion.3), channel_id=1, source_target_pairs={{0,2},{1,3},{2,0},{3,1},{4,6},{5,7},{6,4},{7,5},{8,10},{9,11},{10,... | collective-permute-start | bytes 786440 | tf_op jit(solution)/shard_map/ppermute | solution.py:90
  65.9 10.9 %collective-permute-start.18 = (bf16[2,128,512]{2,1,0:T(8,128)(2,1)S(1)}, bf16[2,128,512]{2,1,0:T(8,128)(2,1)S(1)}, u32[]{:S(2)}, u32[]{:S(2)}) collective-permute-start(bf16[2,128,512]{2,1,0:T(8,128)(2,1)S(1)} %fusion.3), channel_id=1, source_target_pairs={{0,1},{1,2},{2,3},{4,5},{5,6},{6,7},{8,9},{9,10},{10,11},{12,13},{... | collective-permute-start | bytes 786440 | tf_op jit(solution)/shard_map/ppermute | solution.py:90
  67.2 7.0 %collective-permute-start.13 = (bf16[2,128,256]{2,1,0:T(8,128)(2,1)S(1)}, bf16[2,128,256]{2,1,0:T(8,128)(2,1)}, u32[]{:S(2)}, u32[]{:S(2)}) collective-permute-start(bf16[2,128,256]{2,1,0:T(8,128)(2,1)S(1)} %get-tuple-element.9), channel_id=1, source_target_pairs={{1,0},{2,1},{3,2},{5,4},{6,5},{7,6},{9,8},{10,9},{11,10},{13,12},{... | collective-permute-start | bytes 393224 | tf_op jit(solution)/shard_map/ppermute | solution.py:90
  74.2 11.2 %collective-permute-start.19 = (bf16[2,128,512]{2,1,0:T(8,128)(2,1)S(1)}, bf16[2,128,512]{2,1,0:T(8,128)(2,1)}, u32[]{:S(2)}, u32[]{:S(2)}) collective-permute-start(bf16[2,128,512]{2,1,0:T(8,128)(2,1)S(1)} %fusion.3), channel_id=1, source_target_pairs={{1,0},{2,1},{3,2},{5,4},{6,5},{7,6},{9,8},{10,9},{11,10},{13,12},{... | collective-permute-start | bytes 786440 | tf_op jit(solution)/shard_map/ppermute | solution.py:90
  75.5 15.3 %collective-permute-start.17 = (bf16[2,128,512]{2,1,0:T(8,128)(2,1)S(1)}, bf16[2,128,512]{2,1,0:T(8,128)(2,1)}, u32[]{:S(2)}, u32[]{:S(2)}) collective-permute-start(bf16[2,128,512]{2,1,0:T(8,128)(2,1)S(1)} %collective-permute-done.16), channel_id=1, source_target_pairs={{2,3},{1,0},{6,7},{5,4},{10,11},{9,8},{14,15},{13,12},{18,19},{17,... | collective-permute-start | bytes 786440 | tf_op jit(solution)/shard_map/ppermute | solution.py:90
  76.8 42.0 %collective-permute-start.30 = (bf16[2,384,1024]{2,1,0:T(8,128)(2,1)}, bf16[2,384,1024]{2,1,0:T(8,128)(2,1)}, u32[]{:S(2)}, u32[]{:S(2)}) collective-permute-start(bf16[2,384,1024]{2,1,0:T(8,128)(2,1)} %pad_maximum_fusion.1.refs_2_), channel_id=1, source_target_pairs={{0,4},{1,5},{2,6},{3,7},{4,0},{5,1},{6,2},{7,3},{8,12},{9,13},{10,... | collective-permute-start | bytes 4718600 | tf_op jit(solution)/shard_map/ppermute | solution.py:90
  77.8 12.9 %collective-permute-start.11 = (bf16[2,128,256]{2,1,0:T(8,128)(2,1)}, bf16[2,128,256]{2,1,0:T(8,128)(2,1)S(1)}, u32[]{:S(2)}, u32[]{:S(2)}) collective-permute-start(bf16[2,128,256]{2,1,0:T(8,128)(2,1)} %collective-permute-done.10), channel_id=1, source_target_pairs={{2,3},{1,0},{6,7},{5,4},{10,11},{9,8},{14,15},{13,12},{18,19},{17,... | collective-permute-start | bytes 393224 | tf_op jit(solution)/shard_map/ppermute | solution.py:90
  79.2 124.7 %copy-start.3 = (s32[4]{0:T(128)}, s32[4]{0:T(128)S(1)}, u32[]{:S(2)}) copy-start(s32[4]{0:T(128)S(1)} %pad_add_fusion.refs_0_.where_ref) | copy-start | bytes 52
  85.4 32.8 %collective-permute-start.7 = (bf16[2,128,2048]{2,1,0:T(8,128)(2,1)S(1)}, bf16[2,128,2048]{2,1,0:T(8,128)(2,1)S(1)}, u32[]{:S(2)}, u32[]{:S(2)}) collective-permute-start(bf16[2,128,2048]{2,1,0:T(8,128)(2,1)S(1)} %pad_maximum_fusion.refs_1_.refs_5_), channel_id=1, source_target_pairs={{0,4},{1,5},{2,6},{3,7},{4,0},{5,1},{6,2},{7,3},{8,12},{9,13},{10,... | collective-permute-start | bytes 3145736 | tf_op jit(solution)/shard_map/ppermute | solution.py:90
  90.7 12.0 %collective-permute-start.3 = (bf16[4,128,256]{2,1,0:T(8,128)(2,1)S(1)}, bf16[4,128,256]{2,1,0:T(8,128)(2,1)S(1)}, u32[]{:S(2)}, u32[]{:S(2)}) collective-permute-start(bf16[4,128,256]{2,1,0:T(8,128)(2,1)S(1)} %pad_maximum_fusion.5), channel_id=1, source_target_pairs={{0,2},{1,3},{2,0},{3,1},{4,6},{5,7},{6,4},{7,5},{8,10},{9,11},{10,... | collective-permute-start | bytes 786440 | tf_op jit(solution)/shard_map/ppermute | solution.py:90
  90.7 13.2 %collective-permute-start.5 = (bf16[4,128,256]{2,1,0:T(8,128)(2,1)S(1)}, bf16[4,128,256]{2,1,0:T(8,128)(2,1)S(1)}, u32[]{:S(2)}, u32[]{:S(2)}) collective-permute-start(bf16[4,128,256]{2,1,0:T(8,128)(2,1)S(1)} %pad_maximum_fusion.5), channel_id=1, source_target_pairs={{0,1},{1,2},{2,3},{4,5},{5,6},{6,7},{8,9},{9,10},{10,11},{12,13},{... | collective-permute-start | bytes 786440 | tf_op jit(solution)/shard_map/ppermute | solution.py:90
  102.7 9.5 %collective-permute-start.6 = (bf16[4,128,256]{2,1,0:T(8,128)(2,1)S(1)}, bf16[4,128,256]{2,1,0:T(8,128)(2,1)S(1)}, u32[]{:S(2)}, u32[]{:S(2)}) collective-permute-start(bf16[4,128,256]{2,1,0:T(8,128)(2,1)S(1)} %pad_maximum_fusion.5), channel_id=1, source_target_pairs={{1,0},{2,1},{3,2},{5,4},{6,5},{7,6},{9,8},{10,9},{11,10},{13,12},{... | collective-permute-start | bytes 786440 | tf_op jit(solution)/shard_map/ppermute | solution.py:90
  104.0 13.2 %collective-permute-start.4 = (bf16[4,128,256]{2,1,0:T(8,128)(2,1)S(1)}, bf16[4,128,256]{2,1,0:T(8,128)(2,1)S(1)}, u32[]{:S(2)}, u32[]{:S(2)}) collective-permute-start(bf16[4,128,256]{2,1,0:T(8,128)(2,1)S(1)} %collective-permute-done.3), channel_id=1, source_target_pairs={{2,3},{1,0},{6,7},{5,4},{10,11},{9,8},{14,15},{13,12},{18,19},{17,... | collective-permute-start | bytes 786440 | tf_op jit(solution)/shard_map/ppermute | solution.py:90
  106.4 34.1 %collective-permute-start.28 = (bf16[2,384,1024]{2,1,0:T(8,128)(2,1)}, bf16[2,384,1024]{2,1,0:T(8,128)(2,1)S(1)}, u32[]{:S(2)}, u32[]{:S(2)}) collective-permute-start(bf16[2,384,1024]{2,1,0:T(8,128)(2,1)} %collective-permute-done.27.refs_2_), channel_id=1, source_target_pairs={{0,4},{1,5},{2,6},{3,7},{4,0},{5,1},{6,2},{7,3},{8,12},{9,13},{10,... | collective-permute-start | bytes 4718600 | tf_op jit(solution)/shard_map/ppermute | solution.py:90
  112.1 27.2 %collective-permute-start.14 = (bf16[2,384,256]{2,1,0:T(8,128)(2,1)S(1)}, bf16[2,384,256]{2,1,0:T(8,128)(2,1)}, u32[]{:S(2)}, u32[]{:S(2)}) collective-permute-start(bf16[2,384,256]{2,1,0:T(8,128)(2,1)S(1)} %pad_maximum_fusion.4.refs_6_), channel_id=1, source_target_pairs={{0,8},{1,9},{2,10},{3,11},{4,12},{5,13},{6,14},{7,15},{8,0},{9,1},... | collective-permute-start | bytes 1179656 | tf_op jit(solution)/shard_map/ppermute | solution.py:90
  117.2 22.5 %collective-permute-start.29 = (bf16[2,384,512]{2,1,0:T(8,128)(2,1)S(1)}, bf16[2,384,512]{2,1,0:T(8,128)(2,1)S(1)}, u32[]{:S(2)}, u32[]{:S(2)}) collective-permute-start(bf16[2,384,512]{2,1,0:T(8,128)(2,1)S(1)} %pad_maximum_fusion.3.refs_6_), channel_id=1, source_target_pairs={{0,4},{1,5},{2,6},{3,7},{4,0},{5,1},{6,2},{7,3},{8,12},{9,13},{10,... | collective-permute-start | bytes 2359304 | tf_op jit(solution)/shard_map/ppermute | solution.py:90
  118.2 21.8 %collective-permute-start.20 = (bf16[2,384,512]{2,1,0:T(8,128)(2,1)S(1)}, bf16[2,384,512]{2,1,0:T(8,128)(2,1)S(1)}, u32[]{:S(2)}, u32[]{:S(2)}) collective-permute-start(bf16[2,384,512]{2,1,0:T(8,128)(2,1)S(1)} %pad_maximum_fusion.3.refs_6_), channel_id=1, source_target_pairs={{0,8},{1,9},{2,10},{3,11},{4,12},{5,13},{6,14},{7,15},{8,0},{9,1},... | collective-permute-start | bytes 2359304 | tf_op jit(solution)/shard_map/ppermute | solution.py:90
  118.7 21.6 %collective-permute-start.9 = (bf16[2,128,2048]{2,1,0:T(8,128)(2,1)S(1)}, bf16[2,128,2048]{2,1,0:T(8,128)(2,1)S(1)}, u32[]{:S(2)}, u32[]{:S(2)}) collective-permute-start(bf16[2,128,2048]{2,1,0:T(8,128)(2,1)S(1)} %collective-permute-done.2.refs_1_.refs_3_), channel_id=1, source_target_pairs={{0,4},{1,5},{2,6},{3,7},{4,0},{5,1},{6,2},{7,3},{8,12},{9,13},{10,... | collective-permute-start | bytes 3145736 | tf_op jit(solution)/shard_map/ppermute | solution.py:90
  139.4 29.2 %collective-permute-start.22 = (bf16[2,384,256]{2,1,0:T(8,128)(2,1)S(1)}, bf16[2,384,256]{2,1,0:T(8,128)(2,1)S(1)}, u32[]{:S(2)}, u32[]{:S(2)}) collective-permute-start(bf16[2,384,256]{2,1,0:T(8,128)(2,1)S(1)} %pad_maximum_fusion.4.refs_6_), channel_id=1, source_target_pairs={{0,4},{1,5},{2,6},{3,7},{4,0},{5,1},{6,2},{7,3},{8,12},{9,13},{10,... | collective-permute-start | bytes 1179656 | tf_op jit(solution)/shard_map/ppermute | solution.py:90
  139.8 48.7 %collective-permute-start.15 = (bf16[2,384,256]{2,1,0:T(8,128)(2,1)}, bf16[2,384,256]{2,1,0:T(8,128)(2,1)}, u32[]{:S(2)}, u32[]{:S(2)}) collective-permute-start(bf16[2,384,256]{2,1,0:T(8,128)(2,1)} %collective-permute-done.14.refs_2_), channel_id=1, source_target_pairs={{0,4},{1,5},{2,6},{3,7},{4,0},{5,1},{6,2},{7,3},{8,12},{9,13},{10,... | collective-permute-start | bytes 1179656 | tf_op jit(solution)/shard_map/ppermute | solution.py:90
  140.0 28.7 %collective-permute-start.21 = (bf16[2,384,512]{2,1,0:T(8,128)(2,1)S(1)}, bf16[2,384,512]{2,1,0:T(8,128)(2,1)S(1)}, u32[]{:S(2)}, u32[]{:S(2)}) collective-permute-start(bf16[2,384,512]{2,1,0:T(8,128)(2,1)S(1)} %collective-permute-done.20.refs_2_), channel_id=1, source_target_pairs={{0,4},{1,5},{2,6},{3,7},{4,0},{5,1},{6,2},{7,3},{8,12},{9,13},{10,... | collective-permute-start | bytes 2359304 | tf_op jit(solution)/shard_map/ppermute | solution.py:90
  140.3 63.7 %collective-permute-start.8 = (bf16[4,384,256]{2,1,0:T(8,128)(2,1)}, bf16[4,384,256]{2,1,0:T(8,128)(2,1)}, u32[]{:S(2)}, u32[]{:S(2)}) collective-permute-start(bf16[4,384,256]{2,1,0:T(8,128)(2,1)} %pad_maximum_fusion.2.refs_2_.refs_4_), channel_id=1, source_target_pairs={{0,4},{1,5},{2,6},{3,7},{4,0},{5,1},{6,2},{7,3},{8,12},{9,13},{10,... | collective-permute-start | bytes 2359304 | tf_op jit(solution)/shard_map/ppermute | solution.py:90
  188.4 15.6 %copy-start.1 = (bf16[1792,192]{0,1:T(8,128)(2,1)S(1)}, bf16[1792,192]{0,1:T(8,128)(2,1)}, u32[]{:S(2)}) copy-start(bf16[1792,192]{0,1:T(8,128)(2,1)} %param.12) | copy-start | bytes 2064388
  204.0 17.9 %copy-start.6 = (bf16[128,2048]{1,0:T(8,128)(2,1)S(1)}, bf16[128,2048]{1,0:T(8,128)(2,1)}, u32[]{:S(2)}) copy-start(bf16[128,2048]{1,0:T(8,128)(2,1)} %param.8) | copy-start | bytes 1572868
  204.0 19.1 %copy-start.8 = (f32[128,128]{1,0:T(8,128)S(1)}, f32[128,128]{1,0:T(8,128)}, u32[]{:S(2)}) copy-start(f32[128,128]{1,0:T(8,128)} %fusion.1) | copy-start | bytes 196612
  221.5 1.9 collective-permute-start.31
  223.1 4.2 %collective-permute-start = (f32[192,128]{1,0:T(8,128)S(1)}, f32[192,128]{1,0:T(8,128)S(1)}, u32[]{:S(2)}, u32[]{:S(2)}) collective-permute-start(f32[192,128]{1,0:T(8,128)S(1)} %pad_maximum_fusion.6), channel_id=1, source_target_pairs={{0,4},{1,5},{2,6},{3,7},{4,0},{5,1},{6,2},{7,3},{8,12},{9,13},{10,... | collective-permute-start | bytes 294920 | tf_op jit(solution)/shard_map/ppermute | solution.py:90
  223.5 5.1 %collective-permute-start.32 = (f32[96,128]{1,0:T(8,128)S(1)}, f32[96,128]{1,0:T(8,128)S(1)}, u32[]{:S(2)}, u32[]{:S(2)}) collective-permute-start(f32[96,128]{1,0:T(8,128)S(1)} %get-tuple-element.17), channel_id=1, source_target_pairs={{0,3},{1,0},{2,1},{3,2},{4,7},{5,4},{6,5},{7,6},{8,11},{9,8},{10,9... | collective-permute-start | bytes 147464 | tf_op jit(solution)/shard_map/ppermute | solution.py:90
  226.3 6.0 %collective-permute-start.33 = (f32[96,128]{1,0:T(8,128)S(1)}, f32[96,128]{1,0:T(8,128)S(1)}, u32[]{:S(2)}, u32[]{:S(2)}) collective-permute-start(f32[96,128]{1,0:T(8,128)S(1)} %get-tuple-element.19), channel_id=1, source_target_pairs={{0,2},{1,3},{2,0},{3,1},{4,6},{5,7},{6,4},{7,5},{8,10},{9,11},{10,... | collective-permute-start | bytes 147464 | tf_op jit(solution)/shard_map/ppermute | solution.py:90
  226.3 6.0 %collective-permute-start.34 = (f32[96,128]{1,0:T(8,128)S(1)}, f32[96,128]{1,0:T(8,128)S(1)}, u32[]{:S(2)}, u32[]{:S(2)}) collective-permute-start(f32[96,128]{1,0:T(8,128)S(1)} %get-tuple-element.18), channel_id=1, source_target_pairs={{0,1},{1,2},{2,3},{3,0},{4,5},{5,6},{6,7},{7,4},{8,9},{9,10},{10,1... | collective-permute-start | bytes 147464 | tf_op jit(solution)/shard_map/ppermute | solution.py:90
  227.3 9.2 %collective-permute-start.1 = (f32[192,128]{1,0:T(8,128)S(1)}, f32[192,128]{1,0:T(8,128)S(1)}, u32[]{:S(2)}, u32[]{:S(2)}) collective-permute-start(f32[192,128]{1,0:T(8,128)S(1)} %fusion.10), channel_id=1, source_target_pairs={{0,8},{1,9},{2,10},{3,11},{4,12},{5,13},{6,14},{7,15},{8,0},{9,1},... | collective-permute-start | bytes 294920 | tf_op jit(solution)/shard_map/ppermute | solution.py:90
  232.3 4.2 %collective-permute-start.35 = (f32[96,128]{1,0:T(8,128)S(1)}, f32[96,128]{1,0:T(8,128)S(1)}, u32[]{:S(2)}, u32[]{:S(2)}) collective-permute-start(f32[96,128]{1,0:T(8,128)S(1)} %fusion.9), channel_id=1, source_target_pairs={{0,8},{1,9},{2,10},{3,11},{4,12},{5,13},{6,14},{7,15},{8,0},{9,1},... | collective-permute-start | bytes 147464 | tf_op jit(solution)/shard_map/ppermute | solution.py:90
  236.4 1.3 collective-permute-start.36
  240.4 6.6 %collective-permute-start.37 = (f32[3,32,128]{2,1,0:T(8,128)}, f32[3,32,128]{2,1,0:T(8,128)S(1)}, u32[]{:S(2)}, u32[]{:S(2)}) collective-permute-start(f32[3,32,128]{2,1,0:T(8,128)} %sketch.1.refs_0_), channel_id=1, source_target_pairs={{0,1},{1,2},{2,3},{3,0},{4,5},{5,6},{6,7},{7,4},{8,9},{9,10},{10,1... | collective-permute-start | bytes 147464 | tf_op jit(solution)/shard_map/ppermute | solution.py:90
  240.5 7.7 %collective-permute-start.38 = (f32[3,32,128]{2,1,0:T(8,128)}, f32[3,32,128]{2,1,0:T(8,128)S(1)}, u32[]{:S(2)}, u32[]{:S(2)}) collective-permute-start(f32[3,32,128]{2,1,0:T(8,128)} %sketch.1.refs_0_), channel_id=1, source_target_pairs={{0,2},{1,3},{2,0},{3,1},{4,6},{5,7},{6,4},{7,5},{8,10},{9,11},{10,... | collective-permute-start | bytes 147464 | tf_op jit(solution)/shard_map/ppermute | solution.py:90
  242.7 5.4 %collective-permute-start.39 = (f32[3,32,128]{2,1,0:T(8,128)}, f32[3,32,128]{2,1,0:T(8,128)S(1)}, u32[]{:S(2)}, u32[]{:S(2)}) collective-permute-start(f32[3,32,128]{2,1,0:T(8,128)} %sketch.1.refs_0_), channel_id=1, source_target_pairs={{0,3},{1,0},{2,1},{3,2},{4,7},{5,4},{6,5},{7,6},{8,11},{9,8},{10,9... | collective-permute-start | bytes 147464 | tf_op jit(solution)/shard_map/ppermute | solution.py:90
  248.2 4.6 %copy-start = (f32[3,256,4096]{2,1,0:T(8,128)S(1)}, f32[3,256,4096]{2,1,0:T(8,128)}, u32[]{:S(2)}) copy-start(f32[3,256,4096]{2,1,0:T(8,128)} %p_ref.1) | copy-start | bytes 37748740
  (3 other events, 2.7 us)

commit v2 on v1

--- a/solution.py
+++ b/solution.py
@@ -77,44 +77,22 @@
     return [(t * ROWS + z, (t ^ flip) * ROWS + z) for t in range(TENSOR) for z in range(ROWS)]
 
 
-def shift_rows(step, wrap=True):
-    return [
-        (t * ROWS + z, t * ROWS + (z + step) % ROWS)
-        for t in range(TENSOR)
-        for z in range(ROWS)
-        if wrap or 0 <= z + step < ROWS
-    ]
+def swap_rows(flip):
+    return [(t * ROWS + z, t * ROWS + (z ^ flip)) for t in range(TENSOR) for z in range(ROWS)]
 
 
 def send(value, pairs):
     return lax.ppermute(value, BOTH, pairs)
 
 
-FORWARD = [(t * ROWS + a, t * ROWS + b) for t in range(TENSOR) for a, b in ((2, 3), (1, 0))]
-
-
-def gather_rows(own):
-    row = lax.axis_index("dp")
-    from_1 = send(own, shift_rows(1, False))
-    from_2 = send(own, shift_rows(2))
-    from_3 = send(own, shift_rows(-1, False))
-    end = send(from_2, FORWARD)
-    from_1 = jnp.where(row == 0, end, from_1)
-    from_3 = jnp.where(row == ROWS - 1, end, from_3)
-    return jnp.concatenate([from_1, from_2, from_3], axis=1)
-
-
-def matmul_kernel(blocks, tokens, first, last, *refs):
-    count = len(blocks)
+def matmul_kernel(count, last, *refs):
     refs = list(refs)
     where_ref = refs.pop(0)
-    arrays = [(refs.pop(0), refs.pop(0)) for _ in range(count)]
+    pieces = [(refs.pop(0), refs.pop(0)) for _ in range(count)]
     gate_up = [refs.pop(0) for _ in range(count)]
     down = [refs.pop(0) for _ in range(count)]
-    acc_in = None if first else refs.pop(0)
     if last:
-        proj_ref = refs.pop(0)
-        mine_ref, theirs_ref = refs.pop(0), refs.pop(0)
+        acc_in, proj_ref, mine_ref, theirs_ref = (refs.pop(0) for _ in range(4))
     else:
         acc_out = refs.pop(0)
     rows = [refs.pop(0) for _ in range(count)]
@@ -124,31 +102,19 @@
     @pl.when(step == 0)
     def _():
         copies = []
-        for n, (block, (own, rest)) in enumerate(zip(blocks, arrays)):
-            _, offset, width, lead = block
-            split = own.shape[1]
-            copies.append(
-                pltpu.make_async_copy(
-                    own.at[:, :, pl.ds(offset, width)], rows[n].at[:, pl.ds(0, split), :], sems.at[2 * n]
-                )
-            )
-            copies.append(
-                pltpu.make_async_copy(
-                    rest.at[pl.ds(lead, 2)],
-                    rows[n].at[:, pl.ds(split, tokens - split), :],
-                    sems.at[2 * n + 1],
-                )
-            )
+        for n in range(count):
+            at = 0
+            for m, piece in enumerate(pieces[n]):
+                target = rows[n].at[:, pl.ds(at, piece.shape[1]), :]
+                copies.append(pltpu.make_async_copy(piece, target, sems.at[2 * n + m]))
+                at += piece.shape[1]
         for copy in copies:
             copy.start()
         for copy in copies:
             copy.wait()
-        if last:
-            ut_ref = refs[0]
-            ut_ref[...] = jnp.zeros_like(ut_ref)
 
     def total(which):
-        value = None if first else acc_in[0, which]
+        value = acc_in[step, which] if last else None
         for n in range(count):
             weight = down[n][...] if which == 2 else gate_up[n][which]
             part = lax.dot_general(
@@ -159,9 +125,14 @@
 
     if not last:
         for which in range(3):
-            acc_out[0, which] = total(which)
+            acc_out[step, which] = total(which)
         return
-    ut_ref = refs[0]
+    ut_ref = refs.pop(0)
+
+    @pl.when(step == 0)
+    def _():
+        ut_ref[...] = jnp.zeros_like(ut_ref)
+
     sides = activations(total(0), total(1), total(2))
     for n, side in enumerate(sides):
         ut_ref[pl.ds(n * K, K), :] += lax.dot_general(
@@ -176,50 +147,45 @@
         theirs_ref[...] = ut_ref[pl.ds(pl.multiple_of((1 - core) * half, 8), half), :]
 
 
-def matmul_step(where, blocks, arrays, w_gate_up, w_down, acc, unit_proj_t=None):
-    first, last = acc is None, unit_proj_t is not None
-    unit_width, model_width = w_down.shape
-    own_width = model_width // TENSOR
-    tokens = arrays[0][0].shape[1] + arrays[0][1].shape[1]
+def matmul_step(where, blocks, w_gate_up, w_down, acc=None, unit_proj_t=None):
+    last = acc is not None
+    count = len(blocks)
+    unit_width = w_down.shape[0]
+    width = blocks[0][1][0].shape[2]
+    tokens = sum(piece.shape[1] for piece in blocks[0][1])
     tile = 256
     tiles = unit_width // tile
-
-    def at(owner, offset, width):
-        per = own_width // width
-        return lambda i, at_ref: at_ref[owner] * per + offset // width
-
-    in_specs = [pl.BlockSpec(memory_space=pl.ANY)] * (2 * len(blocks))
-    operands = [a for pair in arrays for a in pair]
-    for owner, offset, width, _ in blocks:
-        column = at(owner, offset, width)
-        in_specs.append(pl.BlockSpec((2, tile, width), lambda i, r, c=column: (0, i, c(i, r))))
-        operands.append(w_gate_up)
-    for owner, offset, width, _ in blocks:
-        column = at(owner, offset, width)
-        in_specs.append(pl.BlockSpec((tile, width), lambda i, r, c=column: (i, c(i, r))))
-        operands.append(w_down)
-    acc_spec = pl.BlockSpec((1, 3, tokens, tile), lambda i, r: (i, 0, 0, 0))
-    acc_shape = jax.ShapeDtypeStruct((tiles, 3, tokens, tile), jnp.float32)
-    aliases = {}
-    if not first:
-        if not last:
-            aliases = {1 + len(operands): 0}
-        in_specs.append(acc_spec)
-        operands.append(acc)
-    scratch = [pltpu.VMEM((2, tokens, width), jnp.bfloat16) for _, _, width, _ in blocks]
-    scratch.append(pltpu.SemaphoreType.DMA((2 * len(blocks),)))
+    whole = pl.BlockSpec(memory_space=pltpu.VMEM)
+
+    in_specs, operands = [], []
+    for _, pieces in blocks:
+        for piece in pieces:
+            in_specs.append(pl.BlockSpec(memory_space=pl.ANY))
+            operands.append(piece)
+    for owner, _ in blocks:
+        in_specs.append(pl.BlockSpec((2, tile, width), lambda i, r, o=owner: (0, i, r[o])))
+        operands.append(pltpu.with_memory_space_constraint(w_gate_up, pltpu.HBM))
+    for owner, _ in blocks:
+        in_specs.append(pl.BlockSpec((tile, width), lambda i, r, o=owner: (i, r[o])))
+        operands.append(pltpu.with_memory_space_constraint(w_down, pltpu.HBM))
+    need = count * width * (2 * tokens + 2 * 3 * tile) * 2 + 6 * MIB
+    scratch = [pltpu.VMEM((2, tokens, width), jnp.bfloat16) for _ in blocks]
+    scratch.append(pltpu.SemaphoreType.DMA((2 * count,)))
     if last:
+        in_specs.append(whole)
+        operands.append(pltpu.with_memory_space_constraint(acc, pltpu.VMEM))
         in_specs.append(pl.BlockSpec((3 * K, tile), lambda i, r: (0, i)))
         operands.append(unit_proj_t)
         half = jax.ShapeDtypeStruct((3 * K // 2, tokens), jnp.float32)
         out_shape = (half, half)
         out_specs = (pl.BlockSpec(half.shape, lambda i, r: (0, 0)),) * 2
         scratch.append(pltpu.VMEM((3 * K, tokens), jnp.float32))
+        need += 6 * MIB
     else:
-        out_shape, out_specs = acc_shape, acc_spec
-    depth = sum(width for _, _, width, _ in blocks)
+        out_shape = pltpu.VMEM((tiles, 3, tokens, tile), jnp.float32)
+        out_specs = whole
     return pl.pallas_call(
-        functools.partial(matmul_kernel, blocks, tokens, first, last),
+        functools.partial(matmul_kernel, count, last),
         out_shape=out_shape,
         grid_spec=pltpu.PrefetchScalarGridSpec(
             num_scalar_prefetch=1,
@@ -228,11 +194,10 @@
             out_specs=out_specs,
             scratch_shapes=scratch,
         ),
-        input_output_aliases=aliases,
-        compiler_params=pltpu.CompilerParams(vmem_limit_bytes=44 * MIB),
+        compiler_params=pltpu.CompilerParams(vmem_limit_bytes=need),
         cost_estimate=pl.CostEstimate(
-            flops=2 * tokens * 3 * unit_width * depth,
-            bytes_accessed=3 * unit_width * depth * 2 + 4 * depth * tokens,
+            flops=2 * tokens * 3 * unit_width * width * count,
+            bytes_accessed=3 * unit_width * width * count * 2,
             transcendentals=0,
         ),
         name="matmul",
@@ -291,7 +256,7 @@
             sums[n, at, :] = totals[n]
 
     for n in range(ROWS):
-        seq = lax.rem(row_ref[0] - n + ROWS, ROWS)
+        seq = row_ref[0] ^ n
         line = lax.dot_general(
             ones,
             sums[n],
@@ -320,20 +285,34 @@
     )(row, precond, *sketches)
 
 
-CHUNKS = (1024, 512, 256)
 A, C, Y, D = range(4)
+INNER = [(t * ROWS + a, t * ROWS + b) for t in range(TENSOR) for a, b in ((1, 2), (2, 1))]
+OUTER = [(t * ROWS + a, t * ROWS + b) for t in range(TENSOR) for a, b in ((1, 0), (2, 3))]
+
+
+def other_core(value):
+    return send(value, swap_with(1))
+
+
+def other_chip(value):
+    return send(value, swap_with(2))
+
+
+def tie(*values):
+    return lax.optimization_barrier(values)
 
 
 def local_split(hidden_in, out_grad, w_gate_up, w_down, feat_proj, unit_proj, precond):
     tensor, row = lax.axis_index("tensor"), lax.axis_index("dp")
+    inner = jnp.logical_or(row == 1, row == 2)
     where = jnp.stack([tensor, tensor ^ 1, tensor ^ 2, tensor ^ 3]).astype(jnp.int32)
+    step = functools.partial(matmul_step, where)
+
     own = jnp.stack([hidden_in, out_grad])
-    width = own.shape[2]
-    other_y = send(own, swap_with(2))
-    other_core = send(own, swap_with(1))
-    other_both = send(other_y, swap_with(1))
-    unit_proj_t = unit_proj.T
-
+    near = send(own, swap_rows(1))
+    middle = send(own, INNER)
+    own_y = other_chip(own)
+    own_c = other_core(own)
     feat_t = jnp.concatenate(
         [
             lax.dot_general(
@@ -345,42 +324,51 @@
         ],
         axis=0,
     )
-    feat_t = feat_t + send(feat_t, swap_with(1))
-    feat_t = feat_t + send(feat_t, swap_with(2))
-
-    acc = None
-    waiting = ([], [])
-    offset = 0
-    for size in CHUNKS:
-        rest = gather_rows(own[:, :, offset : offset + size])
-        rest_core = send(rest, swap_with(1))
-        rest_y = send(rest, swap_with(2))
-        rest_both = send(rest_y, swap_with(1))
-        blocks = waiting[0] + [(A, offset, size, 0), (C, offset, size, 0)]
-        arrays = waiting[1] + [(own, rest), (other_core, rest_core)]
-        acc = matmul_step(where, blocks, arrays, w_gate_up, w_down, acc)
-        waiting = (
-            [(Y, offset, size, 0), (D, offset, size, 0)],
-            [(other_y, rest_y), (other_both, rest_both)],
-        )
-        offset += size
-    acc = matmul_step(where, *waiting, w_gate_up, w_down, acc)
-    size = width - offset
-    both = jnp.concatenate([own[:, :, offset:], other_y[:, :, offset:]], axis=0)
-    rest = gather_rows(both)
-    rest_core = send(rest, swap_with(1))
-    blocks = [(A, offset, size, 0), (Y, offset, size, 2), (C, offset, size, 0), (D, offset, size, 2)]
-    arrays = [(own, rest), (other_y, rest), (other_core, rest_core), (other_both, rest_core)]
-    mine, theirs = matmul_step(where, blocks, arrays, w_gate_up, w_down, acc, unit_proj_t)
-
-    mine = mine + send(theirs, swap_with(1))
-    part = mine[:, :SEQ]
-    for n in range(1, ROWS):
-        part = part + send(mine[:, n * SEQ : (n + 1) * SEQ], shift_rows(-n))
-    part = part + send(part, swap_with(2))
-    other = send(part, swap_with(1))
+    feat_t = feat_t + other_core(feat_t)
+    unit_proj_t = unit_proj.T
+    near, middle, own_y, own_c, unit_proj_t, feat_t = tie(near, middle, own_y, own_c, unit_proj_t, feat_t)
+
+    near_c = other_core(near)
+    passed = send(middle, OUTER)
+    middle_2 = send(near, INNER)
+    near_y = other_chip(near)
+    own_d = other_core(own_y)
+    feat_y = other_chip(feat_t)
+    acc = step([(A, (own, near)), (C, (own_c, near_c))], w_gate_up, w_down)
+    passed, middle_2, near_y, own_d, feat_y, acc = tie(passed, middle_2, near_y, own_d, feat_y, acc)
+    feat_t = feat_t + feat_y
+
+    near_d = other_core(near_y)
+    third = jnp.where(inner, middle, passed)
+    passed_2 = send(middle_2, OUTER)
+    third_y = other_chip(third)
+    third_c = other_core(third)
+    mine_0, theirs_0 = step(
+        [(Y, (own_y, near_y)), (D, (own_d, near_d))], w_gate_up, w_down, acc, unit_proj_t
+    )
+    passed_2, third_y, third_c, mine_0, theirs_0 = tie(passed_2, third_y, third_c, mine_0, theirs_0)
+
+    fourth = jnp.where(inner, middle_2, passed_2)
+    fourth_c = other_core(fourth)
+    fourth_y = other_chip(fourth)
+    third_d = other_core(third_y)
+    mine_0 = mine_0 + other_core(theirs_0)
+    acc = step([(A, (third, fourth)), (C, (third_c, fourth_c))], w_gate_up, w_down)
+    fourth_y, third_d, mine_0, acc = tie(fourth_y, third_d, mine_0, acc)
+
+    fourth_d = other_core(fourth_y)
+    mine_1, theirs_1 = step(
+        [(Y, (third_y, fourth_y)), (D, (third_d, fourth_d))], w_gate_up, w_down, acc, unit_proj_t
+    )
+
+    part = mine_0[:, :SEQ] + send(mine_0[:, SEQ:], swap_rows(1))
+    mine_1 = mine_1 + other_core(theirs_1)
+    low, high = mine_1[:, :SEQ], mine_1[:, SEQ:]
+    part = part + send(jnp.where(inner, high, low), swap_rows(2)) + send(jnp.where(inner, low, high), swap_rows(3))
+    part = part + other_chip(part)
+    other = other_core(part)
     sketch = sketch_own(where, feat_t, part, other)
-    sketches = [sketch] + [send(sketch, shift_rows(n)) for n in range(1, ROWS)]
+    sketches = [sketch] + [send(sketch, swap_rows(n)) for n in range(1, ROWS)]
     return apply_precond(row.astype(jnp.int32).reshape(1), precond, sketches)
 
 
@@ -390,7 +378,6 @@
         and lax.axis_size("dp") == ROWS
         and hidden_in.shape[0] == SEQ
         and w_down.shape[0] % 256 == 0
-        and hidden_in.shape[1] == 2048
     )
     step = local_split if fits else local_plain
     return step(hidden_in, out_grad, w_gate_up, w_down, feat_proj, unit_proj, precond)

time: 261 us -> 188 us (0.72)
  waiting for transfers between devices: 83.9 us -> 44.5 us
  starting transfers between devices: 47 us -> 25.8 us
  Pallas kernels: 110 us -> 93.7 us
  local copies, waits for them, and re-layouts: 6.06 us -> 16.4 us
  other arithmetic: 10.6 us -> 3.63 us
    ppermute x40 -> x29, waiting for transfers between devices: 83.9 us -> 44.5 us  [send(): return lax.ppermute(value, BOTH, pairs)]
    ppermute x40 -> x29, starting transfers between devices: 47 us -> 25.8 us  [send(): return lax.ppermute(value, BOTH, pairs)]
    pallas_call x5 -> x4, Pallas kernels: 101 us -> 85.4 us  [matmul_step(): pl.pallas_call(functools.partial(matmul_kernel, count, last), out_shape=o...]
    unnamed x22 -> x40, local copies, waits for them, and re-layouts: 6.03 us -> 16.4 us
    concatenate x5 -> x0, other arithmetic: 4.27 us -> none  [the longest x4 4.24 us: gather_rows(): return jnp.concatenate([from_1, from_2, from_3], axis=1)]
  transfers between devices with their start and end apart: 40 -> 29, of which waited for: 15 -> 14; matrix products, arithmetic and copies ran while one was open for 4% -> 3% of each run, Pallas kernels for 32% -> 34%
where the time goes in v2:
time: 188 us; the launch traced here: 187 us
  Pallas kernels  93.7 us (50%)
  waiting for transfers between devices  44.5 us (24%)
  starting transfers between devices  25.8 us (14%)
  local copies, waits for them, and re-layouts  16.4 us (9%)
  other arithmetic  3.63 us (2%)
  matrix products  2.92 us (2%)
    pallas_call x4, Pallas kernels, matmul_step(): pl.pallas_call(functools.partial(matmul_kernel, count, last), out_shape=o...  85.4 us
    ppermute x29, waiting for transfers between devices, send(): return lax.ppermute(value, BOTH, pairs)  44.5 us
    ppermute x29, starting transfers between devices, send(): return lax.ppermute(value, BOTH, pairs)  25.8 us
    unnamed x40, local copies, waits for them, and re-layouts  16.4 us
    pallas_call x1, Pallas kernels, apply_precond(): pl.pallas_call(precond_kernel, out_shape=jax.ShapeDtypeStruct((3, ROWS, h...  6.23 us
  transfers between devices with their start and end apart: 29, of which 14 were waited for; matrix products, arithmetic and copies ran while one was open for 3% of the time, Pallas kernels for 34%

profile of v2, /device:TPU:0, one launch (start us, length us, event | category | flops | bytes accessed | tf_op | source)
XLA Modules:
  0.0 187.2 jit_solution(7922276833239850054)
XLA Ops:
  0.0 1.3 pad_maximum_fusion.refs_1_
  1.3 3.1 %collective-permute-start = (bf16[2,128,2048]{2,1,0:T(8,128)(2,1)S(1)}, bf16[2,128,2048]{2,1,0:T(8,128)(2,1)}, u32[]{:S(2)}, u32[]{:S(2)}) collective-permute-start(bf16[2,128,2048]{2,1,0:T(8,128)(2,1)S(1)} %pad_maximum_fusion.refs_1_), channel_id=1, source_target_pairs={{0,1},{1,0},{2,3},{3,2},{4,5},{5,4},{6,7},{7,6},{8,9},{9,8},{10,11... | collective-permute-start | bytes 3145736 | tf_op jit(solution)/shard_map/ppermute | solution.py:85
  4.4 0.7 collective-permute-start.1
  5.1 1.6 collective-permute-start.2
  6.7 1.4 fusion.2
  8.1 1.5 fusion
  10.2 0.9 collective-permute-done.4
  11.2 16.5 %collective-permute-done.refs_2_ = bf16[2,128,2048]{2,1,0:T(8,128)(2,1)} collective-permute-done((bf16[2,128,2048]{2,1,0:T(8,128)(2,1)S(1)}, bf16[2,128,2048]{2,1,0:T(8,128)(2,1)}, u32[]{:S(2)}, u32[]{:S(2)}) %collective-permute-start) | collective-permute-done | bytes 1048608 | tf_op jit(solution)/shard_map/ppermute | solution.py:85
  27.7 2.1 %collective-permute-done.2.refs_1_ = bf16[2,128,2048]{2,1,0:T(8,128)(2,1)S(1)} collective-permute-done((bf16[2,128,2048]{2,1,0:T(8,128)(2,1)S(1)}, bf16[2,128,2048]{2,1,0:T(8,128)(2,1)S(1)}, u32[]{:S(2)}, u32[]{:S(2)}) %collective-permute-start.2) | collective-permute-done | bytes 1048608 | tf_op jit(solution)/shard_map/ppermute | solution.py:85
  29.8 1.0 copy-done.4
  30.9 0.8 collective-permute-start.6
  31.7 1.6 collective-permute-start.7
  33.3 1.3 collective-permute-start.5
  35.4 1.2 copy-done.5
  36.6 21.9 %matmul.4.refs_9_ = f32[7,3,256,256]{3,2,1,0:T(8,128)S(1)} custom-call(s32[4]{0:T(128)S(1)} %pad_add_fusion.refs_0_.where_ref, bf16[2,128,2048]{2,1,0:T(8,128)(2,1)S(1)} %pad_maximum_fusion.refs_1_, bf16[2,128,2048]{2,1,0:T(8,128)(2,1)} %collective-permute-done.refs_2_, bf16[2,128,2048]{2,1,0:T(8,128)(2,1)S(1)} %copy-done.5, ...), custom_call_target="tpu_custom_call" | custom-call | flops 11274289152 | bytes 44040192 | tf_op jit(solution)/shard_map/matmul/pallas_call | solution.py:187
  58.6 2.4 %copy-done = f32[7,3,256,256]{3,2,1,0:T(8,128)} copy-done((f32[7,3,256,256]{3,2,1,0:T(8,128)}, f32[7,3,256,256]{3,2,1,0:T(8,128)S(1)}, u32[]{:S(2)}) %copy-start) | copy-done | bytes 5505048
  61.0 3.5 %collective-permute-done.5 = bf16[2,128,2048]{2,1,0:T(8,128)(2,1)S(1)} collective-permute-done((bf16[2,128,2048]{2,1,0:T(8,128)(2,1)}, bf16[2,128,2048]{2,1,0:T(8,128)(2,1)S(1)}, u32[]{:S(2)}, u32[]{:S(2)}) %collective-permute-start.5) | collective-permute-done | bytes 1048608 | tf_op jit(solution)/shard_map/ppermute | solution.py:85
  64.5 1.0 copy-done.13
  65.5 1.0 copy-done.6
  66.5 1.4 broadcast_select_fusion.1.refs_1_
  68.7 1.3 collective-permute-start.11
  70.0 2.6 %copy-done.1 = f32[7,3,256,256]{3,2,1,0:T(8,128)S(1)} copy-done((f32[7,3,256,256]{3,2,1,0:T(8,128)S(1)}, f32[7,3,256,256]{3,2,1,0:T(8,128)}, u32[]{:S(2)}) %copy-start.1) | copy-done | bytes 5505048
  72.6 1.2 copy-done.7
  73.8 23.0 %matmul.5 = (f32[96,256]{1,0:T(8,128)S(1)}, f32[96,256]{1,0:T(8,128)S(1)}) custom-call(s32[4]{0:T(128)S(1)} %pad_add_fusion.refs_0_.where_ref, bf16[2,128,2048]{2,1,0:T(8,128)(2,1)S(1)} %collective-permute-done.2.refs_1_, bf16[2,128,2048]{2,1,0:T(8,128)(2,1)} %collective-permute-done.7.refs_2_, bf16[2,128,2048]{2,1,0:T(8,128)(2,1)S(1)} %copy-done.7, ...), custom_call_target="tpu_custom_call" | custom-call | flops 11274289152 | bytes 44040192 | tf_op jit(solution)/shard_map/matmul/pallas_call | solution.py:187
  96.8 1.4 collective-permute-done.11
  99.4 1.8 collective-permute-done.17
  101.2 19.6 %matmul.6.refs_9_ = f32[7,3,256,256]{3,2,1,0:T(8,128)S(1)} custom-call(s32[4]{0:T(128)S(1)} %pad_add_fusion.refs_0_.where_ref, bf16[2,128,2048]{2,1,0:T(8,128)(2,1)S(1)} %broadcast_select_fusion.1.refs_1_, bf16[2,128,2048]{2,1,0:T(8,128)(2,1)S(1)} %broadcast_select_fusion.refs_2_, bf16[2,128,2048]{2,1,0:T(8,128)(2,1)S(1)} %collective-permute-done.13.refs_3_, ...), custom_call_target="tpu_custom_call" | custom-call | flops 11274289152 | bytes 44040192 | tf_op jit(solution)/shard_map/matmul/pallas_call | solution.py:187
  120.8 3.2 %collective-permute-done.15.refs_2_ = bf16[2,128,2048]{2,1,0:T(8,128)(2,1)S(1)} collective-permute-done((bf16[2,128,2048]{2,1,0:T(8,128)(2,1)S(1)}, bf16[2,128,2048]{2,1,0:T(8,128)(2,1)S(1)}, u32[]{:S(2)}, u32[]{:S(2)}) %collective-permute-start.15) | collective-permute-done | bytes 1048608 | tf_op jit(solution)/shard_map/ppermute | solution.py:85
  124.0 2.7 %collective-permute-done.20.refs_4_ = bf16[2,128,2048]{2,1,0:T(8,128)(2,1)S(1)} collective-permute-done((bf16[2,128,2048]{2,1,0:T(8,128)(2,1)S(1)}, bf16[2,128,2048]{2,1,0:T(8,128)(2,1)S(1)}, u32[]{:S(2)}, u32[]{:S(2)}) %collective-permute-start.20) | collective-permute-done | bytes 1048608 | tf_op jit(solution)/shard_map/ppermute | solution.py:85
  126.7 20.9 %matmul.7 = (f32[96,256]{1,0:T(8,128)S(1)}, f32[96,256]{1,0:T(8,128)S(1)}) custom-call(s32[4]{0:T(128)S(1)} %pad_add_fusion.refs_0_.where_ref, bf16[2,128,2048]{2,1,0:T(8,128)(2,1)S(1)} %collective-permute-done.12.refs_1_, bf16[2,128,2048]{2,1,0:T(8,128)(2,1)S(1)} %collective-permute-done.15.refs_2_, ...), custom_call_target="tpu_custom_call" | custom-call | flops 11274289152 | bytes 44040192 | tf_op jit(solution)/shard_map/matmul/pallas_call | solution.py:187
  147.8 3.3 %collective-permute-start.19 = (f32[96,128]{1,0:T(8,128)S(1)}, f32[96,128]{1,0:T(8,128)S(1)}, u32[]{:S(2)}, u32[]{:S(2)}) collective-permute-start(f32[96,128]{1,0:T(8,128)S(1)} %slice.21), channel_id=1, source_target_pairs={{0,1},{1,0},{2,3},{3,2},{4,5},{5,4},{6,7},{7,6},{8,9},{9,8},{10,11... | collective-permute-start | bytes 147464 | tf_op jit(solution)/shard_map/ppermute | solution.py:85
  151.2 1.5 collective-permute-start.22
  152.7 2.1 %collective-permute-start.23 = (f32[96,128]{1,0:T(8,128)S(1)}, f32[96,128]{1,0:T(8,128)S(1)}, u32[]{:S(2)}, u32[]{:S(2)}) collective-permute-start(f32[96,128]{1,0:T(8,128)S(1)} %get-tuple-element.56), channel_id=1, source_target_pairs={{0,3},{1,2},{2,1},{3,0},{4,7},{5,6},{6,5},{7,4},{8,11},{9,10},{10,... | collective-permute-start | bytes 147464 | tf_op jit(solution)/shard_map/ppermute | solution.py:85
  154.8 3.3 %collective-permute-done.22 = f32[96,128]{1,0:T(8,128)S(1)} collective-permute-done((f32[96,128]{1,0:T(8,128)S(1)}, f32[96,128]{1,0:T(8,128)S(1)}, u32[]{:S(2)}, u32[]{:S(2)}) %collective-permute-start.22) | collective-permute-done | bytes 49184 | tf_op jit(solution)/shard_map/ppermute | solution.py:85
  158.0 0.6 collective-permute-done.23
  158.7 0.6 collective-permute-start.24
  159.2 3.6 %collective-permute-done.24 = f32[96,128]{1,0:T(8,128)S(1)} collective-permute-done((f32[96,128]{1,0:T(8,128)S(1)}, f32[96,128]{1,0:T(8,128)S(1)}, u32[]{:S(2)}, u32[]{:S(2)}) %collective-permute-start.24) | collective-permute-done | bytes 49184 | tf_op jit(solution)/shard_map/ppermute | solution.py:85
  162.9 0.6 add.25.feat_ref
  164.1 0.6 copy-done.19
  164.8 2.1 %sketch.1.refs_0_ = f32[3,32,128]{2,1,0:T(8,128)} custom-call(s32[4]{0:T(128)} %copy-done.9, f32[192,128]{1,0:T(8,128)} %add.25.feat_ref, f32[96,128]{1,0:T(8,128)} %copy-done.16, f32[96,128]{1,0:T(8,128)} %copy-done.19), custom_call_target="tpu_custom_call" | custom-call | tf_op jit(solution)/shard_map/sketch/pallas_call | solution.py:230
  166.8 1.0 collective-permute-start.26
  167.8 1.7 collective-permute-start.27
  169.5 1.7 collective-permute-start.28
  171.2 3.3 %collective-permute-done.27.refs_2_ = f32[3,32,128]{2,1,0:T(8,128)S(1)} collective-permute-done((f32[3,32,128]{2,1,0:T(8,128)}, f32[3,32,128]{2,1,0:T(8,128)S(1)}, u32[]{:S(2)}, u32[]{:S(2)}) %collective-permute-start.27) | collective-permute-done | bytes 49184 | tf_op jit(solution)/shard_map/ppermute | solution.py:85
  174.5 1.1 collective-permute-done.28.refs_3_
  175.6 4.6 %copy-done.2 = f32[3,256,4096]{2,1,0:T(8,128)S(1)} copy-done((f32[3,256,4096]{2,1,0:T(8,128)S(1)}, f32[3,256,4096]{2,1,0:T(8,128)}, u32[]{:S(2)}) %copy-start.2) | copy-done | bytes 12582936
  180.2 0.8 copy-done.8
  181.0 6.2 %precond.1 = f32[3,4,256]{2,1,0:T(4,128)} custom-call(s32[1]{0:T(128)} %bitcast.row_ref, f32[3,256,4096]{2,1,0:T(8,128)S(1)} %copy-done.2, f32[3,32,128]{2,1,0:T(8,128)S(1)} %copy-done.8, f32[3,32,128]{2,1,0:T(8,128)S(1)} %collective-permute-done.26.refs_1_, f32[3,32,128]{2,1,0:T(8,128)S(1)} %collective-permute-done.27.refs_2_, ...), custom_call_target="tpu_custom_call" | custom-call | tf_op jit(solution)/shard_map/precond/pallas_call | solution.py:273
  (71 shorter events, 4.4 us)
Async XLA Ops:
  1.3 26.4 %collective-permute-start = (bf16[2,128,2048]{2,1,0:T(8,128)(2,1)S(1)}, bf16[2,128,2048]{2,1,0:T(8,128)(2,1)}, u32[]{:S(2)}, u32[]{:S(2)}) collective-permute-start(bf16[2,128,2048]{2,1,0:T(8,128)(2,1)S(1)} %pad_maximum_fusion.refs_1_), channel_id=1, source_target_pairs={{0,1},{1,0},{2,3},{3,2},{4,5},{5,4},{6,7},{7,6},{8,9},{9,8},{10,11... | collective-permute-start | bytes 3145736 | tf_op jit(solution)/shard_map/ppermute | solution.py:85
  4.4 23.3 %collective-permute-start.1 = (bf16[2,128,2048]{2,1,0:T(8,128)(2,1)S(1)}, bf16[2,128,2048]{2,1,0:T(8,128)(2,1)S(1)}, u32[]{:S(2)}, u32[]{:S(2)}) collective-permute-start(bf16[2,128,2048]{2,1,0:T(8,128)(2,1)S(1)} %pad_maximum_fusion.refs_1_), channel_id=1, source_target_pairs={{1,2},{2,1},{5,6},{6,5},{9,10},{10,9},{13,14},{14,13},{17,18},{18,... | collective-permute-start | bytes 3145736 | tf_op jit(solution)/shard_map/ppermute | solution.py:85
  5.1 24.7 %collective-permute-start.2 = (bf16[2,128,2048]{2,1,0:T(8,128)(2,1)S(1)}, bf16[2,128,2048]{2,1,0:T(8,128)(2,1)S(1)}, u32[]{:S(2)}, u32[]{:S(2)}) collective-permute-start(bf16[2,128,2048]{2,1,0:T(8,128)(2,1)S(1)} %pad_maximum_fusion.refs_1_), channel_id=1, source_target_pairs={{0,8},{1,9},{2,10},{3,11},{4,12},{5,13},{6,14},{7,15},{8,0},{9,1},... | collective-permute-start | bytes 3145736 | tf_op jit(solution)/shard_map/ppermute | solution.py:85
  6.7 23.1 %collective-permute-start.3 = (bf16[2,128,2048]{2,1,0:T(8,128)(2,1)S(1)}, bf16[2,128,2048]{2,1,0:T(8,128)(2,1)S(1)}, u32[]{:S(2)}, u32[]{:S(2)}) collective-permute-start(bf16[2,128,2048]{2,1,0:T(8,128)(2,1)S(1)} %pad_maximum_fusion.refs_1_), channel_id=1, source_target_pairs={{0,4},{1,5},{2,6},{3,7},{4,0},{5,1},{6,2},{7,3},{8,12},{9,13},{10,... | collective-permute-start | bytes 3145736 | tf_op jit(solution)/shard_map/ppermute | solution.py:85
  9.7 1.5 collective-permute-start.4
  11.2 47.4 %copy-start.14 = (f32[192,128]{1,0:T(8,128)}, f32[192,128]{1,0:T(8,128)S(1)}, u32[]{:S(2)}) copy-start(f32[192,128]{1,0:T(8,128)S(1)} %fusion.4) | copy-start | bytes 294916
  27.7 2.1 %copy-start.10 = (bf16[2,128,2048]{2,1,0:T(8,128)(2,1)}, bf16[2,128,2048]{2,1,0:T(8,128)(2,1)S(1)}, u32[]{:S(2)}) copy-start(bf16[2,128,2048]{2,1,0:T(8,128)(2,1)S(1)} %collective-permute-done.1) | copy-start | bytes 3145732
  29.8 1.0 copy-start.4
  30.8 4.1 %collective-permute-start.10 = (bf16[2,128,2048]{2,1,0:T(8,128)(2,1)}, bf16[2,128,2048]{2,1,0:T(8,128)(2,1)}, u32[]{:S(2)}, u32[]{:S(2)}) collective-permute-start(bf16[2,128,2048]{2,1,0:T(8,128)(2,1)} %collective-permute-done.refs_2_), channel_id=1, source_target_pairs={{0,4},{1,5},{2,6},{3,7},{4,0},{5,1},{6,2},{7,3},{8,12},{9,13},{10,... | collective-permute-start | bytes 3145736 | tf_op jit(solution)/shard_map/ppermute | solution.py:85
  30.9 95.8 %copy-start.9 = (s32[4]{0:T(128)}, s32[4]{0:T(128)S(1)}, u32[]{:S(2)}) copy-start(s32[4]{0:T(128)S(1)} %pad_add_fusion.refs_0_.where_ref) | copy-start | bytes 52
  30.9 39.1 %copy-start.3 = (bf16[1792,192]{0,1:T(8,128)(2,1)S(1)}, bf16[1792,192]{0,1:T(8,128)(2,1)}, u32[]{:S(2)}) copy-start(bf16[1792,192]{0,1:T(8,128)(2,1)} %param.12) | copy-start | bytes 2064388
  30.9 30.1 %collective-permute-start.6 = (bf16[2,128,2048]{2,1,0:T(8,128)(2,1)}, bf16[2,128,2048]{2,1,0:T(8,128)(2,1)S(1)}, u32[]{:S(2)}, u32[]{:S(2)}) collective-permute-start(bf16[2,128,2048]{2,1,0:T(8,128)(2,1)} %collective-permute-done.refs_2_), channel_id=1, source_target_pairs={{1,2},{2,1},{5,6},{6,5},{9,10},{10,9},{13,14},{14,13},{17,18},{18,... | collective-permute-start | bytes 3145736 | tf_op jit(solution)/shard_map/ppermute | solution.py:85
  31.7 29.3 %collective-permute-start.7 = (bf16[2,128,2048]{2,1,0:T(8,128)(2,1)}, bf16[2,128,2048]{2,1,0:T(8,128)(2,1)}, u32[]{:S(2)}, u32[]{:S(2)}) collective-permute-start(bf16[2,128,2048]{2,1,0:T(8,128)(2,1)} %collective-permute-done.refs_2_), channel_id=1, source_target_pairs={{0,8},{1,9},{2,10},{3,11},{4,12},{5,13},{6,14},{7,15},{8,0},{9,1},... | collective-permute-start | bytes 3145736 | tf_op jit(solution)/shard_map/ppermute | solution.py:85
  33.3 31.2 %collective-permute-start.5 = (bf16[2,128,2048]{2,1,0:T(8,128)(2,1)}, bf16[2,128,2048]{2,1,0:T(8,128)(2,1)S(1)}, u32[]{:S(2)}, u32[]{:S(2)}) collective-permute-start(bf16[2,128,2048]{2,1,0:T(8,128)(2,1)} %copy-done.10), channel_id=1, source_target_pairs={{1,0},{2,3},{5,4},{6,7},{9,8},{10,11},{13,12},{14,15},{17,16},{18,... | collective-permute-start | bytes 3145736 | tf_op jit(solution)/shard_map/ppermute | solution.py:85
  34.6 29.9 %collective-permute-start.8 = (bf16[2,128,2048]{2,1,0:T(8,128)(2,1)S(1)}, bf16[2,128,2048]{2,1,0:T(8,128)(2,1)S(1)}, u32[]{:S(2)}, u32[]{:S(2)}) collective-permute-start(bf16[2,128,2048]{2,1,0:T(8,128)(2,1)S(1)} %collective-permute-done.2.refs_1_), channel_id=1, source_target_pairs={{0,4},{1,5},{2,6},{3,7},{4,0},{5,1},{6,2},{7,3},{8,12},{9,13},{10,... | collective-permute-start | bytes 3145736 | tf_op jit(solution)/shard_map/ppermute | solution.py:85
  34.9 26.1 %collective-permute-start.9 = (f32[192,128]{1,0:T(8,128)S(1)}, f32[192,128]{1,0:T(8,128)S(1)}, u32[]{:S(2)}, u32[]{:S(2)}) collective-permute-start(f32[192,128]{1,0:T(8,128)S(1)} %fusion.4), channel_id=1, source_target_pairs={{0,8},{1,9},{2,10},{3,11},{4,12},{5,13},{6,14},{7,15},{8,0},{9,1},... | collective-permute-start | bytes 294920 | tf_op jit(solution)/shard_map/ppermute | solution.py:85
  35.4 1.2 copy-start.5
  58.6 2.4 %copy-start = (f32[7,3,256,256]{3,2,1,0:T(8,128)}, f32[7,3,256,256]{3,2,1,0:T(8,128)S(1)}, u32[]{:S(2)}) copy-start(f32[7,3,256,256]{3,2,1,0:T(8,128)S(1)} %matmul.4.refs_9_) | copy-start | bytes 16515076
  61.0 3.5 %copy-start.17 = (f32[192,128]{1,0:T(8,128)}, f32[192,128]{1,0:T(8,128)S(1)}, u32[]{:S(2)}) copy-start(f32[192,128]{1,0:T(8,128)S(1)} %collective-permute-done.9) | copy-start | bytes 294916
  61.0 3.5 %copy-start.11 = (bf16[2,128,2048]{2,1,0:T(8,128)(2,1)}, bf16[2,128,2048]{2,1,0:T(8,128)(2,1)S(1)}, u32[]{:S(2)}) copy-start(bf16[2,128,2048]{2,1,0:T(8,128)(2,1)S(1)} %collective-permute-done.6) | copy-start | bytes 3145732
  64.5 1.0 copy-start.13
  65.5 1.0 copy-start.6
  66.5 3.5 %collective-permute-start.14 = (bf16[2,128,2048]{2,1,0:T(8,128)(2,1)}, bf16[2,128,2048]{2,1,0:T(8,128)(2,1)S(1)}, u32[]{:S(2)}, u32[]{:S(2)}) collective-permute-start(bf16[2,128,2048]{2,1,0:T(8,128)(2,1)} %collective-permute-done.7.refs_2_), channel_id=1, source_target_pairs={{0,4},{1,5},{2,6},{3,7},{4,0},{5,1},{6,2},{7,3},{8,12},{9,13},{10,... | collective-permute-start | bytes 3145736 | tf_op jit(solution)/shard_map/ppermute | solution.py:85
  66.5 31.7 %copy-start.12 = (bf16[2,128,2048]{2,1,0:T(8,128)(2,1)S(1)}, bf16[2,128,2048]{2,1,0:T(8,128)(2,1)}, u32[]{:S(2)}) copy-start(bf16[2,128,2048]{2,1,0:T(8,128)(2,1)} %copy-done.11) | copy-start | bytes 3145732
  67.9 28.9 %collective-permute-start.12 = (bf16[2,128,2048]{2,1,0:T(8,128)(2,1)S(1)}, bf16[2,128,2048]{2,1,0:T(8,128)(2,1)S(1)}, u32[]{:S(2)}, u32[]{:S(2)}) collective-permute-start(bf16[2,128,2048]{2,1,0:T(8,128)(2,1)S(1)} %broadcast_select_fusion.1.refs_1_), channel_id=1, source_target_pairs={{0,8},{1,9},{2,10},{3,11},{4,12},{5,13},{6,14},{7,15},{8,0},{9,1},... | collective-permute-start | bytes 3145736 | tf_op jit(solution)/shard_map/ppermute | solution.py:85
  68.5 28.3 %collective-permute-start.13 = (bf16[2,128,2048]{2,1,0:T(8,128)(2,1)S(1)}, bf16[2,128,2048]{2,1,0:T(8,128)(2,1)S(1)}, u32[]{:S(2)}, u32[]{:S(2)}) collective-permute-start(bf16[2,128,2048]{2,1,0:T(8,128)(2,1)S(1)} %broadcast_select_fusion.1.refs_1_), channel_id=1, source_target_pairs={{0,4},{1,5},{2,6},{3,7},{4,0},{5,1},{6,2},{7,3},{8,12},{9,13},{10,... | collective-permute-start | bytes 3145736 | tf_op jit(solution)/shard_map/ppermute | solution.py:85
  68.7 29.5 %collective-permute-start.11 = (bf16[2,128,2048]{2,1,0:T(8,128)(2,1)}, bf16[2,128,2048]{2,1,0:T(8,128)(2,1)S(1)}, u32[]{:S(2)}, u32[]{:S(2)}) collective-permute-start(bf16[2,128,2048]{2,1,0:T(8,128)(2,1)} %copy-done.11), channel_id=1, source_target_pairs={{1,0},{2,3},{5,4},{6,7},{9,8},{10,11},{13,12},{14,15},{17,16},{18,... | collective-permute-start | bytes 3145736 | tf_op jit(solution)/shard_map/ppermute | solution.py:85
  70.0 2.6 %copy-start.1 = (f32[7,3,256,256]{3,2,1,0:T(8,128)S(1)}, f32[7,3,256,256]{3,2,1,0:T(8,128)}, u32[]{:S(2)}) copy-start(f32[7,3,256,256]{3,2,1,0:T(8,128)} %copy-done) | copy-start | bytes 16515076
  72.6 1.2 copy-start.7
  98.3 2.9 %collective-permute-start.18 = (bf16[2,128,2048]{2,1,0:T(8,128)(2,1)S(1)}, bf16[2,128,2048]{2,1,0:T(8,128)(2,1)S(1)}, u32[]{:S(2)}, u32[]{:S(2)}) collective-permute-start(bf16[2,128,2048]{2,1,0:T(8,128)(2,1)S(1)} %broadcast_select_fusion.refs_2_), channel_id=1, source_target_pairs={{0,4},{1,5},{2,6},{3,7},{4,0},{5,1},{6,2},{7,3},{8,12},{9,13},{10,... | collective-permute-start | bytes 3145736 | tf_op jit(solution)/shard_map/ppermute | solution.py:85
  98.3 2.8 %collective-permute-start.17 = (f32[96,256]{1,0:T(8,128)S(1)}, f32[96,256]{1,0:T(8,128)S(1)}, u32[]{:S(2)}, u32[]{:S(2)}) collective-permute-start(f32[96,256]{1,0:T(8,128)S(1)} %get-tuple-element.47), channel_id=1, source_target_pairs={{0,4},{1,5},{2,6},{3,7},{4,0},{5,1},{6,2},{7,3},{8,12},{9,13},{10,... | collective-permute-start | bytes 294920 | tf_op jit(solution)/shard_map/ppermute | solution.py:85
  98.8 25.1 %collective-permute-start.15 = (bf16[2,128,2048]{2,1,0:T(8,128)(2,1)S(1)}, bf16[2,128,2048]{2,1,0:T(8,128)(2,1)S(1)}, u32[]{:S(2)}, u32[]{:S(2)}) collective-permute-start(bf16[2,128,2048]{2,1,0:T(8,128)(2,1)S(1)} %broadcast_select_fusion.refs_2_), channel_id=1, source_target_pairs={{0,8},{1,9},{2,10},{3,11},{4,12},{5,13},{6,14},{7,15},{8,0},{9,1},... | collective-permute-start | bytes 3145736 | tf_op jit(solution)/shard_map/ppermute | solution.py:85
  99.4 24.6 %collective-permute-start.16 = (bf16[2,128,2048]{2,1,0:T(8,128)(2,1)S(1)}, bf16[2,128,2048]{2,1,0:T(8,128)(2,1)S(1)}, u32[]{:S(2)}, u32[]{:S(2)}) collective-permute-start(bf16[2,128,2048]{2,1,0:T(8,128)(2,1)S(1)} %collective-permute-done.12.refs_1_), channel_id=1, source_target_pairs={{0,4},{1,5},{2,6},{3,7},{4,0},{5,1},{6,2},{7,3},{8,12},{9,13},{10,... | collective-permute-start | bytes 3145736 | tf_op jit(solution)/shard_map/ppermute | solution.py:85
  120.8 42.2 %copy-start.15 = (f32[192,128]{1,0:T(8,128)S(1)}, f32[192,128]{1,0:T(8,128)}, u32[]{:S(2)}) copy-start(f32[192,128]{1,0:T(8,128)} %copy-done.14) | copy-start | bytes 294916
  120.8 42.2 %copy-start.18 = (f32[192,128]{1,0:T(8,128)S(1)}, f32[192,128]{1,0:T(8,128)}, u32[]{:S(2)}) copy-start(f32[192,128]{1,0:T(8,128)} %copy-done.17) | copy-start | bytes 294916
  124.0 2.7 %collective-permute-start.20 = (bf16[2,128,2048]{2,1,0:T(8,128)(2,1)S(1)}, bf16[2,128,2048]{2,1,0:T(8,128)(2,1)S(1)}, u32[]{:S(2)}, u32[]{:S(2)}) collective-permute-start(bf16[2,128,2048]{2,1,0:T(8,128)(2,1)S(1)} %collective-permute-done.15.refs_2_), channel_id=1, source_target_pairs={{0,4},{1,5},{2,6},{3,7},{4,0},{5,1},{6,2},{7,3},{8,12},{9,13},{10,... | collective-permute-start | bytes 3145736 | tf_op jit(solution)/shard_map/ppermute | solution.py:85
  147.6 3.5 %collective-permute-start.21 = (f32[96,256]{1,0:T(8,128)S(1)}, f32[96,256]{1,0:T(8,128)S(1)}, u32[]{:S(2)}, u32[]{:S(2)}) collective-permute-start(f32[96,256]{1,0:T(8,128)S(1)} %get-tuple-element.54), channel_id=1, source_target_pairs={{0,4},{1,5},{2,6},{3,7},{4,0},{5,1},{6,2},{7,3},{8,12},{9,13},{10,... | collective-permute-start | bytes 294920 | tf_op jit(solution)/shard_map/ppermute | solution.py:85
  147.8 7.0 %collective-permute-start.19 = (f32[96,128]{1,0:T(8,128)S(1)}, f32[96,128]{1,0:T(8,128)S(1)}, u32[]{:S(2)}, u32[]{:S(2)}) collective-permute-start(f32[96,128]{1,0:T(8,128)S(1)} %slice.21), channel_id=1, source_target_pairs={{0,1},{1,0},{2,3},{3,2},{4,5},{5,4},{6,7},{7,6},{8,9},{9,8},{10,11... | collective-permute-start | bytes 147464 | tf_op jit(solution)/shard_map/ppermute | solution.py:85
  151.2 6.8 %collective-permute-start.22 = (f32[96,128]{1,0:T(8,128)S(1)}, f32[96,128]{1,0:T(8,128)S(1)}, u32[]{:S(2)}, u32[]{:S(2)}) collective-permute-start(f32[96,128]{1,0:T(8,128)S(1)} %get-tuple-element.55), channel_id=1, source_target_pairs={{0,2},{1,3},{2,0},{3,1},{4,6},{5,7},{6,4},{7,5},{8,10},{9,11},{10,... | collective-permute-start | bytes 147464 | tf_op jit(solution)/shard_map/ppermute | solution.py:85
  152.7 6.0 %collective-permute-start.23 = (f32[96,128]{1,0:T(8,128)S(1)}, f32[96,128]{1,0:T(8,128)S(1)}, u32[]{:S(2)}, u32[]{:S(2)}) collective-permute-start(f32[96,128]{1,0:T(8,128)S(1)} %get-tuple-element.56), channel_id=1, source_target_pairs={{0,3},{1,2},{2,1},{3,0},{4,7},{5,6},{6,5},{7,4},{8,11},{9,10},{10,... | collective-permute-start | bytes 147464 | tf_op jit(solution)/shard_map/ppermute | solution.py:85
  158.7 4.2 %collective-permute-start.24 = (f32[96,128]{1,0:T(8,128)S(1)}, f32[96,128]{1,0:T(8,128)S(1)}, u32[]{:S(2)}, u32[]{:S(2)}) collective-permute-start(f32[96,128]{1,0:T(8,128)S(1)} %add_add_fusion), channel_id=1, source_target_pairs={{0,8},{1,9},{2,10},{3,11},{4,12},{5,13},{6,14},{7,15},{8,0},{9,1},... | collective-permute-start | bytes 147464 | tf_op jit(solution)/shard_map/ppermute | solution.py:85
  162.8 1.3 copy-start.16
  162.8 1.3 collective-permute-start.25
  166.8 4.4 %collective-permute-start.26 = (f32[3,32,128]{2,1,0:T(8,128)}, f32[3,32,128]{2,1,0:T(8,128)S(1)}, u32[]{:S(2)}, u32[]{:S(2)}) collective-permute-start(f32[3,32,128]{2,1,0:T(8,128)} %sketch.1.refs_0_), channel_id=1, source_target_pairs={{0,1},{1,0},{2,3},{3,2},{4,5},{5,4},{6,7},{7,6},{8,9},{9,8},{10,11... | collective-permute-start | bytes 147464 | tf_op jit(solution)/shard_map/ppermute | solution.py:85
  167.8 6.7 %collective-permute-start.27 = (f32[3,32,128]{2,1,0:T(8,128)}, f32[3,32,128]{2,1,0:T(8,128)S(1)}, u32[]{:S(2)}, u32[]{:S(2)}) collective-permute-start(f32[3,32,128]{2,1,0:T(8,128)} %sketch.1.refs_0_), channel_id=1, source_target_pairs={{0,2},{1,3},{2,0},{3,1},{4,6},{5,7},{6,4},{7,5},{8,10},{9,11},{10,... | collective-permute-start | bytes 147464 | tf_op jit(solution)/shard_map/ppermute | solution.py:85
  169.5 6.1 %collective-permute-start.28 = (f32[3,32,128]{2,1,0:T(8,128)}, f32[3,32,128]{2,1,0:T(8,128)S(1)}, u32[]{:S(2)}, u32[]{:S(2)}) collective-permute-start(f32[3,32,128]{2,1,0:T(8,128)} %sketch.1.refs_0_), channel_id=1, source_target_pairs={{0,3},{1,2},{2,1},{3,0},{4,7},{5,6},{6,5},{7,4},{8,11},{9,10},{10,... | collective-permute-start | bytes 147464 | tf_op jit(solution)/shard_map/ppermute | solution.py:85
  175.6 4.6 %copy-start.2 = (f32[3,256,4096]{2,1,0:T(8,128)S(1)}, f32[3,256,4096]{2,1,0:T(8,128)}, u32[]{:S(2)}) copy-start(f32[3,256,4096]{2,1,0:T(8,128)} %p_ref.1) | copy-start | bytes 37748740
  180.2 0.8 copy-start.8
  (1 other events, 0.6 us)

commit v3 on v2

--- a/solution.py
+++ b/solution.py
@@ -160,30 +160,31 @@
     in_specs, operands = [], []
     for _, pieces in blocks:
         for piece in pieces:
-            in_specs.append(pl.BlockSpec(memory_space=pl.ANY))
-            operands.append(piece)
+            in_specs.append(whole)
+            operands.append(pltpu.with_memory_space_constraint(piece, pltpu.VMEM))
     for owner, _ in blocks:
         in_specs.append(pl.BlockSpec((2, tile, width), lambda i, r, o=owner: (0, i, r[o])))
         operands.append(pltpu.with_memory_space_constraint(w_gate_up, pltpu.HBM))
     for owner, _ in blocks:
         in_specs.append(pl.BlockSpec((tile, width), lambda i, r, o=owner: (i, r[o])))
         operands.append(pltpu.with_memory_space_constraint(w_down, pltpu.HBM))
-    need = count * width * (2 * tokens + 2 * 3 * tile) * 2 + 6 * MIB
+    need = count * width * (2 * tokens + 2 * 3 * tile) * 2 + 4 * MIB
     scratch = [pltpu.VMEM((2, tokens, width), jnp.bfloat16) for _ in blocks]
     scratch.append(pltpu.SemaphoreType.DMA((2 * count,)))
     if last:
         in_specs.append(whole)
         operands.append(pltpu.with_memory_space_constraint(acc, pltpu.VMEM))
+        out_shape, out_specs = [], []
+    else:
+        out_shape, out_specs = [pltpu.VMEM((tiles, 3, tokens, tile), jnp.float32)], [whole]
+    if last:
         in_specs.append(pl.BlockSpec((3 * K, tile), lambda i, r: (0, i)))
         operands.append(unit_proj_t)
         half = jax.ShapeDtypeStruct((3 * K // 2, tokens), jnp.float32)
-        out_shape = (half, half)
-        out_specs = (pl.BlockSpec(half.shape, lambda i, r: (0, 0)),) * 2
+        out_shape += [half] * 2
+        out_specs += [pl.BlockSpec(half.shape, lambda i, r: (0, 0))] * 2
         scratch.append(pltpu.VMEM((3 * K, tokens), jnp.float32))
-        need += 6 * MIB
-    else:
-        out_shape = pltpu.VMEM((tiles, 3, tokens, tile), jnp.float32)
-        out_specs = whole
+        need += 4 * MIB
     return pl.pallas_call(
         functools.partial(matmul_kernel, count, last),
         out_shape=out_shape,
@@ -233,6 +234,7 @@
         in_specs=[pl.BlockSpec(memory_space=pltpu.SMEM), whole, whole, whole],
         out_specs=whole,
         scratch_shapes=[pltpu.VMEM((3 * K, SEQ), jnp.float32)],
+        compiler_params=pltpu.CompilerParams(vmem_limit_bytes=4 * MIB),
         name="sketch",
     )(where, feat_t, mine, other)
 
@@ -280,7 +282,7 @@
             out_specs=pl.BlockSpec((1, ROWS, height), lambda w, r: (w, 0, 0)),
             scratch_shapes=[pltpu.VMEM((ROWS, height, 2 * K), jnp.float32)],
         ),
-        compiler_params=pltpu.CompilerParams(vmem_limit_bytes=24 * MIB),
+        compiler_params=pltpu.CompilerParams(vmem_limit_bytes=12 * MIB),
         name="precond",
     )(row, precond, *sketches)
 
@@ -306,6 +308,8 @@
     tensor, row = lax.axis_index("tensor"), lax.axis_index("dp")
     inner = jnp.logical_or(row == 1, row == 2)
     where = jnp.stack([tensor, tensor ^ 1, tensor ^ 2, tensor ^ 3]).astype(jnp.int32)
+    row = row.astype(jnp.int32).reshape(1)
+    hidden_in, out_grad, where, row, inner = tie(hidden_in, out_grad, where, row, inner)
     step = functools.partial(matmul_step, where)
 
     own = jnp.stack([hidden_in, out_grad])
@@ -334,7 +338,7 @@
     near_y = other_chip(near)
     own_d = other_core(own_y)
     feat_y = other_chip(feat_t)
-    acc = step([(A, (own, near)), (C, (own_c, near_c))], w_gate_up, w_down)
+    (acc,) = step([(A, (own, near)), (C, (own_c, near_c))], w_gate_up, w_down)
     passed, middle_2, near_y, own_d, feat_y, acc = tie(passed, middle_2, near_y, own_d, feat_y, acc)
     feat_t = feat_t + feat_y
 
@@ -346,22 +350,24 @@
     mine_0, theirs_0 = step(
         [(Y, (own_y, near_y)), (D, (own_d, near_d))], w_gate_up, w_down, acc, unit_proj_t
     )
-    passed_2, third_y, third_c, mine_0, theirs_0 = tie(passed_2, third_y, third_c, mine_0, theirs_0)
+    passed_2, third_y, third_c, mine_0, theirs_0, feat_t = tie(
+        passed_2, third_y, third_c, mine_0, theirs_0, feat_t
+    )
 
     fourth = jnp.where(inner, middle_2, passed_2)
     fourth_c = other_core(fourth)
     fourth_y = other_chip(fourth)
     third_d = other_core(third_y)
     mine_0 = mine_0 + other_core(theirs_0)
-    acc = step([(A, (third, fourth)), (C, (third_c, fourth_c))], w_gate_up, w_down)
-    fourth_y, third_d, mine_0, acc = tie(fourth_y, third_d, mine_0, acc)
+    part = mine_0[:, :SEQ] + send(mine_0[:, SEQ:], swap_rows(1))
+    (acc,) = step([(A, (third, fourth)), (C, (third_c, fourth_c))], w_gate_up, w_down)
+    fourth_y, third_d, part, acc = tie(fourth_y, third_d, part, acc)
 
     fourth_d = other_core(fourth_y)
     mine_1, theirs_1 = step(
         [(Y, (third_y, fourth_y)), (D, (third_d, fourth_d))], w_gate_up, w_down, acc, unit_proj_t
     )
 
-    part = mine_0[:, :SEQ] + send(mine_0[:, SEQ:], swap_rows(1))
     mine_1 = mine_1 + other_core(theirs_1)
     low, high = mine_1[:, :SEQ], mine_1[:, SEQ:]
     part = part + send(jnp.where(inner, high, low), swap_rows(2)) + send(jnp.where(inner, low, high), swap_rows(3))
@@ -369,7 +375,7 @@
     other = other_core(part)
     sketch = sketch_own(where, feat_t, part, other)
     sketches = [sketch] + [send(sketch, swap_rows(n)) for n in range(1, ROWS)]
-    return apply_precond(row.astype(jnp.int32).reshape(1), precond, sketches)
+    return apply_precond(row, precond, sketches)
 
 
 def local(hidden_in, out_grad, w_gate_up, w_down, feat_proj, unit_proj, precond):

time: 188 us -> 174 us (0.926)
  local copies, waits for them, and re-layouts: 16.4 us -> 0.03 us
  waiting for transfers between devices: 44.5 us -> 54.3 us
  Pallas kernels: 93.7 us -> 89.5 us
  other arithmetic: 3.63 us -> 1.69 us
    unnamed x40 -> x8, local copies, waits for them, and re-layouts: 16.4 us -> 0.02 us
    ppermute x29, waiting for transfers between devices: 44.5 us -> 54.3 us  [send(): return lax.ppermute(value, BOTH, pairs)]
    pallas_call x4, Pallas kernels: 85.4 us -> 81.7 us  [matmul_step(): pl.pallas_call(functools.partial(matmul_kernel, count, last), out_shape=o...]
  transfers between devices with their start and end apart: 29 -> 29, of which waited for: 14 -> 20; matrix products, arithmetic and copies ran while one was open for 3% -> 2% of each run, Pallas kernels for 34% -> 35%
where the time goes in v3:
time: 174 us
  Pallas kernels  89.5 us (51%)
  waiting for transfers between devices  54.3 us (31%)
  starting transfers between devices  25.1 us (14%)
  matrix products  2.9 us (2%)
    pallas_call x4, Pallas kernels, matmul_step(): pl.pallas_call(functools.partial(matmul_kernel, count, last), out_shape=o...  81.7 us
    ppermute x29, waiting for transfers between devices, send(): return lax.ppermute(value, BOTH, pairs)  54.3 us
    ppermute x29, starting transfers between devices, send(): return lax.ppermute(value, BOTH, pairs)  25.1 us
    pallas_call x1, Pallas kernels, apply_precond(): pl.pallas_call(precond_kernel, out_shape=jax.ShapeDtypeStruct((3, ROWS, h...  6.79 us
  transfers between devices with their start and end apart: 29, of which 20 were waited for; matrix products, arithmetic and copies ran while one was open for 2% of the time, Pallas kernels for 35%

profile of v3, /device:TPU:0, one launch (start us, length us, event | category | flops | bytes accessed | tf_op | source)
XLA Modules:
  0.0 173.8 jit_solution(6011499830718302681)
XLA Ops:
  0.1 1.3 pad_maximum_fusion.refs_1_
  1.4 3.1 %collective-permute-start = (bf16[2,128,2048]{2,1,0:T(8,128)(2,1)S(1)}, bf16[2,128,2048]{2,1,0:T(8,128)(2,1)S(1)}, u32[]{:S(2)}, u32[]{:S(2)}) collective-permute-start(bf16[2,128,2048]{2,1,0:T(8,128)(2,1)S(1)} %pad_maximum_fusion.refs_1_), channel_id=1, source_target_pairs={{0,1},{1,0},{2,3},{3,2},{4,5},{5,4},{6,7},{7,6},{8,9},{9,8},{10,11... | collective-permute-start | bytes 3145736 | tf_op jit(solution)/shard_map/ppermute | solution.py:85
  4.5 0.7 collective-permute-start.1
  5.2 1.6 collective-permute-start.2
  6.8 1.4 convolution_bitcast_fusion.1
  8.2 1.5 convolution_bitcast_fusion
  9.7 0.6 collective-permute-start.4
  10.3 0.9 collective-permute-done.4
  11.2 16.4 %collective-permute-done.refs_2_ = bf16[2,128,2048]{2,1,0:T(8,128)(2,1)S(1)} collective-permute-done((bf16[2,128,2048]{2,1,0:T(8,128)(2,1)S(1)}, bf16[2,128,2048]{2,1,0:T(8,128)(2,1)S(1)}, u32[]{:S(2)}, u32[]{:S(2)}) %collective-permute-start) | collective-permute-done | bytes 1048608 | tf_op jit(solution)/shard_map/ppermute | solution.py:85
  27.6 2.2 %collective-permute-done.2.refs_1_ = bf16[2,128,2048]{2,1,0:T(8,128)(2,1)S(1)} collective-permute-done((bf16[2,128,2048]{2,1,0:T(8,128)(2,1)S(1)}, bf16[2,128,2048]{2,1,0:T(8,128)(2,1)S(1)}, u32[]{:S(2)}, u32[]{:S(2)}) %collective-permute-start.2) | collective-permute-done | bytes 1048608 | tf_op jit(solution)/shard_map/ppermute | solution.py:85
  29.9 0.9 collective-permute-start.6
  30.8 1.6 collective-permute-start.7
  32.4 1.3 collective-permute-start.5
  33.8 0.5 collective-permute-start.9
  34.3 19.6 %matmul.4.refs_9_ = f32[7,3,256,256]{3,2,1,0:T(8,128)S(1)} custom-call(s32[4]{0:T(128)S(1)} %pad_add_fusion.refs_0_.where_ref, bf16[2,128,2048]{2,1,0:T(8,128)(2,1)S(1)} %pad_maximum_fusion.refs_1_, bf16[2,128,2048]{2,1,0:T(8,128)(2,1)S(1)} %collective-permute-done.refs_2_, bf16[2,128,2048]{2,1,0:T(8,128)(2,1)S(1)} %collective-permute-done.3.refs_3_, ...), custom_call_target="tpu_custom_call" | custom-call | flops 11274289152 | bytes 44040192 | tf_op jit(solution)/shard_map/matmul/pallas_call | solution.py:188
  53.9 4.5 %collective-permute-done.9 = f32[192,128]{1,0:T(8,128)S(1)} collective-permute-done((f32[192,128]{1,0:T(8,128)S(1)}, f32[192,128]{1,0:T(8,128)S(1)}, u32[]{:S(2)}, u32[]{:S(2)}) %collective-permute-start.9) | collective-permute-done | bytes 98336 | tf_op jit(solution)/shard_map/ppermute | solution.py:85
  58.4 3.9 %collective-permute-done.5 = bf16[2,128,2048]{2,1,0:T(8,128)(2,1)S(1)} collective-permute-done((bf16[2,128,2048]{2,1,0:T(8,128)(2,1)S(1)}, bf16[2,128,2048]{2,1,0:T(8,128)(2,1)S(1)}, u32[]{:S(2)}, u32[]{:S(2)}) %collective-permute-start.5) | collective-permute-done | bytes 1048608 | tf_op jit(solution)/shard_map/ppermute | solution.py:85
  62.5 0.6 collective-permute-start.12
  63.0 0.2 collective-permute-start.13
  63.3 1.3 collective-permute-start.11
  64.6 0.4 collective-permute-done.14.refs_4_
  65.0 21.0 %matmul.5 = (f32[96,256]{1,0:T(8,128)S(1)}, f32[96,256]{1,0:T(8,128)S(1)}) custom-call(s32[4]{0:T(128)S(1)} %pad_add_fusion.refs_0_.where_ref, bf16[2,128,2048]{2,1,0:T(8,128)(2,1)S(1)} %collective-permute-done.2.refs_1_, bf16[2,128,2048]{2,1,0:T(8,128)(2,1)S(1)} %collective-permute-done.7.refs_2_, bf16[2,128,2048]{2,1,0:T(8,128)(2,1)S(1)} %collective-permute-done.8.refs_3_, ...), custom_call_target="tpu_custom_call" | custom-call | flops 11274289152 | bytes 44040192 | tf_op jit(solution)/shard_map/matmul/pallas_call | solution.py:188
  86.0 2.1 %collective-permute-done.12.refs_1_ = bf16[2,128,2048]{2,1,0:T(8,128)(2,1)S(1)} collective-permute-done((bf16[2,128,2048]{2,1,0:T(8,128)(2,1)S(1)}, bf16[2,128,2048]{2,1,0:T(8,128)(2,1)S(1)}, u32[]{:S(2)}, u32[]{:S(2)}) %collective-permute-start.12) | collective-permute-done | bytes 1048608 | tf_op jit(solution)/shard_map/ppermute | solution.py:85
  88.1 2.4 %collective-permute-done.11 = bf16[2,128,2048]{2,1,0:T(8,128)(2,1)S(1)} collective-permute-done((bf16[2,128,2048]{2,1,0:T(8,128)(2,1)S(1)}, bf16[2,128,2048]{2,1,0:T(8,128)(2,1)S(1)}, u32[]{:S(2)}, u32[]{:S(2)}) %collective-permute-start.11) | collective-permute-done | bytes 1048608 | tf_op jit(solution)/shard_map/ppermute | solution.py:85
  90.7 0.5 collective-permute-start.17
  91.2 2.3 %collective-permute-done.17 = f32[96,256]{1,0:T(8,128)S(1)} collective-permute-done((f32[96,256]{1,0:T(8,128)S(1)}, f32[96,256]{1,0:T(8,128)S(1)}, u32[]{:S(2)}, u32[]{:S(2)}) %collective-permute-start.17) | collective-permute-done | bytes 98336 | tf_op jit(solution)/shard_map/ppermute | solution.py:85
  93.6 1.6 collective-permute-start.15
  95.2 2.5 %collective-permute-done.18 = f32[96,128]{1,0:T(8,128)S(1)} collective-permute-done((f32[96,128]{1,0:T(8,128)S(1)}, f32[96,128]{1,0:T(8,128)S(1)}, u32[]{:S(2)}, u32[]{:S(2)}) %collective-permute-start.18) | collective-permute-done | bytes 49184 | tf_op jit(solution)/shard_map/ppermute | solution.py:85
  97.7 20.2 %matmul.6.refs_9_ = f32[7,3,256,256]{3,2,1,0:T(8,128)S(1)} custom-call(s32[4]{0:T(128)S(1)} %pad_add_fusion.refs_0_.where_ref, bf16[2,128,2048]{2,1,0:T(8,128)(2,1)S(1)} %broadcast_select_fusion.1.refs_1_, bf16[2,128,2048]{2,1,0:T(8,128)(2,1)S(1)} %broadcast_select_fusion.refs_2_, bf16[2,128,2048]{2,1,0:T(8,128)(2,1)S(1)} %collective-permute-done.13.refs_3_, ...), custom_call_target="tpu_custom_call" | custom-call | flops 11274289152 | bytes 44040192 | tf_op jit(solution)/shard_map/matmul/pallas_call | solution.py:188
  117.9 0.9 collective-permute-done.15.refs_2_
  118.9 2.7 %collective-permute-done.20.refs_4_ = bf16[2,128,2048]{2,1,0:T(8,128)(2,1)S(1)} collective-permute-done((bf16[2,128,2048]{2,1,0:T(8,128)(2,1)S(1)}, bf16[2,128,2048]{2,1,0:T(8,128)(2,1)S(1)}, u32[]{:S(2)}, u32[]{:S(2)}) %collective-permute-start.20) | collective-permute-done | bytes 1048608 | tf_op jit(solution)/shard_map/ppermute | solution.py:85
  121.5 21.0 %matmul.7 = (f32[96,256]{1,0:T(8,128)S(1)}, f32[96,256]{1,0:T(8,128)S(1)}) custom-call(s32[4]{0:T(128)S(1)} %pad_add_fusion.refs_0_.where_ref, bf16[2,128,2048]{2,1,0:T(8,128)(2,1)S(1)} %collective-permute-done.12.refs_1_, bf16[2,128,2048]{2,1,0:T(8,128)(2,1)S(1)} %collective-permute-done.15.refs_2_, ...), custom_call_target="tpu_custom_call" | custom-call | flops 11274289152 | bytes 44040192 | tf_op jit(solution)/shard_map/matmul/pallas_call | solution.py:188
  142.5 0.2 collective-permute-start.21
  142.7 1.2 collective-permute-done.21
  143.9 2.9 %collective-permute-start.22 = (f32[96,128]{1,0:T(8,128)S(1)}, f32[96,128]{1,0:T(8,128)S(1)}, u32[]{:S(2)}, u32[]{:S(2)}) collective-permute-start(f32[96,128]{1,0:T(8,128)S(1)} %get-tuple-element.67), channel_id=1, source_target_pairs={{0,2},{1,3},{2,0},{3,1},{4,6},{5,7},{6,4},{7,5},{8,10},{9,11},{10,... | collective-permute-start | bytes 147464 | tf_op jit(solution)/shard_map/ppermute | solution.py:85
  146.8 1.2 collective-permute-start.23
  148.0 2.2 %collective-permute-done.22 = f32[96,128]{1,0:T(8,128)S(1)} collective-permute-done((f32[96,128]{1,0:T(8,128)S(1)}, f32[96,128]{1,0:T(8,128)S(1)}, u32[]{:S(2)}, u32[]{:S(2)}) %collective-permute-start.22) | collective-permute-done | bytes 49184 | tf_op jit(solution)/shard_map/ppermute | solution.py:85
  150.2 2.5 %collective-permute-done.23 = f32[96,128]{1,0:T(8,128)S(1)} collective-permute-done((f32[96,128]{1,0:T(8,128)S(1)}, f32[96,128]{1,0:T(8,128)S(1)}, u32[]{:S(2)}, u32[]{:S(2)}) %collective-permute-start.23) | collective-permute-done | bytes 49184 | tf_op jit(solution)/shard_map/ppermute | solution.py:85
  152.7 1.6 collective-permute-start.24
  154.3 2.6 %collective-permute-done.24 = f32[96,128]{1,0:T(8,128)S(1)} collective-permute-done((f32[96,128]{1,0:T(8,128)S(1)}, f32[96,128]{1,0:T(8,128)S(1)}, u32[]{:S(2)}, u32[]{:S(2)}) %collective-permute-start.24) | collective-permute-done | bytes 49184 | tf_op jit(solution)/shard_map/ppermute | solution.py:85
  157.0 1.2 collective-permute-done.25.other_ref
  158.2 1.0 sketch.1.refs_0_
  159.2 1.8 %collective-permute-start.27 = (f32[3,32,128]{2,1,0:T(8,128)S(1)}, f32[3,32,128]{2,1,0:T(8,128)S(1)}, u32[]{:S(2)}, u32[]{:S(2)}) collective-permute-start(f32[3,32,128]{2,1,0:T(8,128)S(1)} %sketch.1.refs_0_), channel_id=1, source_target_pairs={{0,2},{1,3},{2,0},{3,1},{4,6},{5,7},{6,4},{7,5},{8,10},{9,11},{10,... | collective-permute-start | bytes 147464 | tf_op jit(solution)/shard_map/ppermute | solution.py:85
  161.0 2.6 %collective-permute-start.28 = (f32[3,32,128]{2,1,0:T(8,128)S(1)}, f32[3,32,128]{2,1,0:T(8,128)S(1)}, u32[]{:S(2)}, u32[]{:S(2)}) collective-permute-start(f32[3,32,128]{2,1,0:T(8,128)S(1)} %sketch.1.refs_0_), channel_id=1, source_target_pairs={{0,3},{1,2},{2,1},{3,0},{4,7},{5,6},{6,5},{7,4},{8,11},{9,10},{10,... | collective-permute-start | bytes 147464 | tf_op jit(solution)/shard_map/ppermute | solution.py:85
  163.6 0.3 collective-permute-done.26.refs_1_
  163.9 2.5 %collective-permute-done.27.refs_2_ = f32[3,32,128]{2,1,0:T(8,128)S(1)} collective-permute-done((f32[3,32,128]{2,1,0:T(8,128)S(1)}, f32[3,32,128]{2,1,0:T(8,128)S(1)}, u32[]{:S(2)}, u32[]{:S(2)}) %collective-permute-start.27) | collective-permute-done | bytes 49184 | tf_op jit(solution)/shard_map/ppermute | solution.py:85
  166.4 0.6 collective-permute-done.28.refs_3_
  167.0 6.8 %precond.1 = f32[3,4,256]{2,1,0:T(4,128)} custom-call(s32[1]{0:T(128)} %bitcast.4.row_ref, f32[3,256,4096]{2,1,0:T(8,128)S(1)} %bitcast.15, f32[3,32,128]{2,1,0:T(8,128)S(1)} %sketch.1.refs_0_, f32[3,32,128]{2,1,0:T(8,128)S(1)} %collective-permute-done.26.refs_1_, f32[3,32,128]{2,1,0:T(8,128)S(1)} %collective-permute-done.27.refs_2_, ...), custom_call_target="tpu_custom_call" | custom-call | tf_op jit(solution)/shard_map/precond/pallas_call | solution.py:275
  (41 shorter events, 0.9 us)
Async XLA Ops:
  1.4 26.2 %collective-permute-start = (bf16[2,128,2048]{2,1,0:T(8,128)(2,1)S(1)}, bf16[2,128,2048]{2,1,0:T(8,128)(2,1)S(1)}, u32[]{:S(2)}, u32[]{:S(2)}) collective-permute-start(bf16[2,128,2048]{2,1,0:T(8,128)(2,1)S(1)} %pad_maximum_fusion.refs_1_), channel_id=1, source_target_pairs={{0,1},{1,0},{2,3},{3,2},{4,5},{5,4},{6,7},{7,6},{8,9},{9,8},{10,11... | collective-permute-start | bytes 3145736 | tf_op jit(solution)/shard_map/ppermute | solution.py:85
  4.5 23.2 %collective-permute-start.1 = (bf16[2,128,2048]{2,1,0:T(8,128)(2,1)S(1)}, bf16[2,128,2048]{2,1,0:T(8,128)(2,1)S(1)}, u32[]{:S(2)}, u32[]{:S(2)}) collective-permute-start(bf16[2,128,2048]{2,1,0:T(8,128)(2,1)S(1)} %pad_maximum_fusion.refs_1_), channel_id=1, source_target_pairs={{1,2},{2,1},{5,6},{6,5},{9,10},{10,9},{13,14},{14,13},{17,18},{18,... | collective-permute-start | bytes 3145736 | tf_op jit(solution)/shard_map/ppermute | solution.py:85
  5.2 24.7 %collective-permute-start.2 = (bf16[2,128,2048]{2,1,0:T(8,128)(2,1)S(1)}, bf16[2,128,2048]{2,1,0:T(8,128)(2,1)S(1)}, u32[]{:S(2)}, u32[]{:S(2)}) collective-permute-start(bf16[2,128,2048]{2,1,0:T(8,128)(2,1)S(1)} %pad_maximum_fusion.refs_1_), channel_id=1, source_target_pairs={{0,8},{1,9},{2,10},{3,11},{4,12},{5,13},{6,14},{7,15},{8,0},{9,1},... | collective-permute-start | bytes 3145736 | tf_op jit(solution)/shard_map/ppermute | solution.py:85
  6.8 23.1 %collective-permute-start.3 = (bf16[2,128,2048]{2,1,0:T(8,128)(2,1)S(1)}, bf16[2,128,2048]{2,1,0:T(8,128)(2,1)S(1)}, u32[]{:S(2)}, u32[]{:S(2)}) collective-permute-start(bf16[2,128,2048]{2,1,0:T(8,128)(2,1)S(1)} %pad_maximum_fusion.refs_1_), channel_id=1, source_target_pairs={{0,4},{1,5},{2,6},{3,7},{4,0},{5,1},{6,2},{7,3},{8,12},{9,13},{10,... | collective-permute-start | bytes 3145736 | tf_op jit(solution)/shard_map/ppermute | solution.py:85
  9.7 1.5 collective-permute-start.4
  29.9 35.1 %copy-start = (bf16[1792,192]{0,1:T(8,128)(2,1)S(1)}, bf16[1792,192]{0,1:T(8,128)(2,1)}, u32[]{:S(2)}) copy-start(bf16[1792,192]{0,1:T(8,128)(2,1)} %param.12) | copy-start | bytes 2064388
  29.9 3.9 %collective-permute-start.10 = (bf16[2,128,2048]{2,1,0:T(8,128)(2,1)S(1)}, bf16[2,128,2048]{2,1,0:T(8,128)(2,1)S(1)}, u32[]{:S(2)}, u32[]{:S(2)}) collective-permute-start(bf16[2,128,2048]{2,1,0:T(8,128)(2,1)S(1)} %collective-permute-done.refs_2_), channel_id=1, source_target_pairs={{0,4},{1,5},{2,6},{3,7},{4,0},{5,1},{6,2},{7,3},{8,12},{9,13},{10,... | collective-permute-start | bytes 3145736 | tf_op jit(solution)/shard_map/ppermute | solution.py:85
  29.9 32.4 %collective-permute-start.6 = (bf16[2,128,2048]{2,1,0:T(8,128)(2,1)S(1)}, bf16[2,128,2048]{2,1,0:T(8,128)(2,1)S(1)}, u32[]{:S(2)}, u32[]{:S(2)}) collective-permute-start(bf16[2,128,2048]{2,1,0:T(8,128)(2,1)S(1)} %collective-permute-done.refs_2_), channel_id=1, source_target_pairs={{1,2},{2,1},{5,6},{6,5},{9,10},{10,9},{13,14},{14,13},{17,18},{18,... | collective-permute-start | bytes 3145736 | tf_op jit(solution)/shard_map/ppermute | solution.py:85
  30.8 31.5 %collective-permute-start.7 = (bf16[2,128,2048]{2,1,0:T(8,128)(2,1)S(1)}, bf16[2,128,2048]{2,1,0:T(8,128)(2,1)S(1)}, u32[]{:S(2)}, u32[]{:S(2)}) collective-permute-start(bf16[2,128,2048]{2,1,0:T(8,128)(2,1)S(1)} %collective-permute-done.refs_2_), channel_id=1, source_target_pairs={{0,8},{1,9},{2,10},{3,11},{4,12},{5,13},{6,14},{7,15},{8,0},{9,1},... | collective-permute-start | bytes 3145736 | tf_op jit(solution)/shard_map/ppermute | solution.py:85
  32.4 29.9 %collective-permute-start.5 = (bf16[2,128,2048]{2,1,0:T(8,128)(2,1)S(1)}, bf16[2,128,2048]{2,1,0:T(8,128)(2,1)S(1)}, u32[]{:S(2)}, u32[]{:S(2)}) collective-permute-start(bf16[2,128,2048]{2,1,0:T(8,128)(2,1)S(1)} %collective-permute-done.1), channel_id=1, source_target_pairs={{1,0},{2,3},{5,4},{6,7},{9,8},{10,11},{13,12},{14,15},{17,16},{18,... | collective-permute-start | bytes 3145736 | tf_op jit(solution)/shard_map/ppermute | solution.py:85
  33.6 28.6 %collective-permute-start.8 = (bf16[2,128,2048]{2,1,0:T(8,128)(2,1)S(1)}, bf16[2,128,2048]{2,1,0:T(8,128)(2,1)S(1)}, u32[]{:S(2)}, u32[]{:S(2)}) collective-permute-start(bf16[2,128,2048]{2,1,0:T(8,128)(2,1)S(1)} %collective-permute-done.2.refs_1_), channel_id=1, source_target_pairs={{0,4},{1,5},{2,6},{3,7},{4,0},{5,1},{6,2},{7,3},{8,12},{9,13},{10,... | collective-permute-start | bytes 3145736 | tf_op jit(solution)/shard_map/ppermute | solution.py:85
  33.8 24.6 %collective-permute-start.9 = (f32[192,128]{1,0:T(8,128)S(1)}, f32[192,128]{1,0:T(8,128)S(1)}, u32[]{:S(2)}, u32[]{:S(2)}) collective-permute-start(f32[192,128]{1,0:T(8,128)S(1)} %fusion.2), channel_id=1, source_target_pairs={{0,8},{1,9},{2,10},{3,11},{4,12},{5,13},{6,14},{7,15},{8,0},{9,1},... | collective-permute-start | bytes 294920 | tf_op jit(solution)/shard_map/ppermute | solution.py:85
  62.3 2.7 %collective-permute-start.14 = (bf16[2,128,2048]{2,1,0:T(8,128)(2,1)S(1)}, bf16[2,128,2048]{2,1,0:T(8,128)(2,1)S(1)}, u32[]{:S(2)}, u32[]{:S(2)}) collective-permute-start(bf16[2,128,2048]{2,1,0:T(8,128)(2,1)S(1)} %collective-permute-done.7.refs_2_), channel_id=1, source_target_pairs={{0,4},{1,5},{2,6},{3,7},{4,0},{5,1},{6,2},{7,3},{8,12},{9,13},{10,... | collective-permute-start | bytes 3145736 | tf_op jit(solution)/shard_map/ppermute | solution.py:85
  62.5 25.6 %collective-permute-start.12 = (bf16[2,128,2048]{2,1,0:T(8,128)(2,1)S(1)}, bf16[2,128,2048]{2,1,0:T(8,128)(2,1)S(1)}, u32[]{:S(2)}, u32[]{:S(2)}) collective-permute-start(bf16[2,128,2048]{2,1,0:T(8,128)(2,1)S(1)} %broadcast_select_fusion.1.refs_1_), channel_id=1, source_target_pairs={{0,8},{1,9},{2,10},{3,11},{4,12},{5,13},{6,14},{7,15},{8,0},{9,1},... | collective-permute-start | bytes 3145736 | tf_op jit(solution)/shard_map/ppermute | solution.py:85
  63.0 25.1 %collective-permute-start.13 = (bf16[2,128,2048]{2,1,0:T(8,128)(2,1)S(1)}, bf16[2,128,2048]{2,1,0:T(8,128)(2,1)S(1)}, u32[]{:S(2)}, u32[]{:S(2)}) collective-permute-start(bf16[2,128,2048]{2,1,0:T(8,128)(2,1)S(1)} %broadcast_select_fusion.1.refs_1_), channel_id=1, source_target_pairs={{0,4},{1,5},{2,6},{3,7},{4,0},{5,1},{6,2},{7,3},{8,12},{9,13},{10,... | collective-permute-start | bytes 3145736 | tf_op jit(solution)/shard_map/ppermute | solution.py:85
  63.3 27.3 %collective-permute-start.11 = (bf16[2,128,2048]{2,1,0:T(8,128)(2,1)S(1)}, bf16[2,128,2048]{2,1,0:T(8,128)(2,1)S(1)}, u32[]{:S(2)}, u32[]{:S(2)}) collective-permute-start(bf16[2,128,2048]{2,1,0:T(8,128)(2,1)S(1)} %collective-permute-done.6), channel_id=1, source_target_pairs={{1,0},{2,3},{5,4},{6,7},{9,8},{10,11},{13,12},{14,15},{17,16},{18,... | collective-permute-start | bytes 3145736 | tf_op jit(solution)/shard_map/ppermute | solution.py:85
  90.6 7.1 %collective-permute-start.19 = (bf16[2,128,2048]{2,1,0:T(8,128)(2,1)S(1)}, bf16[2,128,2048]{2,1,0:T(8,128)(2,1)S(1)}, u32[]{:S(2)}, u32[]{:S(2)}) collective-permute-start(bf16[2,128,2048]{2,1,0:T(8,128)(2,1)S(1)} %broadcast_select_fusion.refs_2_), channel_id=1, source_target_pairs={{0,4},{1,5},{2,6},{3,7},{4,0},{5,1},{6,2},{7,3},{8,12},{9,13},{10,... | collective-permute-start | bytes 3145736 | tf_op jit(solution)/shard_map/ppermute | solution.py:85
  90.7 2.8 %collective-permute-start.17 = (f32[96,256]{1,0:T(8,128)S(1)}, f32[96,256]{1,0:T(8,128)S(1)}, u32[]{:S(2)}, u32[]{:S(2)}) collective-permute-start(f32[96,256]{1,0:T(8,128)S(1)} %get-tuple-element.59), channel_id=1, source_target_pairs={{0,4},{1,5},{2,6},{3,7},{4,0},{5,1},{6,2},{7,3},{8,12},{9,13},{10,... | collective-permute-start | bytes 294920 | tf_op jit(solution)/shard_map/ppermute | solution.py:85
  93.5 4.2 %collective-permute-start.18 = (f32[96,128]{1,0:T(8,128)S(1)}, f32[96,128]{1,0:T(8,128)S(1)}, u32[]{:S(2)}, u32[]{:S(2)}) collective-permute-start(f32[96,128]{1,0:T(8,128)S(1)} %slice.25), channel_id=1, source_target_pairs={{0,1},{1,0},{2,3},{3,2},{4,5},{5,4},{6,7},{7,6},{8,9},{9,8},{10,11... | collective-permute-start | bytes 147464 | tf_op jit(solution)/shard_map/ppermute | solution.py:85
  93.6 25.3 %collective-permute-start.15 = (bf16[2,128,2048]{2,1,0:T(8,128)(2,1)S(1)}, bf16[2,128,2048]{2,1,0:T(8,128)(2,1)S(1)}, u32[]{:S(2)}, u32[]{:S(2)}) collective-permute-start(bf16[2,128,2048]{2,1,0:T(8,128)(2,1)S(1)} %broadcast_select_fusion.refs_2_), channel_id=1, source_target_pairs={{0,8},{1,9},{2,10},{3,11},{4,12},{5,13},{6,14},{7,15},{8,0},{9,1},... | collective-permute-start | bytes 3145736 | tf_op jit(solution)/shard_map/ppermute | solution.py:85
  95.2 23.7 %collective-permute-start.16 = (bf16[2,128,2048]{2,1,0:T(8,128)(2,1)S(1)}, bf16[2,128,2048]{2,1,0:T(8,128)(2,1)S(1)}, u32[]{:S(2)}, u32[]{:S(2)}) collective-permute-start(bf16[2,128,2048]{2,1,0:T(8,128)(2,1)S(1)} %collective-permute-done.12.refs_1_), channel_id=1, source_target_pairs={{0,4},{1,5},{2,6},{3,7},{4,0},{5,1},{6,2},{7,3},{8,12},{9,13},{10,... | collective-permute-start | bytes 3145736 | tf_op jit(solution)/shard_map/ppermute | solution.py:85
  97.7 69.3 %slice-start = ((s8[12582912]{0:T(1024)(128)(4,1)}), s8[4194304]{0:T(1024)(128)(4,1)S(1)}, s32[]{:S(2)}) async-start(s8[12582912]{0:T(1024)(128)(4,1)} %bitcast.14), calls=%async_computation | async-start | bytes 8388608
  97.7 69.3 %slice-start.1 = ((s8[12582912]{0:T(1024)(128)(4,1)}), s8[4194304]{0:T(1024)(128)(4,1)S(1)}, s32[]{:S(2)}) async-start(s8[12582912]{0:T(1024)(128)(4,1)} %bitcast.14), calls=%async_computation.1 | async-start | bytes 8388608
  117.9 49.1 %slice-start.2 = ((s8[12582912]{0:T(1024)(128)(4,1)}), s8[4194304]{0:T(1024)(128)(4,1)S(1)}, s32[]{:S(2)}) async-start(s8[12582912]{0:T(1024)(128)(4,1)} %bitcast.14), calls=%async_computation.2 | async-start | bytes 8388608
  118.9 2.7 %collective-permute-start.20 = (bf16[2,128,2048]{2,1,0:T(8,128)(2,1)S(1)}, bf16[2,128,2048]{2,1,0:T(8,128)(2,1)S(1)}, u32[]{:S(2)}, u32[]{:S(2)}) collective-permute-start(bf16[2,128,2048]{2,1,0:T(8,128)(2,1)S(1)} %collective-permute-done.15.refs_2_), channel_id=1, source_target_pairs={{0,4},{1,5},{2,6},{3,7},{4,0},{5,1},{6,2},{7,3},{8,12},{9,13},{10,... | collective-permute-start | bytes 3145736 | tf_op jit(solution)/shard_map/ppermute | solution.py:85
  142.5 1.4 collective-permute-start.21
  143.9 6.3 %collective-permute-start.22 = (f32[96,128]{1,0:T(8,128)S(1)}, f32[96,128]{1,0:T(8,128)S(1)}, u32[]{:S(2)}, u32[]{:S(2)}) collective-permute-start(f32[96,128]{1,0:T(8,128)S(1)} %get-tuple-element.67), channel_id=1, source_target_pairs={{0,2},{1,3},{2,0},{3,1},{4,6},{5,7},{6,4},{7,5},{8,10},{9,11},{10,... | collective-permute-start | bytes 147464 | tf_op jit(solution)/shard_map/ppermute | solution.py:85
  146.8 5.9 %collective-permute-start.23 = (f32[96,128]{1,0:T(8,128)S(1)}, f32[96,128]{1,0:T(8,128)S(1)}, u32[]{:S(2)}, u32[]{:S(2)}) collective-permute-start(f32[96,128]{1,0:T(8,128)S(1)} %get-tuple-element.68), channel_id=1, source_target_pairs={{0,3},{1,2},{2,1},{3,0},{4,7},{5,6},{6,5},{7,4},{8,11},{9,10},{10,... | collective-permute-start | bytes 147464 | tf_op jit(solution)/shard_map/ppermute | solution.py:85
  152.7 4.2 %collective-permute-start.24 = (f32[96,128]{1,0:T(8,128)S(1)}, f32[96,128]{1,0:T(8,128)S(1)}, u32[]{:S(2)}, u32[]{:S(2)}) collective-permute-start(f32[96,128]{1,0:T(8,128)S(1)} %add_add_fusion), channel_id=1, source_target_pairs={{0,8},{1,9},{2,10},{3,11},{4,12},{5,13},{6,14},{7,15},{8,0},{9,1},... | collective-permute-start | bytes 147464 | tf_op jit(solution)/shard_map/ppermute | solution.py:85
  156.9 1.3 collective-permute-start.25
  159.2 4.7 %collective-permute-start.26 = (f32[3,32,128]{2,1,0:T(8,128)S(1)}, f32[3,32,128]{2,1,0:T(8,128)S(1)}, u32[]{:S(2)}, u32[]{:S(2)}) collective-permute-start(f32[3,32,128]{2,1,0:T(8,128)S(1)} %sketch.1.refs_0_), channel_id=1, source_target_pairs={{0,1},{1,0},{2,3},{3,2},{4,5},{5,4},{6,7},{7,6},{8,9},{9,8},{10,11... | collective-permute-start | bytes 147464 | tf_op jit(solution)/shard_map/ppermute | solution.py:85
  159.2 7.2 %collective-permute-start.27 = (f32[3,32,128]{2,1,0:T(8,128)S(1)}, f32[3,32,128]{2,1,0:T(8,128)S(1)}, u32[]{:S(2)}, u32[]{:S(2)}) collective-permute-start(f32[3,32,128]{2,1,0:T(8,128)S(1)} %sketch.1.refs_0_), channel_id=1, source_target_pairs={{0,2},{1,3},{2,0},{3,1},{4,6},{5,7},{6,4},{7,5},{8,10},{9,11},{10,... | collective-permute-start | bytes 147464 | tf_op jit(solution)/shard_map/ppermute | solution.py:85
  161.0 5.9 %collective-permute-start.28 = (f32[3,32,128]{2,1,0:T(8,128)S(1)}, f32[3,32,128]{2,1,0:T(8,128)S(1)}, u32[]{:S(2)}, u32[]{:S(2)}) collective-permute-start(f32[3,32,128]{2,1,0:T(8,128)S(1)} %sketch.1.refs_0_), channel_id=1, source_target_pairs={{0,3},{1,2},{2,1},{3,0},{4,7},{5,6},{6,5},{7,4},{8,11},{9,10},{10,... | collective-permute-start | bytes 147464 | tf_op jit(solution)/shard_map/ppermute | solution.py:85

commit v4 on v3

--- a/solution.py
+++ b/solution.py
@@ -244,47 +244,38 @@
     height = p_ref.shape[1]
     lanes = 2 * K
     group = 32
-    ones = jnp.ones((8, lanes), jnp.float32)
-
-    @pl.loop(0, height // group)
-    def _(g):
-        at = pl.ds(pl.multiple_of(g * group, group), group)
-        totals = [jnp.zeros((group, lanes), jnp.float32) for _ in range(ROWS)]
-        for q in range(K // 2):
-            part = p_ref[0, at, pl.ds(q * lanes, lanes)]
+
+    for w in range(3):
+
+        @pl.loop(0, height // group)
+        def _(g):
+            at = pl.ds(pl.multiple_of(g * group, group), group)
+            totals = [jnp.zeros((group, lanes), jnp.float32) for _ in range(ROWS)]
+            for q in range(K // 2):
+                part = p_ref[w, at, pl.ds(q * lanes, lanes)]
+                for n in range(ROWS):
+                    totals[n] = totals[n] + part * sketches[n][w, pl.ds(q, 1), :]
             for n in range(ROWS):
-                totals[n] = totals[n] + part * sketches[n][0, pl.ds(q, 1), :]
+                sums[n, at, :] = totals[n]
+
         for n in range(ROWS):
-            sums[n, at, :] = totals[n]
-
-    for n in range(ROWS):
-        seq = row_ref[0] ^ n
-        line = lax.dot_general(
-            ones,
-            sums[n],
-            NT,
-            precision=lax.Precision.HIGHEST,
-            preferred_element_type=jnp.float32,
-        )
-        out_ref[0, pl.ds(seq, 1), :] = line[:1]
+            line = jnp.sum(sums[n].T, axis=0, keepdims=True)
+            out_ref[w, pl.ds(row_ref[0] ^ n, 1), :] = line
 
 
 def apply_precond(row, precond, sketches):
-    height, order = precond.shape[1:]
-    piece = pl.BlockSpec((1, K // 2, 2 * K), lambda w, r: (w, 0, 0))
+    height = precond.shape[1]
+    whole = pl.BlockSpec(memory_space=pltpu.VMEM)
+    operands = [pltpu.with_memory_space_constraint(a, pltpu.VMEM) for a in [precond, *sketches]]
     return pl.pallas_call(
         precond_kernel,
         out_shape=jax.ShapeDtypeStruct((3, ROWS, height), jnp.float32),
-        grid_spec=pltpu.PrefetchScalarGridSpec(
-            num_scalar_prefetch=1,
-            grid=(3,),
-            in_specs=[pl.BlockSpec((1, height, order), lambda w, r: (w, 0, 0))] + [piece] * ROWS,
-            out_specs=pl.BlockSpec((1, ROWS, height), lambda w, r: (w, 0, 0)),
-            scratch_shapes=[pltpu.VMEM((ROWS, height, 2 * K), jnp.float32)],
-        ),
-        compiler_params=pltpu.CompilerParams(vmem_limit_bytes=12 * MIB),
+        in_specs=[pl.BlockSpec(memory_space=pltpu.SMEM)] + [whole] * (1 + ROWS),
+        out_specs=whole,
+        scratch_shapes=[pltpu.VMEM((ROWS, height, 2 * K), jnp.float32)],
+        compiler_params=pltpu.CompilerParams(vmem_limit_bytes=4 * MIB),
         name="precond",
-    )(row, precond, *sketches)
+    )(row, *operands)
 
 
 A, C, Y, D = range(4)
@@ -337,10 +328,8 @@
     middle_2 = send(near, INNER)
     near_y = other_chip(near)
     own_d = other_core(own_y)
-    feat_y = other_chip(feat_t)
     (acc,) = step([(A, (own, near)), (C, (own_c, near_c))], w_gate_up, w_down)
-    passed, middle_2, near_y, own_d, feat_y, acc = tie(passed, middle_2, near_y, own_d, feat_y, acc)
-    feat_t = feat_t + feat_y
+    passed, middle_2, near_y, own_d, acc = tie(passed, middle_2, near_y, own_d, acc)
 
     near_d = other_core(near_y)
     third = jnp.where(inner, middle, passed)
@@ -350,26 +339,30 @@
     mine_0, theirs_0 = step(
         [(Y, (own_y, near_y)), (D, (own_d, near_d))], w_gate_up, w_down, acc, unit_proj_t
     )
-    passed_2, third_y, third_c, mine_0, theirs_0, feat_t = tie(
-        passed_2, third_y, third_c, mine_0, theirs_0, feat_t
-    )
+    passed_2, third_y, third_c, mine_0, theirs_0 = tie(passed_2, third_y, third_c, mine_0, theirs_0)
 
     fourth = jnp.where(inner, middle_2, passed_2)
     fourth_c = other_core(fourth)
     fourth_y = other_chip(fourth)
     third_d = other_core(third_y)
-    mine_0 = mine_0 + other_core(theirs_0)
-    part = mine_0[:, :SEQ] + send(mine_0[:, SEQ:], swap_rows(1))
+    theirs_0 = other_core(theirs_0)
     (acc,) = step([(A, (third, fourth)), (C, (third_c, fourth_c))], w_gate_up, w_down)
-    fourth_y, third_d, part, acc = tie(fourth_y, third_d, part, acc)
+    fourth_y, third_d, mine_0, theirs_0, feat_t, acc = tie(fourth_y, third_d, mine_0, theirs_0, feat_t, acc)
 
     fourth_d = other_core(fourth_y)
+    feat_y = other_chip(feat_t)
+    mine_0 = mine_0 + theirs_0
+    near_part = send(mine_0[:, SEQ:], swap_rows(1))
     mine_1, theirs_1 = step(
         [(Y, (third_y, fourth_y)), (D, (third_d, fourth_d))], w_gate_up, w_down, acc, unit_proj_t
     )
 
+    near_part, feat_y, mine_1, theirs_1 = tie(near_part, feat_y, mine_1, theirs_1)
+
     mine_1 = mine_1 + other_core(theirs_1)
     low, high = mine_1[:, :SEQ], mine_1[:, SEQ:]
+    part = mine_0[:, :SEQ] + near_part
+    feat_t = feat_t + feat_y
     part = part + send(jnp.where(inner, high, low), swap_rows(2)) + send(jnp.where(inner, low, high), swap_rows(3))
     part = part + other_chip(part)
     other = other_core(part)

time: 174 us -> 171 us (0.983)
  waiting for transfers between devices: 54.3 us -> 51.9 us
    ppermute x29, waiting for transfers between devices: 54.3 us -> 51.9 us  [send(): return lax.ppermute(value, BOTH, pairs)]
  transfers between devices with their start and end apart: 29 -> 29, of which waited for: 20 -> 17; matrix products, arithmetic and copies ran while one was open for 2% -> 2% of each run, Pallas kernels for 35% -> 48%
where the time goes in v4:
time: 171 us; the launch traced here: 170 us
  Pallas kernels  88.3 us (52%)
  waiting for transfers between devices  51.9 us (30%)
  starting transfers between devices  24.7 us (14%)
  matrix products  2.9 us (2%)
  other arithmetic  2.32 us (1%)
    pallas_call x4, Pallas kernels, matmul_step(): pl.pallas_call(functools.partial(matmul_kernel, count, last), out_shape=o...  81.6 us
    ppermute x29, waiting for transfers between devices, send(): return lax.ppermute(value, BOTH, pairs)  51.9 us
    ppermute x29, starting transfers between devices, send(): return lax.ppermute(value, BOTH, pairs)  24.7 us
    pallas_call x1, Pallas kernels, apply_precond(): pl.pallas_call(precond_kernel, out_shape=jax.ShapeDtypeStruct((3, ROWS, h...  5.71 us
  transfers between devices with their start and end apart: 29, of which 17 were waited for; matrix products, arithmetic and copies ran while one was open for 2% of the time, Pallas kernels for 48%

profile of v4, /device:TPU:0, one launch (start us, length us, event | category | flops | bytes accessed | tf_op | source)
XLA Modules:
  0.0 170.4 jit_solution(17691553909513966058)
XLA Ops:
  0.1 1.3 pad_maximum_fusion.refs_1_
  1.4 3.1 %collective-permute-start = (bf16[2,128,2048]{2,1,0:T(8,128)(2,1)S(1)}, bf16[2,128,2048]{2,1,0:T(8,128)(2,1)S(1)}, u32[]{:S(2)}, u32[]{:S(2)}) collective-permute-start(bf16[2,128,2048]{2,1,0:T(8,128)(2,1)S(1)} %pad_maximum_fusion.refs_1_), channel_id=1, source_target_pairs={{0,1},{1,0},{2,3},{3,2},{4,5},{5,4},{6,7},{7,6},{8,9},{9,8},{10,11... | collective-permute-start | bytes 3145736 | tf_op jit(solution)/shard_map/ppermute | solution.py:85
  4.5 0.7 collective-permute-start.1
  5.2 1.6 collective-permute-start.2
  6.8 1.4 convolution_bitcast_fusion.1
  8.2 1.5 convolution_bitcast_fusion
  9.7 0.6 collective-permute-start.4
  10.3 0.9 collective-permute-done.4
  11.2 0.6 fusion.4
  11.9 15.7 %collective-permute-done.refs_2_ = bf16[2,128,2048]{2,1,0:T(8,128)(2,1)S(1)} collective-permute-done((bf16[2,128,2048]{2,1,0:T(8,128)(2,1)S(1)}, bf16[2,128,2048]{2,1,0:T(8,128)(2,1)S(1)}, u32[]{:S(2)}, u32[]{:S(2)}) %collective-permute-start) | collective-permute-done | bytes 1048608 | tf_op jit(solution)/shard_map/ppermute | solution.py:85
  27.6 2.2 %collective-permute-done.2.refs_1_ = bf16[2,128,2048]{2,1,0:T(8,128)(2,1)S(1)} collective-permute-done((bf16[2,128,2048]{2,1,0:T(8,128)(2,1)S(1)}, bf16[2,128,2048]{2,1,0:T(8,128)(2,1)S(1)}, u32[]{:S(2)}, u32[]{:S(2)}) %collective-permute-start.2) | collective-permute-done | bytes 1048608 | tf_op jit(solution)/shard_map/ppermute | solution.py:85
  29.9 0.9 collective-permute-start.6
  30.8 1.6 collective-permute-start.7
  32.4 1.3 collective-permute-start.5
  33.8 19.6 %matmul.4.refs_9_ = f32[7,3,256,256]{3,2,1,0:T(8,128)S(1)} custom-call(s32[4]{0:T(128)S(1)} %pad_add_fusion.refs_0_.where_ref, bf16[2,128,2048]{2,1,0:T(8,128)(2,1)S(1)} %pad_maximum_fusion.refs_1_, bf16[2,128,2048]{2,1,0:T(8,128)(2,1)S(1)} %collective-permute-done.refs_2_, bf16[2,128,2048]{2,1,0:T(8,128)(2,1)S(1)} %collective-permute-done.3.refs_3_, ...), custom_call_target="tpu_custom_call" | custom-call | flops 11274289152 | bytes 44040192 | tf_op jit(solution)/shard_map/matmul/pallas_call | solution.py:188
  53.4 8.9 %collective-permute-done.5 = bf16[2,128,2048]{2,1,0:T(8,128)(2,1)S(1)} collective-permute-done((bf16[2,128,2048]{2,1,0:T(8,128)(2,1)S(1)}, bf16[2,128,2048]{2,1,0:T(8,128)(2,1)S(1)}, u32[]{:S(2)}, u32[]{:S(2)}) %collective-permute-start.5) | collective-permute-done | bytes 1048608 | tf_op jit(solution)/shard_map/ppermute | solution.py:85
  62.5 0.6 collective-permute-start.11
  63.0 0.2 collective-permute-start.12
  63.2 1.3 collective-permute-start.10
  64.5 0.5 collective-permute-done.13.refs_4_
  65.0 21.0 %matmul.5 = (f32[96,256]{1,0:T(8,128)S(1)}, f32[96,256]{1,0:T(8,128)S(1)}) custom-call(s32[4]{0:T(128)S(1)} %pad_add_fusion.refs_0_.where_ref, bf16[2,128,2048]{2,1,0:T(8,128)(2,1)S(1)} %collective-permute-done.2.refs_1_, bf16[2,128,2048]{2,1,0:T(8,128)(2,1)S(1)} %collective-permute-done.7.refs_2_, bf16[2,128,2048]{2,1,0:T(8,128)(2,1)S(1)} %collective-permute-done.8.refs_3_, ...), custom_call_target="tpu_custom_call" | custom-call | flops 11274289152 | bytes 44040192 | tf_op jit(solution)/shard_map/matmul/pallas_call | solution.py:188
  86.0 2.1 %collective-permute-done.11.refs_1_ = bf16[2,128,2048]{2,1,0:T(8,128)(2,1)S(1)} collective-permute-done((bf16[2,128,2048]{2,1,0:T(8,128)(2,1)S(1)}, bf16[2,128,2048]{2,1,0:T(8,128)(2,1)S(1)}, u32[]{:S(2)}, u32[]{:S(2)}) %collective-permute-start.11) | collective-permute-done | bytes 1048608 | tf_op jit(solution)/shard_map/ppermute | solution.py:85
  88.1 2.4 %collective-permute-done.10 = bf16[2,128,2048]{2,1,0:T(8,128)(2,1)S(1)} collective-permute-done((bf16[2,128,2048]{2,1,0:T(8,128)(2,1)S(1)}, bf16[2,128,2048]{2,1,0:T(8,128)(2,1)S(1)}, u32[]{:S(2)}, u32[]{:S(2)}) %collective-permute-start.10) | collective-permute-done | bytes 1048608 | tf_op jit(solution)/shard_map/ppermute | solution.py:85
  90.7 1.6 collective-permute-start.14
  92.3 0.2 collective-permute-start.15
  92.4 0.3 collective-permute-start.16
  92.8 0.6 collective-permute-done.17.refs_4_
  93.3 19.6 %matmul.6.refs_9_ = f32[7,3,256,256]{3,2,1,0:T(8,128)S(1)} custom-call(s32[4]{0:T(128)S(1)} %pad_add_fusion.refs_0_.where_ref, bf16[2,128,2048]{2,1,0:T(8,128)(2,1)S(1)} %broadcast_select_fusion.1.refs_1_, bf16[2,128,2048]{2,1,0:T(8,128)(2,1)S(1)} %broadcast_select_fusion.refs_2_, bf16[2,128,2048]{2,1,0:T(8,128)(2,1)S(1)} %collective-permute-done.12.refs_3_, ...), custom_call_target="tpu_custom_call" | custom-call | flops 11274289152 | bytes 44040192 | tf_op jit(solution)/shard_map/matmul/pallas_call | solution.py:188
  112.9 3.3 %collective-permute-done.14.refs_2_ = bf16[2,128,2048]{2,1,0:T(8,128)(2,1)S(1)} collective-permute-done((bf16[2,128,2048]{2,1,0:T(8,128)(2,1)S(1)}, bf16[2,128,2048]{2,1,0:T(8,128)(2,1)S(1)}, u32[]{:S(2)}, u32[]{:S(2)}) %collective-permute-start.14) | collective-permute-done | bytes 1048608 | tf_op jit(solution)/shard_map/ppermute | solution.py:85
  116.4 1.6 collective-permute-start.19
  118.0 0.9 collective-permute-done.20.refs_4_
  118.9 21.4 %matmul.7 = (f32[96,256]{1,0:T(8,128)S(1)}, f32[96,256]{1,0:T(8,128)S(1)}) custom-call(s32[4]{0:T(128)S(1)} %pad_add_fusion.refs_0_.where_ref, bf16[2,128,2048]{2,1,0:T(8,128)(2,1)S(1)} %collective-permute-done.11.refs_1_, bf16[2,128,2048]{2,1,0:T(8,128)(2,1)S(1)} %collective-permute-done.14.refs_2_, ...), custom_call_target="tpu_custom_call" | custom-call | flops 11274289152 | bytes 44040192 | tf_op jit(solution)/shard_map/matmul/pallas_call | solution.py:188
  140.4 0.5 collective-permute-start.21
  140.9 0.9 collective-permute-done.21
  141.9 1.7 %collective-permute-start.22 = (f32[96,128]{1,0:T(8,128)S(1)}, f32[96,128]{1,0:T(8,128)S(1)}, u32[]{:S(2)}, u32[]{:S(2)}) collective-permute-start(f32[96,128]{1,0:T(8,128)S(1)} %get-tuple-element.75), channel_id=1, source_target_pairs={{0,2},{1,3},{2,0},{3,1},{4,6},{5,7},{6,4},{7,5},{8,10},{9,11},{10,... | collective-permute-start | bytes 147464 | tf_op jit(solution)/shard_map/ppermute | solution.py:85
  143.6 1.2 collective-permute-start.23
  144.8 3.2 %collective-permute-done.22 = f32[96,128]{1,0:T(8,128)S(1)} collective-permute-done((f32[96,128]{1,0:T(8,128)S(1)}, f32[96,128]{1,0:T(8,128)S(1)}, u32[]{:S(2)}, u32[]{:S(2)}) %collective-permute-start.22) | collective-permute-done | bytes 49184 | tf_op jit(solution)/shard_map/ppermute | solution.py:85
  148.0 1.6 collective-permute-done.23
  149.6 1.0 collective-permute-start.24
  150.6 3.2 %collective-permute-done.24 = f32[96,128]{1,0:T(8,128)S(1)} collective-permute-done((f32[96,128]{1,0:T(8,128)S(1)}, f32[96,128]{1,0:T(8,128)S(1)}, u32[]{:S(2)}, u32[]{:S(2)}) %collective-permute-start.24) | collective-permute-done | bytes 49184 | tf_op jit(solution)/shard_map/ppermute | solution.py:85
  153.9 1.2 collective-permute-done.25.other_ref
  155.1 1.0 sketch.1.refs_0_
  156.1 1.0 collective-permute-start.26
  157.1 1.6 collective-permute-start.27
  158.7 1.8 %collective-permute-start.28 = (f32[3,32,128]{2,1,0:T(8,128)S(1)}, f32[3,32,128]{2,1,0:T(8,128)S(1)}, u32[]{:S(2)}, u32[]{:S(2)}) collective-permute-start(f32[3,32,128]{2,1,0:T(8,128)S(1)} %sketch.1.refs_0_), channel_id=1, source_target_pairs={{0,3},{1,2},{2,1},{3,0},{4,7},{5,6},{6,5},{7,4},{8,11},{9,10},{10,... | collective-permute-start | bytes 147464 | tf_op jit(solution)/shard_map/ppermute | solution.py:85
  160.5 3.3 %collective-permute-done.27.refs_2_ = f32[3,32,128]{2,1,0:T(8,128)S(1)} collective-permute-done((f32[3,32,128]{2,1,0:T(8,128)S(1)}, f32[3,32,128]{2,1,0:T(8,128)S(1)}, u32[]{:S(2)}, u32[]{:S(2)}) %collective-permute-start.27) | collective-permute-done | bytes 49184 | tf_op jit(solution)/shard_map/ppermute | solution.py:85
  163.8 0.8 collective-permute-done.28.refs_3_
  164.7 5.7 %precond.1 = f32[3,4,256]{2,1,0:T(4,128)} custom-call(s32[1]{0:T(128)} %bitcast.4.row_ref, f32[3,256,4096]{2,1,0:T(8,128)S(1)} %bitcast.15, f32[3,32,128]{2,1,0:T(8,128)S(1)} %sketch.1.refs_0_, f32[3,32,128]{2,1,0:T(8,128)S(1)} %collective-permute-done.26.refs_1_, f32[3,32,128]{2,1,0:T(8,128)S(1)} %collective-permute-done.27.refs_2_, ...), custom_call_target="tpu_custom_call" | custom-call | tf_op jit(solution)/shard_map/precond/pallas_call | solution.py:270
  (42 shorter events, 0.9 us)
Async XLA Ops:
  1.4 26.2 %collective-permute-start = (bf16[2,128,2048]{2,1,0:T(8,128)(2,1)S(1)}, bf16[2,128,2048]{2,1,0:T(8,128)(2,1)S(1)}, u32[]{:S(2)}, u32[]{:S(2)}) collective-permute-start(bf16[2,128,2048]{2,1,0:T(8,128)(2,1)S(1)} %pad_maximum_fusion.refs_1_), channel_id=1, source_target_pairs={{0,1},{1,0},{2,3},{3,2},{4,5},{5,4},{6,7},{7,6},{8,9},{9,8},{10,11... | collective-permute-start | bytes 3145736 | tf_op jit(solution)/shard_map/ppermute | solution.py:85
  4.5 23.2 %collective-permute-start.1 = (bf16[2,128,2048]{2,1,0:T(8,128)(2,1)S(1)}, bf16[2,128,2048]{2,1,0:T(8,128)(2,1)S(1)}, u32[]{:S(2)}, u32[]{:S(2)}) collective-permute-start(bf16[2,128,2048]{2,1,0:T(8,128)(2,1)S(1)} %pad_maximum_fusion.refs_1_), channel_id=1, source_target_pairs={{1,2},{2,1},{5,6},{6,5},{9,10},{10,9},{13,14},{14,13},{17,18},{18,... | collective-permute-start | bytes 3145736 | tf_op jit(solution)/shard_map/ppermute | solution.py:85
  5.2 24.7 %collective-permute-start.2 = (bf16[2,128,2048]{2,1,0:T(8,128)(2,1)S(1)}, bf16[2,128,2048]{2,1,0:T(8,128)(2,1)S(1)}, u32[]{:S(2)}, u32[]{:S(2)}) collective-permute-start(bf16[2,128,2048]{2,1,0:T(8,128)(2,1)S(1)} %pad_maximum_fusion.refs_1_), channel_id=1, source_target_pairs={{0,8},{1,9},{2,10},{3,11},{4,12},{5,13},{6,14},{7,15},{8,0},{9,1},... | collective-permute-start | bytes 3145736 | tf_op jit(solution)/shard_map/ppermute | solution.py:85
  6.8 23.1 %collective-permute-start.3 = (bf16[2,128,2048]{2,1,0:T(8,128)(2,1)S(1)}, bf16[2,128,2048]{2,1,0:T(8,128)(2,1)S(1)}, u32[]{:S(2)}, u32[]{:S(2)}) collective-permute-start(bf16[2,128,2048]{2,1,0:T(8,128)(2,1)S(1)} %pad_maximum_fusion.refs_1_), channel_id=1, source_target_pairs={{0,4},{1,5},{2,6},{3,7},{4,0},{5,1},{6,2},{7,3},{8,12},{9,13},{10,... | collective-permute-start | bytes 3145736 | tf_op jit(solution)/shard_map/ppermute | solution.py:85
  9.7 1.5 collective-permute-start.4
  29.9 35.1 %copy-start = (bf16[1792,192]{0,1:T(8,128)(2,1)S(1)}, bf16[1792,192]{0,1:T(8,128)(2,1)}, u32[]{:S(2)}) copy-start(bf16[1792,192]{0,1:T(8,128)(2,1)} %param.12) | copy-start | bytes 2064388
  29.9 3.9 %collective-permute-start.9 = (bf16[2,128,2048]{2,1,0:T(8,128)(2,1)S(1)}, bf16[2,128,2048]{2,1,0:T(8,128)(2,1)S(1)}, u32[]{:S(2)}, u32[]{:S(2)}) collective-permute-start(bf16[2,128,2048]{2,1,0:T(8,128)(2,1)S(1)} %collective-permute-done.refs_2_), channel_id=1, source_target_pairs={{0,4},{1,5},{2,6},{3,7},{4,0},{5,1},{6,2},{7,3},{8,12},{9,13},{10,... | collective-permute-start | bytes 3145736 | tf_op jit(solution)/shard_map/ppermute | solution.py:85
  29.9 32.4 %collective-permute-start.6 = (bf16[2,128,2048]{2,1,0:T(8,128)(2,1)S(1)}, bf16[2,128,2048]{2,1,0:T(8,128)(2,1)S(1)}, u32[]{:S(2)}, u32[]{:S(2)}) collective-permute-start(bf16[2,128,2048]{2,1,0:T(8,128)(2,1)S(1)} %collective-permute-done.refs_2_), channel_id=1, source_target_pairs={{1,2},{2,1},{5,6},{6,5},{9,10},{10,9},{13,14},{14,13},{17,18},{18,... | collective-permute-start | bytes 3145736 | tf_op jit(solution)/shard_map/ppermute | solution.py:85
  30.8 31.5 %collective-permute-start.7 = (bf16[2,128,2048]{2,1,0:T(8,128)(2,1)S(1)}, bf16[2,128,2048]{2,1,0:T(8,128)(2,1)S(1)}, u32[]{:S(2)}, u32[]{:S(2)}) collective-permute-start(bf16[2,128,2048]{2,1,0:T(8,128)(2,1)S(1)} %collective-permute-done.refs_2_), channel_id=1, source_target_pairs={{0,8},{1,9},{2,10},{3,11},{4,12},{5,13},{6,14},{7,15},{8,0},{9,1},... | collective-permute-start | bytes 3145736 | tf_op jit(solution)/shard_map/ppermute | solution.py:85
  32.4 29.9 %collective-permute-start.5 = (bf16[2,128,2048]{2,1,0:T(8,128)(2,1)S(1)}, bf16[2,128,2048]{2,1,0:T(8,128)(2,1)S(1)}, u32[]{:S(2)}, u32[]{:S(2)}) collective-permute-start(bf16[2,128,2048]{2,1,0:T(8,128)(2,1)S(1)} %collective-permute-done.1), channel_id=1, source_target_pairs={{1,0},{2,3},{5,4},{6,7},{9,8},{10,11},{13,12},{14,15},{17,16},{18,... | collective-permute-start | bytes 3145736 | tf_op jit(solution)/shard_map/ppermute | solution.py:85
  33.6 28.6 %collective-permute-start.8 = (bf16[2,128,2048]{2,1,0:T(8,128)(2,1)S(1)}, bf16[2,128,2048]{2,1,0:T(8,128)(2,1)S(1)}, u32[]{:S(2)}, u32[]{:S(2)}) collective-permute-start(bf16[2,128,2048]{2,1,0:T(8,128)(2,1)S(1)} %collective-permute-done.2.refs_1_), channel_id=1, source_target_pairs={{0,4},{1,5},{2,6},{3,7},{4,0},{5,1},{6,2},{7,3},{8,12},{9,13},{10,... | collective-permute-start | bytes 3145736 | tf_op jit(solution)/shard_map/ppermute | solution.py:85
  62.3 2.7 %collective-permute-start.13 = (bf16[2,128,2048]{2,1,0:T(8,128)(2,1)S(1)}, bf16[2,128,2048]{2,1,0:T(8,128)(2,1)S(1)}, u32[]{:S(2)}, u32[]{:S(2)}) collective-permute-start(bf16[2,128,2048]{2,1,0:T(8,128)(2,1)S(1)} %collective-permute-done.7.refs_2_), channel_id=1, source_target_pairs={{0,4},{1,5},{2,6},{3,7},{4,0},{5,1},{6,2},{7,3},{8,12},{9,13},{10,... | collective-permute-start | bytes 3145736 | tf_op jit(solution)/shard_map/ppermute | solution.py:85
  62.5 25.6 %collective-permute-start.11 = (bf16[2,128,2048]{2,1,0:T(8,128)(2,1)S(1)}, bf16[2,128,2048]{2,1,0:T(8,128)(2,1)S(1)}, u32[]{:S(2)}, u32[]{:S(2)}) collective-permute-start(bf16[2,128,2048]{2,1,0:T(8,128)(2,1)S(1)} %broadcast_select_fusion.1.refs_1_), channel_id=1, source_target_pairs={{0,8},{1,9},{2,10},{3,11},{4,12},{5,13},{6,14},{7,15},{8,0},{9,1},... | collective-permute-start | bytes 3145736 | tf_op jit(solution)/shard_map/ppermute | solution.py:85
  63.0 25.1 %collective-permute-start.12 = (bf16[2,128,2048]{2,1,0:T(8,128)(2,1)S(1)}, bf16[2,128,2048]{2,1,0:T(8,128)(2,1)S(1)}, u32[]{:S(2)}, u32[]{:S(2)}) collective-permute-start(bf16[2,128,2048]{2,1,0:T(8,128)(2,1)S(1)} %broadcast_select_fusion.1.refs_1_), channel_id=1, source_target_pairs={{0,4},{1,5},{2,6},{3,7},{4,0},{5,1},{6,2},{7,3},{8,12},{9,13},{10,... | collective-permute-start | bytes 3145736 | tf_op jit(solution)/shard_map/ppermute | solution.py:85
  63.2 27.2 %collective-permute-start.10 = (bf16[2,128,2048]{2,1,0:T(8,128)(2,1)S(1)}, bf16[2,128,2048]{2,1,0:T(8,128)(2,1)S(1)}, u32[]{:S(2)}, u32[]{:S(2)}) collective-permute-start(bf16[2,128,2048]{2,1,0:T(8,128)(2,1)S(1)} %collective-permute-done.6), channel_id=1, source_target_pairs={{1,0},{2,3},{5,4},{6,7},{9,8},{10,11},{13,12},{14,15},{17,16},{18,... | collective-permute-start | bytes 3145736 | tf_op jit(solution)/shard_map/ppermute | solution.py:85
  90.6 25.8 %copy-start.1 = (f32[192,128]{1,0:T(8,128)S(1)}, f32[192,128]{1,0:T(8,128)}, u32[]{:S(2)}) copy-start(f32[192,128]{1,0:T(8,128)} %fusion.4) | copy-start | bytes 294916
  90.6 2.7 %collective-permute-start.17 = (bf16[2,128,2048]{2,1,0:T(8,128)(2,1)S(1)}, bf16[2,128,2048]{2,1,0:T(8,128)(2,1)S(1)}, u32[]{:S(2)}, u32[]{:S(2)}) collective-permute-start(bf16[2,128,2048]{2,1,0:T(8,128)(2,1)S(1)} %broadcast_select_fusion.refs_2_), channel_id=1, source_target_pairs={{0,4},{1,5},{2,6},{3,7},{4,0},{5,1},{6,2},{7,3},{8,12},{9,13},{10,... | collective-permute-start | bytes 3145736 | tf_op jit(solution)/shard_map/ppermute | solution.py:85
  90.7 25.6 %collective-permute-start.14 = (bf16[2,128,2048]{2,1,0:T(8,128)(2,1)S(1)}, bf16[2,128,2048]{2,1,0:T(8,128)(2,1)S(1)}, u32[]{:S(2)}, u32[]{:S(2)}) collective-permute-start(bf16[2,128,2048]{2,1,0:T(8,128)(2,1)S(1)} %broadcast_select_fusion.refs_2_), channel_id=1, source_target_pairs={{0,8},{1,9},{2,10},{3,11},{4,12},{5,13},{6,14},{7,15},{8,0},{9,1},... | collective-permute-start | bytes 3145736 | tf_op jit(solution)/shard_map/ppermute | solution.py:85
  92.3 24.0 %collective-permute-start.15 = (bf16[2,128,2048]{2,1,0:T(8,128)(2,1)S(1)}, bf16[2,128,2048]{2,1,0:T(8,128)(2,1)S(1)}, u32[]{:S(2)}, u32[]{:S(2)}) collective-permute-start(bf16[2,128,2048]{2,1,0:T(8,128)(2,1)S(1)} %collective-permute-done.11.refs_1_), channel_id=1, source_target_pairs={{0,4},{1,5},{2,6},{3,7},{4,0},{5,1},{6,2},{7,3},{8,12},{9,13},{10,... | collective-permute-start | bytes 3145736 | tf_op jit(solution)/shard_map/ppermute | solution.py:85
  92.4 20.5 %collective-permute-start.16 = (f32[96,256]{1,0:T(8,128)S(1)}, f32[96,256]{1,0:T(8,128)S(1)}, u32[]{:S(2)}, u32[]{:S(2)}) collective-permute-start(f32[96,256]{1,0:T(8,128)S(1)} %get-tuple-element.60), channel_id=1, source_target_pairs={{0,4},{1,5},{2,6},{3,7},{4,0},{5,1},{6,2},{7,3},{8,12},{9,13},{10,... | collective-permute-start | bytes 294920 | tf_op jit(solution)/shard_map/ppermute | solution.py:85
  116.3 2.7 %collective-permute-start.20 = (bf16[2,128,2048]{2,1,0:T(8,128)(2,1)S(1)}, bf16[2,128,2048]{2,1,0:T(8,128)(2,1)S(1)}, u32[]{:S(2)}, u32[]{:S(2)}) collective-permute-start(bf16[2,128,2048]{2,1,0:T(8,128)(2,1)S(1)} %collective-permute-done.14.refs_2_), channel_id=1, source_target_pairs={{0,4},{1,5},{2,6},{3,7},{4,0},{5,1},{6,2},{7,3},{8,12},{9,13},{10,... | collective-permute-start | bytes 3145736 | tf_op jit(solution)/shard_map/ppermute | solution.py:85
  116.3 48.4 %slice-start = ((s8[12582912]{0:T(1024)(128)(4,1)}), s8[4194304]{0:T(1024)(128)(4,1)S(1)}, s32[]{:S(2)}) async-start(s8[12582912]{0:T(1024)(128)(4,1)} %bitcast.14), calls=%async_computation | async-start | bytes 8388608
  116.3 48.4 %slice-start.1 = ((s8[12582912]{0:T(1024)(128)(4,1)}), s8[4194304]{0:T(1024)(128)(4,1)S(1)}, s32[]{:S(2)}) async-start(s8[12582912]{0:T(1024)(128)(4,1)} %bitcast.14), calls=%async_computation.1 | async-start | bytes 8388608
  116.3 48.3 %slice-start.2 = ((s8[12582912]{0:T(1024)(128)(4,1)}), s8[4194304]{0:T(1024)(128)(4,1)S(1)}, s32[]{:S(2)}) async-start(s8[12582912]{0:T(1024)(128)(4,1)} %bitcast.14), calls=%async_computation.2 | async-start | bytes 8388608
  116.3 24.0 %collective-permute-start.18 = (f32[96,128]{1,0:T(8,128)S(1)}, f32[96,128]{1,0:T(8,128)S(1)}, u32[]{:S(2)}, u32[]{:S(2)}) collective-permute-start(f32[96,128]{1,0:T(8,128)S(1)} %slice.24), channel_id=1, source_target_pairs={{0,1},{1,0},{2,3},{3,2},{4,5},{5,4},{6,7},{7,6},{8,9},{9,8},{10,11... | collective-permute-start | bytes 147464 | tf_op jit(solution)/shard_map/ppermute | solution.py:85
  116.4 23.9 %collective-permute-start.19 = (f32[192,128]{1,0:T(8,128)S(1)}, f32[192,128]{1,0:T(8,128)S(1)}, u32[]{:S(2)}, u32[]{:S(2)}) collective-permute-start(f32[192,128]{1,0:T(8,128)S(1)} %copy-done.1), channel_id=1, source_target_pairs={{0,8},{1,9},{2,10},{3,11},{4,12},{5,13},{6,14},{7,15},{8,0},{9,1},... | collective-permute-start | bytes 294920 | tf_op jit(solution)/shard_map/ppermute | solution.py:85
  140.4 1.5 collective-permute-start.21
  141.9 6.1 %collective-permute-start.22 = (f32[96,128]{1,0:T(8,128)S(1)}, f32[96,128]{1,0:T(8,128)S(1)}, u32[]{:S(2)}, u32[]{:S(2)}) collective-permute-start(f32[96,128]{1,0:T(8,128)S(1)} %get-tuple-element.75), channel_id=1, source_target_pairs={{0,2},{1,3},{2,0},{3,1},{4,6},{5,7},{6,4},{7,5},{8,10},{9,11},{10,... | collective-permute-start | bytes 147464 | tf_op jit(solution)/shard_map/ppermute | solution.py:85
  143.6 6.0 %collective-permute-start.23 = (f32[96,128]{1,0:T(8,128)S(1)}, f32[96,128]{1,0:T(8,128)S(1)}, u32[]{:S(2)}, u32[]{:S(2)}) collective-permute-start(f32[96,128]{1,0:T(8,128)S(1)} %get-tuple-element.76), channel_id=1, source_target_pairs={{0,3},{1,2},{2,1},{3,0},{4,7},{5,6},{6,5},{7,4},{8,11},{9,10},{10,... | collective-permute-start | bytes 147464 | tf_op jit(solution)/shard_map/ppermute | solution.py:85
  149.6 4.2 %collective-permute-start.24 = (f32[96,128]{1,0:T(8,128)S(1)}, f32[96,128]{1,0:T(8,128)S(1)}, u32[]{:S(2)}, u32[]{:S(2)}) collective-permute-start(f32[96,128]{1,0:T(8,128)S(1)} %fusion.3), channel_id=1, source_target_pairs={{0,8},{1,9},{2,10},{3,11},{4,12},{5,13},{6,14},{7,15},{8,0},{9,1},... | collective-permute-start | bytes 147464 | tf_op jit(solution)/shard_map/ppermute | solution.py:85
  153.8 1.3 collective-permute-start.25
  156.1 4.4 %collective-permute-start.26 = (f32[3,32,128]{2,1,0:T(8,128)S(1)}, f32[3,32,128]{2,1,0:T(8,128)S(1)}, u32[]{:S(2)}, u32[]{:S(2)}) collective-permute-start(f32[3,32,128]{2,1,0:T(8,128)S(1)} %sketch.1.refs_0_), channel_id=1, source_target_pairs={{0,1},{1,0},{2,3},{3,2},{4,5},{5,4},{6,7},{7,6},{8,9},{9,8},{10,11... | collective-permute-start | bytes 147464 | tf_op jit(solution)/shard_map/ppermute | solution.py:85
  157.1 6.7 %collective-permute-start.27 = (f32[3,32,128]{2,1,0:T(8,128)S(1)}, f32[3,32,128]{2,1,0:T(8,128)S(1)}, u32[]{:S(2)}, u32[]{:S(2)}) collective-permute-start(f32[3,32,128]{2,1,0:T(8,128)S(1)} %sketch.1.refs_0_), channel_id=1, source_target_pairs={{0,2},{1,3},{2,0},{3,1},{4,6},{5,7},{6,4},{7,5},{8,10},{9,11},{10,... | collective-permute-start | bytes 147464 | tf_op jit(solution)/shard_map/ppermute | solution.py:85
  158.7 6.0 %collective-permute-start.28 = (f32[3,32,128]{2,1,0:T(8,128)S(1)}, f32[3,32,128]{2,1,0:T(8,128)S(1)}, u32[]{:S(2)}, u32[]{:S(2)}) collective-permute-start(f32[3,32,128]{2,1,0:T(8,128)S(1)} %sketch.1.refs_0_), channel_id=1, source_target_pairs={{0,3},{1,2},{2,1},{3,0},{4,7},{5,6},{6,5},{7,4},{8,11},{9,10},{10,... | collective-permute-start | bytes 147464 | tf_op jit(solution)/shard_map/ppermute | solution.py:85

commit v5 on v4

--- a/solution.py
+++ b/solution.py
@@ -239,8 +239,14 @@
     )(where, feat_t, mine, other)
 
 
-def precond_kernel(row_ref, p_ref, *refs):
-    sketches, out_ref, sums = refs[:ROWS], refs[ROWS], refs[ROWS + 1]
+def precond_kernel(flips, row_ref, p_ref, *refs):
+    count = len(flips)
+    sketches, refs = refs[:count], refs[count:]
+    if count < ROWS and 0 not in flips:
+        own_ref, out_ref, sums = refs
+        out_ref[:, pl.ds(row_ref[0], 1), :] = own_ref[...]
+    else:
+        out_ref, sums = refs
     height = p_ref.shape[1]
     lanes = 2 * K
     group = 32
@@ -250,29 +256,33 @@
         @pl.loop(0, height // group)
         def _(g):
             at = pl.ds(pl.multiple_of(g * group, group), group)
-            totals = [jnp.zeros((group, lanes), jnp.float32) for _ in range(ROWS)]
+            totals = [jnp.zeros((group, lanes), jnp.float32) for _ in range(count)]
             for q in range(K // 2):
                 part = p_ref[w, at, pl.ds(q * lanes, lanes)]
-                for n in range(ROWS):
+                for n in range(count):
                     totals[n] = totals[n] + part * sketches[n][w, pl.ds(q, 1), :]
-            for n in range(ROWS):
+            for n in range(count):
                 sums[n, at, :] = totals[n]
 
-        for n in range(ROWS):
+        for n in range(count):
             line = jnp.sum(sums[n].T, axis=0, keepdims=True)
-            out_ref[w, pl.ds(row_ref[0] ^ n, 1), :] = line
-
-
-def apply_precond(row, precond, sketches):
+            if out_ref.shape[1] == 1:
+                out_ref[w] = line
+            else:
+                out_ref[w, pl.ds(row_ref[0] ^ flips[n], 1), :] = line
+
+
+def apply_precond(row, precond, sketches, flips, own=None):
     height = precond.shape[1]
     whole = pl.BlockSpec(memory_space=pltpu.VMEM)
-    operands = [pltpu.with_memory_space_constraint(a, pltpu.VMEM) for a in [precond, *sketches]]
+    operands = [precond, *sketches] + ([] if own is None else [own])
+    operands = [pltpu.with_memory_space_constraint(a, pltpu.VMEM) for a in operands]
     return pl.pallas_call(
-        precond_kernel,
-        out_shape=jax.ShapeDtypeStruct((3, ROWS, height), jnp.float32),
-        in_specs=[pl.BlockSpec(memory_space=pltpu.SMEM)] + [whole] * (1 + ROWS),
+        functools.partial(precond_kernel, flips),
+        out_shape=jax.ShapeDtypeStruct((3, 1 if own is None else ROWS, height), jnp.float32),
+        in_specs=[pl.BlockSpec(memory_space=pltpu.SMEM)] + [whole] * len(operands),
         out_specs=whole,
-        scratch_shapes=[pltpu.VMEM((ROWS, height, 2 * K), jnp.float32)],
+        scratch_shapes=[pltpu.VMEM((len(flips), height, 2 * K), jnp.float32)],
         compiler_params=pltpu.CompilerParams(vmem_limit_bytes=4 * MIB),
         name="precond",
     )(row, *operands)
@@ -329,7 +339,8 @@
     near_y = other_chip(near)
     own_d = other_core(own_y)
     (acc,) = step([(A, (own, near)), (C, (own_c, near_c))], w_gate_up, w_down)
-    passed, middle_2, near_y, own_d, acc = tie(passed, middle_2, near_y, own_d, acc)
+    passed, middle_2, near_y, own_d, feat_t, acc = tie(passed, middle_2, near_y, own_d, feat_t, acc)
+    feat_y = other_chip(feat_t)
 
     near_d = other_core(near_y)
     third = jnp.where(inner, middle, passed)
@@ -339,7 +350,10 @@
     mine_0, theirs_0 = step(
         [(Y, (own_y, near_y)), (D, (own_d, near_d))], w_gate_up, w_down, acc, unit_proj_t
     )
-    passed_2, third_y, third_c, mine_0, theirs_0 = tie(passed_2, third_y, third_c, mine_0, theirs_0)
+    passed_2, third_y, third_c, mine_0, theirs_0, feat_y = tie(
+        passed_2, third_y, third_c, mine_0, theirs_0, feat_y
+    )
+    feat_t = feat_t + feat_y
 
     fourth = jnp.where(inner, middle_2, passed_2)
     fourth_c = other_core(fourth)
@@ -350,25 +364,25 @@
     fourth_y, third_d, mine_0, theirs_0, feat_t, acc = tie(fourth_y, third_d, mine_0, theirs_0, feat_t, acc)
 
     fourth_d = other_core(fourth_y)
-    feat_y = other_chip(feat_t)
     mine_0 = mine_0 + theirs_0
     near_part = send(mine_0[:, SEQ:], swap_rows(1))
     mine_1, theirs_1 = step(
         [(Y, (third_y, fourth_y)), (D, (third_d, fourth_d))], w_gate_up, w_down, acc, unit_proj_t
     )
 
-    near_part, feat_y, mine_1, theirs_1 = tie(near_part, feat_y, mine_1, theirs_1)
+    near_part, mine_1, theirs_1 = tie(near_part, mine_1, theirs_1)
 
     mine_1 = mine_1 + other_core(theirs_1)
     low, high = mine_1[:, :SEQ], mine_1[:, SEQ:]
     part = mine_0[:, :SEQ] + near_part
-    feat_t = feat_t + feat_y
     part = part + send(jnp.where(inner, high, low), swap_rows(2)) + send(jnp.where(inner, low, high), swap_rows(3))
     part = part + other_chip(part)
     other = other_core(part)
     sketch = sketch_own(where, feat_t, part, other)
-    sketches = [sketch] + [send(sketch, swap_rows(n)) for n in range(1, ROWS)]
-    return apply_precond(row, precond, sketches)
+    sketches = [send(sketch, swap_rows(n)) for n in range(1, ROWS)]
+    own_line = apply_precond(row, precond, [sketch], (0,))
+    sketches, own_line = tie(sketches, own_line)
+    return apply_precond(row, precond, sketches, (1, 2, 3), own_line)
 
 
 def local(hidden_in, out_grad, w_gate_up, w_down, feat_proj, unit_proj, precond):

time: 171 us -> 169 us (0.988)
  waiting for transfers between devices: 51.9 us -> 49.7 us
    ppermute x29, waiting for transfers between devices: 51.9 us -> 49.7 us  [send(): return lax.ppermute(value, BOTH, pairs)]
    pallas_call x1 -> x2, Pallas kernels: 5.71 us -> 6.58 us  [apply_precond(): pl.pallas_call(functools.partial(precond_kernel, flips), out_shape=jax.Sh...]
  transfers between devices with their start and end apart: 29 -> 29, of which waited for: 17 -> 15; matrix products, arithmetic and copies ran while one was open for 2% -> 2% of each run, Pallas kernels for 48% -> 49%
where the time goes in v5:
time: 169 us
  Pallas kernels  89.2 us (53%)
  waiting for transfers between devices  49.7 us (29%)
  starting transfers between devices  25.2 us (15%)
  matrix products  2.9 us (2%)
  other arithmetic  1.69 us (1%)
    pallas_call x4, Pallas kernels, matmul_step(): pl.pallas_call(functools.partial(matmul_kernel, count, last), out_shape=o...  81.5 us
    ppermute x29, waiting for transfers between devices, send(): return lax.ppermute(value, BOTH, pairs)  49.7 us
    ppermute x29, starting transfers between devices, send(): return lax.ppermute(value, BOTH, pairs)  25.2 us
    pallas_call x2, Pallas kernels, apply_precond(): pl.pallas_call(functools.partial(precond_kernel, flips), out_shape=jax.Sh...  6.58 us
  transfers between devices with their start and end apart: 29, of which 15 were waited for; matrix products, arithmetic and copies ran while one was open for 2% of the time, Pallas kernels for 49%

profile of v5, /device:TPU:0, one launch (start us, length us, event | category | flops | bytes accessed | tf_op | source)
XLA Modules:
  0.0 168.9 jit_solution(7116925011047333980)
XLA Ops:
  0.1 1.3 pad_maximum_fusion.refs_1_
  1.4 3.1 %collective-permute-start = (bf16[2,128,2048]{2,1,0:T(8,128)(2,1)S(1)}, bf16[2,128,2048]{2,1,0:T(8,128)(2,1)S(1)}, u32[]{:S(2)}, u32[]{:S(2)}) collective-permute-start(bf16[2,128,2048]{2,1,0:T(8,128)(2,1)S(1)} %pad_maximum_fusion.refs_1_), channel_id=1, source_target_pairs={{0,1},{1,0},{2,3},{3,2},{4,5},{5,4},{6,7},{7,6},{8,9},{9,8},{10,11... | collective-permute-start | bytes 3145736 | tf_op jit(solution)/shard_map/ppermute | solution.py:85
  4.5 0.7 collective-permute-start.1
  5.2 1.6 collective-permute-start.2
  6.8 1.4 convolution_bitcast_fusion.1
  8.2 1.5 convolution_bitcast_fusion
  9.7 0.6 collective-permute-start.4
  10.3 0.9 collective-permute-done.4
  11.2 16.4 %collective-permute-done.refs_2_ = bf16[2,128,2048]{2,1,0:T(8,128)(2,1)S(1)} collective-permute-done((bf16[2,128,2048]{2,1,0:T(8,128)(2,1)S(1)}, bf16[2,128,2048]{2,1,0:T(8,128)(2,1)S(1)}, u32[]{:S(2)}, u32[]{:S(2)}) %collective-permute-start) | collective-permute-done | bytes 1048608 | tf_op jit(solution)/shard_map/ppermute | solution.py:85
  27.6 2.2 %collective-permute-done.2.refs_1_ = bf16[2,128,2048]{2,1,0:T(8,128)(2,1)S(1)} collective-permute-done((bf16[2,128,2048]{2,1,0:T(8,128)(2,1)S(1)}, bf16[2,128,2048]{2,1,0:T(8,128)(2,1)S(1)}, u32[]{:S(2)}, u32[]{:S(2)}) %collective-permute-start.2) | collective-permute-done | bytes 1048608 | tf_op jit(solution)/shard_map/ppermute | solution.py:85
  29.9 0.9 collective-permute-start.6
  30.8 1.6 collective-permute-start.7
  32.4 1.3 collective-permute-start.5
  33.6 0.1 collective-permute-start.8
  33.8 19.6 %matmul.4.refs_9_ = f32[7,3,256,256]{3,2,1,0:T(8,128)S(1)} custom-call(s32[4]{0:T(128)S(1)} %pad_add_fusion.refs_0_.where_ref, bf16[2,128,2048]{2,1,0:T(8,128)(2,1)S(1)} %pad_maximum_fusion.refs_1_, bf16[2,128,2048]{2,1,0:T(8,128)(2,1)S(1)} %collective-permute-done.refs_2_, bf16[2,128,2048]{2,1,0:T(8,128)(2,1)S(1)} %collective-permute-done.3.refs_3_, ...), custom_call_target="tpu_custom_call" | custom-call | flops 11274289152 | bytes 44040192 | tf_op jit(solution)/shard_map/matmul/pallas_call | solution.py:188
  53.4 8.9 %collective-permute-done.5 = bf16[2,128,2048]{2,1,0:T(8,128)(2,1)S(1)} collective-permute-done((bf16[2,128,2048]{2,1,0:T(8,128)(2,1)S(1)}, bf16[2,128,2048]{2,1,0:T(8,128)(2,1)S(1)}, u32[]{:S(2)}, u32[]{:S(2)}) %collective-permute-start.5) | collective-permute-done | bytes 1048608 | tf_op jit(solution)/shard_map/ppermute | solution.py:85
  62.3 0.1 broadcast_select_fusion.1.refs_1_
  62.5 0.6 collective-permute-start.11
  63.0 0.2 collective-permute-start.12
  63.2 1.3 collective-permute-start.10
  64.5 1.6 collective-permute-start.14
  66.1 21.0 %matmul.5 = (f32[96,256]{1,0:T(8,128)S(1)}, f32[96,256]{1,0:T(8,128)S(1)}) custom-call(s32[4]{0:T(128)S(1)} %pad_add_fusion.refs_0_.where_ref, bf16[2,128,2048]{2,1,0:T(8,128)(2,1)S(1)} %collective-permute-done.2.refs_1_, bf16[2,128,2048]{2,1,0:T(8,128)(2,1)S(1)} %collective-permute-done.7.refs_2_, bf16[2,128,2048]{2,1,0:T(8,128)(2,1)S(1)} %collective-permute-done.8.refs_3_, ...), custom_call_target="tpu_custom_call" | custom-call | flops 11274289152 | bytes 44040192 | tf_op jit(solution)/shard_map/matmul/pallas_call | solution.py:188
  87.1 3.1 %collective-permute-done.14 = f32[192,128]{1,0:T(8,128)S(1)} collective-permute-done((f32[192,128]{1,0:T(8,128)S(1)}, f32[192,128]{1,0:T(8,128)S(1)}, u32[]{:S(2)}, u32[]{:S(2)}) %collective-permute-start.14) | collective-permute-done | bytes 98336 | tf_op jit(solution)/shard_map/ppermute | solution.py:85
  90.2 0.3 collective-permute-done.10
  90.7 1.6 collective-permute-start.15
  92.3 0.2 collective-permute-start.16
  92.5 0.3 collective-permute-start.17
  92.9 0.5 collective-permute-done.18.refs_4_
  93.3 19.6 %matmul.6.refs_9_ = f32[7,3,256,256]{3,2,1,0:T(8,128)S(1)} custom-call(s32[4]{0:T(128)S(1)} %pad_add_fusion.refs_0_.where_ref, bf16[2,128,2048]{2,1,0:T(8,128)(2,1)S(1)} %broadcast_select_fusion.1.refs_1_, bf16[2,128,2048]{2,1,0:T(8,128)(2,1)S(1)} %broadcast_select_fusion.refs_2_, bf16[2,128,2048]{2,1,0:T(8,128)(2,1)S(1)} %collective-permute-done.12.refs_3_, ...), custom_call_target="tpu_custom_call" | custom-call | flops 11274289152 | bytes 44040192 | tf_op jit(solution)/shard_map/matmul/pallas_call | solution.py:188
  112.9 3.3 %collective-permute-done.15.refs_2_ = bf16[2,128,2048]{2,1,0:T(8,128)(2,1)S(1)} collective-permute-done((bf16[2,128,2048]{2,1,0:T(8,128)(2,1)S(1)}, bf16[2,128,2048]{2,1,0:T(8,128)(2,1)S(1)}, u32[]{:S(2)}, u32[]{:S(2)}) %collective-permute-start.15) | collective-permute-done | bytes 1048608 | tf_op jit(solution)/shard_map/ppermute | solution.py:85
  116.4 2.5 %collective-permute-done.20.refs_4_ = bf16[2,128,2048]{2,1,0:T(8,128)(2,1)S(1)} collective-permute-done((bf16[2,128,2048]{2,1,0:T(8,128)(2,1)S(1)}, bf16[2,128,2048]{2,1,0:T(8,128)(2,1)S(1)}, u32[]{:S(2)}, u32[]{:S(2)}) %collective-permute-start.20) | collective-permute-done | bytes 1048608 | tf_op jit(solution)/shard_map/ppermute | solution.py:85
  118.9 21.4 %matmul.7 = (f32[96,256]{1,0:T(8,128)S(1)}, f32[96,256]{1,0:T(8,128)S(1)}) custom-call(s32[4]{0:T(128)S(1)} %pad_add_fusion.refs_0_.where_ref, bf16[2,128,2048]{2,1,0:T(8,128)(2,1)S(1)} %collective-permute-done.11.refs_1_, bf16[2,128,2048]{2,1,0:T(8,128)(2,1)S(1)} %collective-permute-done.15.refs_2_, ...), custom_call_target="tpu_custom_call" | custom-call | flops 11274289152 | bytes 44040192 | tf_op jit(solution)/shard_map/matmul/pallas_call | solution.py:188
  140.4 0.5 collective-permute-start.21
  140.9 0.9 collective-permute-done.21
  141.9 0.8 collective-permute-start.22
  142.7 2.0 %collective-permute-start.23 = (f32[96,128]{1,0:T(8,128)S(1)}, f32[96,128]{1,0:T(8,128)S(1)}, u32[]{:S(2)}, u32[]{:S(2)}) collective-permute-start(f32[96,128]{1,0:T(8,128)S(1)} %get-tuple-element.86), channel_id=1, source_target_pairs={{0,3},{1,2},{2,1},{3,0},{4,7},{5,6},{6,5},{7,4},{8,11},{9,10},{10,... | collective-permute-start | bytes 147464 | tf_op jit(solution)/shard_map/ppermute | solution.py:85
  144.7 4.3 %collective-permute-done.22 = f32[96,128]{1,0:T(8,128)S(1)} collective-permute-done((f32[96,128]{1,0:T(8,128)S(1)}, f32[96,128]{1,0:T(8,128)S(1)}, u32[]{:S(2)}, u32[]{:S(2)}) %collective-permute-start.22) | collective-permute-done | bytes 49184 | tf_op jit(solution)/shard_map/ppermute | solution.py:85
  149.0 1.6 collective-permute-start.24
  150.6 2.6 %collective-permute-done.24 = f32[96,128]{1,0:T(8,128)S(1)} collective-permute-done((f32[96,128]{1,0:T(8,128)S(1)}, f32[96,128]{1,0:T(8,128)S(1)}, u32[]{:S(2)}, u32[]{:S(2)}) %collective-permute-start.24) | collective-permute-done | bytes 49184 | tf_op jit(solution)/shard_map/ppermute | solution.py:85
  153.2 1.2 collective-permute-done.25.other_ref
  154.5 1.0 sketch.1.refs_0_
  155.5 1.6 collective-permute-start.26
  157.1 1.1 collective-permute-start.27
  158.2 1.7 %collective-permute-start.28 = (f32[3,32,128]{2,1,0:T(8,128)S(1)}, f32[3,32,128]{2,1,0:T(8,128)S(1)}, u32[]{:S(2)}, u32[]{:S(2)}) collective-permute-start(f32[3,32,128]{2,1,0:T(8,128)S(1)} %sketch.1.refs_0_), channel_id=1, source_target_pairs={{0,3},{1,2},{2,1},{3,0},{4,7},{5,6},{6,5},{7,4},{8,11},{9,10},{10,... | collective-permute-start | bytes 147464 | tf_op jit(solution)/shard_map/ppermute | solution.py:85
  159.9 1.8 %precond.2.refs_3_ = f32[3,1,256]{2,1,0:T(1,128)S(1)} custom-call(s32[1]{0:T(128)} %bitcast.4.row_ref, f32[3,256,4096]{2,1,0:T(8,128)S(1)} %bitcast.15, f32[3,32,128]{2,1,0:T(8,128)S(1)} %sketch.1.refs_0_), custom_call_target="tpu_custom_call" | custom-call | tf_op jit(solution)/shard_map/precond/pallas_call | solution.py:280
  161.7 1.8 %collective-permute-done.27.refs_1_ = f32[3,32,128]{2,1,0:T(8,128)S(1)} collective-permute-done((f32[3,32,128]{2,1,0:T(8,128)S(1)}, f32[3,32,128]{2,1,0:T(8,128)S(1)}, u32[]{:S(2)}, u32[]{:S(2)}) %collective-permute-start.27) | collective-permute-done | bytes 49184 | tf_op jit(solution)/shard_map/ppermute | solution.py:85
  163.5 0.6 collective-permute-done.28.refs_2_
  164.2 4.8 %precond.3 = f32[3,4,256]{2,1,0:T(4,128)} custom-call(s32[1]{0:T(128)} %bitcast.4.row_ref, f32[3,256,4096]{2,1,0:T(8,128)S(1)} %bitcast.15, f32[3,32,128]{2,1,0:T(8,128)S(1)} %collective-permute-done.26.refs_0_, f32[3,32,128]{2,1,0:T(8,128)S(1)} %collective-permute-done.27.refs_1_, f32[3,32,128]{2,1,0:T(8,128)S(1)} %collective-permute-done.28.refs_2_, ...), custom_call_target="tpu_custom_call" | custom-call | tf_op jit(solution)/shard_map/precond/pallas_call | solution.py:280
  (41 shorter events, 0.6 us)
Async XLA Ops:
  1.4 26.2 %collective-permute-start = (bf16[2,128,2048]{2,1,0:T(8,128)(2,1)S(1)}, bf16[2,128,2048]{2,1,0:T(8,128)(2,1)S(1)}, u32[]{:S(2)}, u32[]{:S(2)}) collective-permute-start(bf16[2,128,2048]{2,1,0:T(8,128)(2,1)S(1)} %pad_maximum_fusion.refs_1_), channel_id=1, source_target_pairs={{0,1},{1,0},{2,3},{3,2},{4,5},{5,4},{6,7},{7,6},{8,9},{9,8},{10,11... | collective-permute-start | bytes 3145736 | tf_op jit(solution)/shard_map/ppermute | solution.py:85
  4.5 23.2 %collective-permute-start.1 = (bf16[2,128,2048]{2,1,0:T(8,128)(2,1)S(1)}, bf16[2,128,2048]{2,1,0:T(8,128)(2,1)S(1)}, u32[]{:S(2)}, u32[]{:S(2)}) collective-permute-start(bf16[2,128,2048]{2,1,0:T(8,128)(2,1)S(1)} %pad_maximum_fusion.refs_1_), channel_id=1, source_target_pairs={{1,2},{2,1},{5,6},{6,5},{9,10},{10,9},{13,14},{14,13},{17,18},{18,... | collective-permute-start | bytes 3145736 | tf_op jit(solution)/shard_map/ppermute | solution.py:85
  5.2 24.7 %collective-permute-start.2 = (bf16[2,128,2048]{2,1,0:T(8,128)(2,1)S(1)}, bf16[2,128,2048]{2,1,0:T(8,128)(2,1)S(1)}, u32[]{:S(2)}, u32[]{:S(2)}) collective-permute-start(bf16[2,128,2048]{2,1,0:T(8,128)(2,1)S(1)} %pad_maximum_fusion.refs_1_), channel_id=1, source_target_pairs={{0,8},{1,9},{2,10},{3,11},{4,12},{5,13},{6,14},{7,15},{8,0},{9,1},... | collective-permute-start | bytes 3145736 | tf_op jit(solution)/shard_map/ppermute | solution.py:85
  6.8 23.1 %collective-permute-start.3 = (bf16[2,128,2048]{2,1,0:T(8,128)(2,1)S(1)}, bf16[2,128,2048]{2,1,0:T(8,128)(2,1)S(1)}, u32[]{:S(2)}, u32[]{:S(2)}) collective-permute-start(bf16[2,128,2048]{2,1,0:T(8,128)(2,1)S(1)} %pad_maximum_fusion.refs_1_), channel_id=1, source_target_pairs={{0,4},{1,5},{2,6},{3,7},{4,0},{5,1},{6,2},{7,3},{8,12},{9,13},{10,... | collective-permute-start | bytes 3145736 | tf_op jit(solution)/shard_map/ppermute | solution.py:85
  9.7 1.5 collective-permute-start.4
  29.9 36.2 %copy-start = (bf16[1792,192]{0,1:T(8,128)(2,1)S(1)}, bf16[1792,192]{0,1:T(8,128)(2,1)}, u32[]{:S(2)}) copy-start(bf16[1792,192]{0,1:T(8,128)(2,1)} %param.12) | copy-start | bytes 2064388
  29.9 3.9 %collective-permute-start.9 = (bf16[2,128,2048]{2,1,0:T(8,128)(2,1)S(1)}, bf16[2,128,2048]{2,1,0:T(8,128)(2,1)S(1)}, u32[]{:S(2)}, u32[]{:S(2)}) collective-permute-start(bf16[2,128,2048]{2,1,0:T(8,128)(2,1)S(1)} %collective-permute-done.refs_2_), channel_id=1, source_target_pairs={{0,4},{1,5},{2,6},{3,7},{4,0},{5,1},{6,2},{7,3},{8,12},{9,13},{10,... | collective-permute-start | bytes 3145736 | tf_op jit(solution)/shard_map/ppermute | solution.py:85
  29.9 32.4 %collective-permute-start.6 = (bf16[2,128,2048]{2,1,0:T(8,128)(2,1)S(1)}, bf16[2,128,2048]{2,1,0:T(8,128)(2,1)S(1)}, u32[]{:S(2)}, u32[]{:S(2)}) collective-permute-start(bf16[2,128,2048]{2,1,0:T(8,128)(2,1)S(1)} %collective-permute-done.refs_2_), channel_id=1, source_target_pairs={{1,2},{2,1},{5,6},{6,5},{9,10},{10,9},{13,14},{14,13},{17,18},{18,... | collective-permute-start | bytes 3145736 | tf_op jit(solution)/shard_map/ppermute | solution.py:85
  30.8 31.5 %collective-permute-start.7 = (bf16[2,128,2048]{2,1,0:T(8,128)(2,1)S(1)}, bf16[2,128,2048]{2,1,0:T(8,128)(2,1)S(1)}, u32[]{:S(2)}, u32[]{:S(2)}) collective-permute-start(bf16[2,128,2048]{2,1,0:T(8,128)(2,1)S(1)} %collective-permute-done.refs_2_), channel_id=1, source_target_pairs={{0,8},{1,9},{2,10},{3,11},{4,12},{5,13},{6,14},{7,15},{8,0},{9,1},... | collective-permute-start | bytes 3145736 | tf_op jit(solution)/shard_map/ppermute | solution.py:85
  32.4 29.9 %collective-permute-start.5 = (bf16[2,128,2048]{2,1,0:T(8,128)(2,1)S(1)}, bf16[2,128,2048]{2,1,0:T(8,128)(2,1)S(1)}, u32[]{:S(2)}, u32[]{:S(2)}) collective-permute-start(bf16[2,128,2048]{2,1,0:T(8,128)(2,1)S(1)} %collective-permute-done.1), channel_id=1, source_target_pairs={{1,0},{2,3},{5,4},{6,7},{9,8},{10,11},{13,12},{14,15},{17,16},{18,... | collective-permute-start | bytes 3145736 | tf_op jit(solution)/shard_map/ppermute | solution.py:85
  33.6 28.6 %collective-permute-start.8 = (bf16[2,128,2048]{2,1,0:T(8,128)(2,1)S(1)}, bf16[2,128,2048]{2,1,0:T(8,128)(2,1)S(1)}, u32[]{:S(2)}, u32[]{:S(2)}) collective-permute-start(bf16[2,128,2048]{2,1,0:T(8,128)(2,1)S(1)} %collective-permute-done.2.refs_1_), channel_id=1, source_target_pairs={{0,4},{1,5},{2,6},{3,7},{4,0},{5,1},{6,2},{7,3},{8,12},{9,13},{10,... | collective-permute-start | bytes 3145736 | tf_op jit(solution)/shard_map/ppermute | solution.py:85
  62.3 3.9 %collective-permute-start.13 = (bf16[2,128,2048]{2,1,0:T(8,128)(2,1)S(1)}, bf16[2,128,2048]{2,1,0:T(8,128)(2,1)S(1)}, u32[]{:S(2)}, u32[]{:S(2)}) collective-permute-start(bf16[2,128,2048]{2,1,0:T(8,128)(2,1)S(1)} %collective-permute-done.7.refs_2_), channel_id=1, source_target_pairs={{0,4},{1,5},{2,6},{3,7},{4,0},{5,1},{6,2},{7,3},{8,12},{9,13},{10,... | collective-permute-start | bytes 3145736 | tf_op jit(solution)/shard_map/ppermute | solution.py:85
  62.5 27.7 %collective-permute-start.11 = (bf16[2,128,2048]{2,1,0:T(8,128)(2,1)S(1)}, bf16[2,128,2048]{2,1,0:T(8,128)(2,1)S(1)}, u32[]{:S(2)}, u32[]{:S(2)}) collective-permute-start(bf16[2,128,2048]{2,1,0:T(8,128)(2,1)S(1)} %broadcast_select_fusion.1.refs_1_), channel_id=1, source_target_pairs={{0,8},{1,9},{2,10},{3,11},{4,12},{5,13},{6,14},{7,15},{8,0},{9,1},... | collective-permute-start | bytes 3145736 | tf_op jit(solution)/shard_map/ppermute | solution.py:85
  63.0 27.2 %collective-permute-start.12 = (bf16[2,128,2048]{2,1,0:T(8,128)(2,1)S(1)}, bf16[2,128,2048]{2,1,0:T(8,128)(2,1)S(1)}, u32[]{:S(2)}, u32[]{:S(2)}) collective-permute-start(bf16[2,128,2048]{2,1,0:T(8,128)(2,1)S(1)} %broadcast_select_fusion.1.refs_1_), channel_id=1, source_target_pairs={{0,4},{1,5},{2,6},{3,7},{4,0},{5,1},{6,2},{7,3},{8,12},{9,13},{10,... | collective-permute-start | bytes 3145736 | tf_op jit(solution)/shard_map/ppermute | solution.py:85
  63.2 27.2 %collective-permute-start.10 = (bf16[2,128,2048]{2,1,0:T(8,128)(2,1)S(1)}, bf16[2,128,2048]{2,1,0:T(8,128)(2,1)S(1)}, u32[]{:S(2)}, u32[]{:S(2)}) collective-permute-start(bf16[2,128,2048]{2,1,0:T(8,128)(2,1)S(1)} %collective-permute-done.6), channel_id=1, source_target_pairs={{1,0},{2,3},{5,4},{6,7},{9,8},{10,11},{13,12},{14,15},{17,16},{18,... | collective-permute-start | bytes 3145736 | tf_op jit(solution)/shard_map/ppermute | solution.py:85
  64.5 25.7 %collective-permute-start.14 = (f32[192,128]{1,0:T(8,128)S(1)}, f32[192,128]{1,0:T(8,128)S(1)}, u32[]{:S(2)}, u32[]{:S(2)}) collective-permute-start(f32[192,128]{1,0:T(8,128)S(1)} %fusion.4), channel_id=1, source_target_pairs={{0,8},{1,9},{2,10},{3,11},{4,12},{5,13},{6,14},{7,15},{8,0},{9,1},... | collective-permute-start | bytes 294920 | tf_op jit(solution)/shard_map/ppermute | solution.py:85
  90.6 2.7 %collective-permute-start.18 = (bf16[2,128,2048]{2,1,0:T(8,128)(2,1)S(1)}, bf16[2,128,2048]{2,1,0:T(8,128)(2,1)S(1)}, u32[]{:S(2)}, u32[]{:S(2)}) collective-permute-start(bf16[2,128,2048]{2,1,0:T(8,128)(2,1)S(1)} %broadcast_select_fusion.refs_2_), channel_id=1, source_target_pairs={{0,4},{1,5},{2,6},{3,7},{4,0},{5,1},{6,2},{7,3},{8,12},{9,13},{10,... | collective-permute-start | bytes 3145736 | tf_op jit(solution)/shard_map/ppermute | solution.py:85
  90.7 25.6 %collective-permute-start.15 = (bf16[2,128,2048]{2,1,0:T(8,128)(2,1)S(1)}, bf16[2,128,2048]{2,1,0:T(8,128)(2,1)S(1)}, u32[]{:S(2)}, u32[]{:S(2)}) collective-permute-start(bf16[2,128,2048]{2,1,0:T(8,128)(2,1)S(1)} %broadcast_select_fusion.refs_2_), channel_id=1, source_target_pairs={{0,8},{1,9},{2,10},{3,11},{4,12},{5,13},{6,14},{7,15},{8,0},{9,1},... | collective-permute-start | bytes 3145736 | tf_op jit(solution)/shard_map/ppermute | solution.py:85
  92.3 24.0 %collective-permute-start.16 = (bf16[2,128,2048]{2,1,0:T(8,128)(2,1)S(1)}, bf16[2,128,2048]{2,1,0:T(8,128)(2,1)S(1)}, u32[]{:S(2)}, u32[]{:S(2)}) collective-permute-start(bf16[2,128,2048]{2,1,0:T(8,128)(2,1)S(1)} %collective-permute-done.11.refs_1_), channel_id=1, source_target_pairs={{0,4},{1,5},{2,6},{3,7},{4,0},{5,1},{6,2},{7,3},{8,12},{9,13},{10,... | collective-permute-start | bytes 3145736 | tf_op jit(solution)/shard_map/ppermute | solution.py:85
  92.5 20.4 %collective-permute-start.17 = (f32[96,256]{1,0:T(8,128)S(1)}, f32[96,256]{1,0:T(8,128)S(1)}, u32[]{:S(2)}, u32[]{:S(2)}) collective-permute-start(f32[96,256]{1,0:T(8,128)S(1)} %get-tuple-element.67), channel_id=1, source_target_pairs={{0,4},{1,5},{2,6},{3,7},{4,0},{5,1},{6,2},{7,3},{8,12},{9,13},{10,... | collective-permute-start | bytes 294920 | tf_op jit(solution)/shard_map/ppermute | solution.py:85
  116.3 2.7 %collective-permute-start.20 = (bf16[2,128,2048]{2,1,0:T(8,128)(2,1)S(1)}, bf16[2,128,2048]{2,1,0:T(8,128)(2,1)S(1)}, u32[]{:S(2)}, u32[]{:S(2)}) collective-permute-start(bf16[2,128,2048]{2,1,0:T(8,128)(2,1)S(1)} %collective-permute-done.15.refs_2_), channel_id=1, source_target_pairs={{0,4},{1,5},{2,6},{3,7},{4,0},{5,1},{6,2},{7,3},{8,12},{9,13},{10,... | collective-permute-start | bytes 3145736 | tf_op jit(solution)/shard_map/ppermute | solution.py:85
  116.3 43.6 %slice-start = ((s8[12582912]{0:T(1024)(128)(4,1)}), s8[4194304]{0:T(1024)(128)(4,1)S(1)}, s32[]{:S(2)}) async-start(s8[12582912]{0:T(1024)(128)(4,1)} %bitcast.14), calls=%async_computation | async-start | bytes 8388608
  116.3 43.6 %slice-start.1 = ((s8[12582912]{0:T(1024)(128)(4,1)}), s8[4194304]{0:T(1024)(128)(4,1)S(1)}, s32[]{:S(2)}) async-start(s8[12582912]{0:T(1024)(128)(4,1)} %bitcast.14), calls=%async_computation.1 | async-start | bytes 8388608
  116.3 43.6 %slice-start.2 = ((s8[12582912]{0:T(1024)(128)(4,1)}), s8[4194304]{0:T(1024)(128)(4,1)S(1)}, s32[]{:S(2)}) async-start(s8[12582912]{0:T(1024)(128)(4,1)} %bitcast.14), calls=%async_computation.2 | async-start | bytes 8388608
  116.3 24.0 %collective-permute-start.19 = (f32[96,128]{1,0:T(8,128)S(1)}, f32[96,128]{1,0:T(8,128)S(1)}, u32[]{:S(2)}, u32[]{:S(2)}) collective-permute-start(f32[96,128]{1,0:T(8,128)S(1)} %slice.25), channel_id=1, source_target_pairs={{0,1},{1,0},{2,3},{3,2},{4,5},{5,4},{6,7},{7,6},{8,9},{9,8},{10,11... | collective-permute-start | bytes 147464 | tf_op jit(solution)/shard_map/ppermute | solution.py:85
  140.4 1.5 collective-permute-start.21
  141.9 7.1 %collective-permute-start.22 = (f32[96,128]{1,0:T(8,128)S(1)}, f32[96,128]{1,0:T(8,128)S(1)}, u32[]{:S(2)}, u32[]{:S(2)}) collective-permute-start(f32[96,128]{1,0:T(8,128)S(1)} %get-tuple-element.85), channel_id=1, source_target_pairs={{0,2},{1,3},{2,0},{3,1},{4,6},{5,7},{6,4},{7,5},{8,10},{9,11},{10,... | collective-permute-start | bytes 147464 | tf_op jit(solution)/shard_map/ppermute | solution.py:85
  142.7 6.3 %collective-permute-start.23 = (f32[96,128]{1,0:T(8,128)S(1)}, f32[96,128]{1,0:T(8,128)S(1)}, u32[]{:S(2)}, u32[]{:S(2)}) collective-permute-start(f32[96,128]{1,0:T(8,128)S(1)} %get-tuple-element.86), channel_id=1, source_target_pairs={{0,3},{1,2},{2,1},{3,0},{4,7},{5,6},{6,5},{7,4},{8,11},{9,10},{10,... | collective-permute-start | bytes 147464 | tf_op jit(solution)/shard_map/ppermute | solution.py:85
  149.0 4.2 %collective-permute-start.24 = (f32[96,128]{1,0:T(8,128)S(1)}, f32[96,128]{1,0:T(8,128)S(1)}, u32[]{:S(2)}, u32[]{:S(2)}) collective-permute-start(f32[96,128]{1,0:T(8,128)S(1)} %fusion.3), channel_id=1, source_target_pairs={{0,8},{1,9},{2,10},{3,11},{4,12},{5,13},{6,14},{7,15},{8,0},{9,1},... | collective-permute-start | bytes 147464 | tf_op jit(solution)/shard_map/ppermute | solution.py:85
  153.2 1.3 collective-permute-start.25
  155.5 6.2 %collective-permute-start.26 = (f32[3,32,128]{2,1,0:T(8,128)S(1)}, f32[3,32,128]{2,1,0:T(8,128)S(1)}, u32[]{:S(2)}, u32[]{:S(2)}) collective-permute-start(f32[3,32,128]{2,1,0:T(8,128)S(1)} %sketch.1.refs_0_), channel_id=1, source_target_pairs={{0,1},{1,0},{2,3},{3,2},{4,5},{5,4},{6,7},{7,6},{8,9},{9,8},{10,11... | collective-permute-start | bytes 147464 | tf_op jit(solution)/shard_map/ppermute | solution.py:85
  157.1 6.5 %collective-permute-start.27 = (f32[3,32,128]{2,1,0:T(8,128)S(1)}, f32[3,32,128]{2,1,0:T(8,128)S(1)}, u32[]{:S(2)}, u32[]{:S(2)}) collective-permute-start(f32[3,32,128]{2,1,0:T(8,128)S(1)} %sketch.1.refs_0_), channel_id=1, source_target_pairs={{0,2},{1,3},{2,0},{3,1},{4,6},{5,7},{6,4},{7,5},{8,10},{9,11},{10,... | collective-permute-start | bytes 147464 | tf_op jit(solution)/shard_map/ppermute | solution.py:85
  158.2 6.0 %collective-permute-start.28 = (f32[3,32,128]{2,1,0:T(8,128)S(1)}, f32[3,32,128]{2,1,0:T(8,128)S(1)}, u32[]{:S(2)}, u32[]{:S(2)}) collective-permute-start(f32[3,32,128]{2,1,0:T(8,128)S(1)} %sketch.1.refs_0_), channel_id=1, source_target_pairs={{0,3},{1,2},{2,1},{3,0},{4,7},{5,6},{6,5},{7,4},{8,11},{9,10},{10,... | collective-permute-start | bytes 147464 | tf_op jit(solution)/shard_map/ppermute | solution.py:85

commit v6 on v5

--- a/solution.py
+++ b/solution.py
@@ -99,23 +99,31 @@
     sems = refs.pop(0)
     step = pl.program_id(0)
 
+    def copies(n):
+        at, made = 0, []
+        for m, piece in enumerate(pieces[n]):
+            target = rows[n].at[:, pl.ds(at, piece.shape[1]), :]
+            made.append(pltpu.make_async_copy(piece, target, sems.at[2 * n + m]))
+            at += piece.shape[1]
+        return made
+
     @pl.when(step == 0)
     def _():
-        copies = []
         for n in range(count):
-            at = 0
-            for m, piece in enumerate(pieces[n]):
-                target = rows[n].at[:, pl.ds(at, piece.shape[1]), :]
-                copies.append(pltpu.make_async_copy(piece, target, sems.at[2 * n + m]))
-                at += piece.shape[1]
-        for copy in copies:
-            copy.start()
-        for copy in copies:
-            copy.wait()
+            for copy in copies(n):
+                copy.start()
+
+    def arrive(n):
+        @pl.when(step == 0)
+        def _():
+            for copy in copies(n):
+                copy.wait()
 
     def total(which):
         value = acc_in[step, which] if last else None
         for n in range(count):
+            if which == 0:
+                arrive(n)
             weight = down[n][...] if which == 2 else gate_up[n][which]
             part = lax.dot_general(
                 rows[n][1 if which == 2 else 0], weight, NT, preferred_element_type=jnp.float32

time: 169 us -> 173 us (1.024)
  Pallas kernels: 89.2 us -> 95.2 us
  waiting for transfers between devices: 49.7 us -> 44.4 us
  starting transfers between devices: 25.2 us -> 28.2 us
    pallas_call x4, Pallas kernels: 81.5 us -> 87.6 us  [matmul_step(): pl.pallas_call(functools.partial(matmul_kernel, count, last), out_shape=o...]
    ppermute x29, waiting for transfers between devices: 49.7 us -> 44.4 us  [send(): return lax.ppermute(value, BOTH, pairs)]
    ppermute x29, starting transfers between devices: 25.2 us -> 28.2 us  [send(): return lax.ppermute(value, BOTH, pairs)]
  transfers between devices with their start and end apart: 29 -> 29, of which waited for: 15 -> 16; matrix products, arithmetic and copies ran while one was open for 2% -> 2% of each run, Pallas kernels for 49% -> 52%
where the time goes in v6:
time: 173 us
  Pallas kernels  95.2 us (55%)
  waiting for transfers between devices  44.4 us (26%)
  starting transfers between devices  28.2 us (16%)
  matrix products  2.91 us (2%)
    pallas_call x4, Pallas kernels, matmul_step(): pl.pallas_call(functools.partial(matmul_kernel, count, last), out_shape=o...  87.6 us
    ppermute x29, waiting for transfers between devices, send(): return lax.ppermute(value, BOTH, pairs)  44.4 us
    ppermute x29, starting transfers between devices, send(): return lax.ppermute(value, BOTH, pairs)  28.2 us
    pallas_call x2, Pallas kernels, apply_precond(): pl.pallas_call(functools.partial(precond_kernel, flips), out_shape=jax.Sh...  6.58 us
  transfers between devices with their start and end apart: 29, of which 16 were waited for; matrix products, arithmetic and copies ran while one was open for 2% of the time, Pallas kernels for 52%

profile of v6, /device:TPU:0, one launch (start us, length us, event | category | flops | bytes accessed | tf_op | source)
XLA Modules:
  0.0 172.6 jit_solution(3193732759404121147)
XLA Ops:
  0.1 1.3 pad_maximum_fusion.refs_1_
  1.4 3.1 %collective-permute-start = (bf16[2,128,2048]{2,1,0:T(8,128)(2,1)S(1)}, bf16[2,128,2048]{2,1,0:T(8,128)(2,1)S(1)}, u32[]{:S(2)}, u32[]{:S(2)}) collective-permute-start(bf16[2,128,2048]{2,1,0:T(8,128)(2,1)S(1)} %pad_maximum_fusion.refs_1_), channel_id=1, source_target_pairs={{0,1},{1,0},{2,3},{3,2},{4,5},{5,4},{6,7},{7,6},{8,9},{9,8},{10,11... | collective-permute-start | bytes 3145736 | tf_op jit(solution)/shard_map/ppermute | solution.py:85
  4.5 0.7 collective-permute-start.1
  5.2 1.6 collective-permute-start.2
  6.8 1.4 convolution_bitcast_fusion.1
  8.2 1.5 convolution_bitcast_fusion
  9.7 0.6 collective-permute-start.4
  10.3 0.9 collective-permute-done.4
  11.2 16.4 %collective-permute-done.refs_2_ = bf16[2,128,2048]{2,1,0:T(8,128)(2,1)S(1)} collective-permute-done((bf16[2,128,2048]{2,1,0:T(8,128)(2,1)S(1)}, bf16[2,128,2048]{2,1,0:T(8,128)(2,1)S(1)}, u32[]{:S(2)}, u32[]{:S(2)}) %collective-permute-start) | collective-permute-done | bytes 1048608 | tf_op jit(solution)/shard_map/ppermute | solution.py:85
  27.6 2.2 %collective-permute-done.2.refs_1_ = bf16[2,128,2048]{2,1,0:T(8,128)(2,1)S(1)} collective-permute-done((bf16[2,128,2048]{2,1,0:T(8,128)(2,1)S(1)}, bf16[2,128,2048]{2,1,0:T(8,128)(2,1)S(1)}, u32[]{:S(2)}, u32[]{:S(2)}) %collective-permute-start.2) | collective-permute-done | bytes 1048608 | tf_op jit(solution)/shard_map/ppermute | solution.py:85
  29.9 0.9 collective-permute-start.6
  30.8 1.6 collective-permute-start.7
  32.4 1.3 collective-permute-start.5
  33.6 0.1 collective-permute-start.8
  33.8 20.1 %matmul.4.refs_9_ = f32[7,3,256,256]{3,2,1,0:T(8,128)S(1)} custom-call(s32[4]{0:T(128)S(1)} %pad_add_fusion.refs_0_.where_ref, bf16[2,128,2048]{2,1,0:T(8,128)(2,1)S(1)} %pad_maximum_fusion.refs_1_, bf16[2,128,2048]{2,1,0:T(8,128)(2,1)S(1)} %collective-permute-done.refs_2_, bf16[2,128,2048]{2,1,0:T(8,128)(2,1)S(1)} %collective-permute-done.3.refs_3_, ...), custom_call_target="tpu_custom_call" | custom-call | flops 11274289152 | bytes 44040192 | tf_op jit(solution)/shard_map/matmul/pallas_call | solution.py:196
  53.9 8.4 %collective-permute-done.5 = bf16[2,128,2048]{2,1,0:T(8,128)(2,1)S(1)} collective-permute-done((bf16[2,128,2048]{2,1,0:T(8,128)(2,1)S(1)}, bf16[2,128,2048]{2,1,0:T(8,128)(2,1)S(1)}, u32[]{:S(2)}, u32[]{:S(2)}) %collective-permute-start.5) | collective-permute-done | bytes 1048608 | tf_op jit(solution)/shard_map/ppermute | solution.py:85
  62.5 0.6 collective-permute-start.11
  63.0 0.2 collective-permute-start.12
  63.2 1.5 collective-permute-start.10
  64.7 1.6 collective-permute-start.14
  66.3 23.5 %matmul.5 = (f32[96,256]{1,0:T(8,128)S(1)}, f32[96,256]{1,0:T(8,128)S(1)}) custom-call(s32[4]{0:T(128)S(1)} %pad_add_fusion.refs_0_.where_ref, bf16[2,128,2048]{2,1,0:T(8,128)(2,1)S(1)} %collective-permute-done.2.refs_1_, bf16[2,128,2048]{2,1,0:T(8,128)(2,1)S(1)} %collective-permute-done.7.refs_2_, bf16[2,128,2048]{2,1,0:T(8,128)(2,1)S(1)} %collective-permute-done.8.refs_3_, ...), custom_call_target="tpu_custom_call" | custom-call | flops 11274289152 | bytes 44040192 | tf_op jit(solution)/shard_map/matmul/pallas_call | solution.py:196
  89.8 0.4 collective-permute-done.14
  90.2 0.3 collective-permute-done.10
  90.7 1.6 collective-permute-start.15
  92.3 0.2 collective-permute-start.16
  92.5 0.3 collective-permute-start.17
  92.9 0.5 collective-permute-done.18.refs_4_
  93.3 20.1 %matmul.6.refs_9_ = f32[7,3,256,256]{3,2,1,0:T(8,128)S(1)} custom-call(s32[4]{0:T(128)S(1)} %pad_add_fusion.refs_0_.where_ref, bf16[2,128,2048]{2,1,0:T(8,128)(2,1)S(1)} %broadcast_select_fusion.1.refs_1_, bf16[2,128,2048]{2,1,0:T(8,128)(2,1)S(1)} %broadcast_select_fusion.refs_2_, bf16[2,128,2048]{2,1,0:T(8,128)(2,1)S(1)} %collective-permute-done.12.refs_3_, ...), custom_call_target="tpu_custom_call" | custom-call | flops 11274289152 | bytes 44040192 | tf_op jit(solution)/shard_map/matmul/pallas_call | solution.py:196
  113.4 2.8 %collective-permute-done.15.refs_2_ = bf16[2,128,2048]{2,1,0:T(8,128)(2,1)S(1)} collective-permute-done((bf16[2,128,2048]{2,1,0:T(8,128)(2,1)S(1)}, bf16[2,128,2048]{2,1,0:T(8,128)(2,1)S(1)}, u32[]{:S(2)}, u32[]{:S(2)}) %collective-permute-start.15) | collective-permute-done | bytes 1048608 | tf_op jit(solution)/shard_map/ppermute | solution.py:85
  116.3 2.1 %collective-permute-start.19 = (f32[96,128]{1,0:T(8,128)S(1)}, f32[96,128]{1,0:T(8,128)S(1)}, u32[]{:S(2)}, u32[]{:S(2)}) collective-permute-start(f32[96,128]{1,0:T(8,128)S(1)} %slice.25), channel_id=1, source_target_pairs={{0,1},{1,0},{2,3},{3,2},{4,5},{5,4},{6,7},{7,6},{8,9},{9,8},{10,11... | collective-permute-start | bytes 147464 | tf_op jit(solution)/shard_map/ppermute | solution.py:85
  118.5 0.4 collective-permute-done.20.refs_4_
  118.9 23.9 %matmul.7 = (f32[96,256]{1,0:T(8,128)S(1)}, f32[96,256]{1,0:T(8,128)S(1)}) custom-call(s32[4]{0:T(128)S(1)} %pad_add_fusion.refs_0_.where_ref, bf16[2,128,2048]{2,1,0:T(8,128)(2,1)S(1)} %collective-permute-done.11.refs_1_, bf16[2,128,2048]{2,1,0:T(8,128)(2,1)S(1)} %collective-permute-done.15.refs_2_, ...), custom_call_target="tpu_custom_call" | custom-call | flops 11274289152 | bytes 44040192 | tf_op jit(solution)/shard_map/matmul/pallas_call | solution.py:196
  142.9 0.5 collective-permute-start.21
  143.4 0.9 collective-permute-done.21
  144.4 3.3 %collective-permute-start.22 = (f32[96,128]{1,0:T(8,128)S(1)}, f32[96,128]{1,0:T(8,128)S(1)}, u32[]{:S(2)}, u32[]{:S(2)}) collective-permute-start(f32[96,128]{1,0:T(8,128)S(1)} %get-tuple-element.85), channel_id=1, source_target_pairs={{0,2},{1,3},{2,0},{3,1},{4,6},{5,7},{6,4},{7,5},{8,10},{9,11},{10,... | collective-permute-start | bytes 147464 | tf_op jit(solution)/shard_map/ppermute | solution.py:85
  147.7 1.2 collective-permute-start.23
  148.9 2.3 %collective-permute-done.22 = f32[96,128]{1,0:T(8,128)S(1)} collective-permute-done((f32[96,128]{1,0:T(8,128)S(1)}, f32[96,128]{1,0:T(8,128)S(1)}, u32[]{:S(2)}, u32[]{:S(2)}) %collective-permute-start.22) | collective-permute-done | bytes 49184 | tf_op jit(solution)/shard_map/ppermute | solution.py:85
  151.2 2.4 %collective-permute-done.23 = f32[96,128]{1,0:T(8,128)S(1)} collective-permute-done((f32[96,128]{1,0:T(8,128)S(1)}, f32[96,128]{1,0:T(8,128)S(1)}, u32[]{:S(2)}, u32[]{:S(2)}) %collective-permute-start.23) | collective-permute-done | bytes 49184 | tf_op jit(solution)/shard_map/ppermute | solution.py:85
  153.6 0.6 collective-permute-start.24
  154.2 3.6 %collective-permute-done.24 = f32[96,128]{1,0:T(8,128)S(1)} collective-permute-done((f32[96,128]{1,0:T(8,128)S(1)}, f32[96,128]{1,0:T(8,128)S(1)}, u32[]{:S(2)}, u32[]{:S(2)}) %collective-permute-start.24) | collective-permute-done | bytes 49184 | tf_op jit(solution)/shard_map/ppermute | solution.py:85
  157.9 1.2 collective-permute-done.25.other_ref
  159.1 1.0 sketch.1.refs_0_
  160.1 1.8 %collective-permute-start.27 = (f32[3,32,128]{2,1,0:T(8,128)S(1)}, f32[3,32,128]{2,1,0:T(8,128)S(1)}, u32[]{:S(2)}, u32[]{:S(2)}) collective-permute-start(f32[3,32,128]{2,1,0:T(8,128)S(1)} %sketch.1.refs_0_), channel_id=1, source_target_pairs={{0,2},{1,3},{2,0},{3,1},{4,6},{5,7},{6,4},{7,5},{8,10},{9,11},{10,... | collective-permute-start | bytes 147464 | tf_op jit(solution)/shard_map/ppermute | solution.py:85
  161.9 2.6 %collective-permute-start.28 = (f32[3,32,128]{2,1,0:T(8,128)S(1)}, f32[3,32,128]{2,1,0:T(8,128)S(1)}, u32[]{:S(2)}, u32[]{:S(2)}) collective-permute-start(f32[3,32,128]{2,1,0:T(8,128)S(1)} %sketch.1.refs_0_), channel_id=1, source_target_pairs={{0,3},{1,2},{2,1},{3,0},{4,7},{5,6},{6,5},{7,4},{8,11},{9,10},{10,... | collective-permute-start | bytes 147464 | tf_op jit(solution)/shard_map/ppermute | solution.py:85
  164.5 1.8 %precond.2.refs_3_ = f32[3,1,256]{2,1,0:T(1,128)S(1)} custom-call(s32[1]{0:T(128)} %bitcast.4.row_ref, f32[3,256,4096]{2,1,0:T(8,128)S(1)} %bitcast.15, f32[3,32,128]{2,1,0:T(8,128)S(1)} %sketch.1.refs_0_), custom_call_target="tpu_custom_call" | custom-call | tf_op jit(solution)/shard_map/precond/pallas_call | solution.py:288
  166.4 0.8 collective-permute-done.27.refs_1_
  167.2 0.7 collective-permute-done.28.refs_2_
  167.9 4.8 %precond.3 = f32[3,4,256]{2,1,0:T(4,128)} custom-call(s32[1]{0:T(128)} %bitcast.4.row_ref, f32[3,256,4096]{2,1,0:T(8,128)S(1)} %bitcast.15, f32[3,32,128]{2,1,0:T(8,128)S(1)} %collective-permute-done.26.refs_0_, f32[3,32,128]{2,1,0:T(8,128)S(1)} %collective-permute-done.27.refs_1_, f32[3,32,128]{2,1,0:T(8,128)S(1)} %collective-permute-done.28.refs_2_, ...), custom_call_target="tpu_custom_call" | custom-call | tf_op jit(solution)/shard_map/precond/pallas_call | solution.py:288
  (41 shorter events, 0.7 us)
Async XLA Ops:
  1.4 26.2 %collective-permute-start = (bf16[2,128,2048]{2,1,0:T(8,128)(2,1)S(1)}, bf16[2,128,2048]{2,1,0:T(8,128)(2,1)S(1)}, u32[]{:S(2)}, u32[]{:S(2)}) collective-permute-start(bf16[2,128,2048]{2,1,0:T(8,128)(2,1)S(1)} %pad_maximum_fusion.refs_1_), channel_id=1, source_target_pairs={{0,1},{1,0},{2,3},{3,2},{4,5},{5,4},{6,7},{7,6},{8,9},{9,8},{10,11... | collective-permute-start | bytes 3145736 | tf_op jit(solution)/shard_map/ppermute | solution.py:85
  4.5 23.2 %collective-permute-start.1 = (bf16[2,128,2048]{2,1,0:T(8,128)(2,1)S(1)}, bf16[2,128,2048]{2,1,0:T(8,128)(2,1)S(1)}, u32[]{:S(2)}, u32[]{:S(2)}) collective-permute-start(bf16[2,128,2048]{2,1,0:T(8,128)(2,1)S(1)} %pad_maximum_fusion.refs_1_), channel_id=1, source_target_pairs={{1,2},{2,1},{5,6},{6,5},{9,10},{10,9},{13,14},{14,13},{17,18},{18,... | collective-permute-start | bytes 3145736 | tf_op jit(solution)/shard_map/ppermute | solution.py:85
  5.2 24.7 %collective-permute-start.2 = (bf16[2,128,2048]{2,1,0:T(8,128)(2,1)S(1)}, bf16[2,128,2048]{2,1,0:T(8,128)(2,1)S(1)}, u32[]{:S(2)}, u32[]{:S(2)}) collective-permute-start(bf16[2,128,2048]{2,1,0:T(8,128)(2,1)S(1)} %pad_maximum_fusion.refs_1_), channel_id=1, source_target_pairs={{0,8},{1,9},{2,10},{3,11},{4,12},{5,13},{6,14},{7,15},{8,0},{9,1},... | collective-permute-start | bytes 3145736 | tf_op jit(solution)/shard_map/ppermute | solution.py:85
  6.8 23.1 %collective-permute-start.3 = (bf16[2,128,2048]{2,1,0:T(8,128)(2,1)S(1)}, bf16[2,128,2048]{2,1,0:T(8,128)(2,1)S(1)}, u32[]{:S(2)}, u32[]{:S(2)}) collective-permute-start(bf16[2,128,2048]{2,1,0:T(8,128)(2,1)S(1)} %pad_maximum_fusion.refs_1_), channel_id=1, source_target_pairs={{0,4},{1,5},{2,6},{3,7},{4,0},{5,1},{6,2},{7,3},{8,12},{9,13},{10,... | collective-permute-start | bytes 3145736 | tf_op jit(solution)/shard_map/ppermute | solution.py:85
  9.7 1.5 collective-permute-start.4
  29.9 36.4 %copy-start = (bf16[1792,192]{0,1:T(8,128)(2,1)S(1)}, bf16[1792,192]{0,1:T(8,128)(2,1)}, u32[]{:S(2)}) copy-start(bf16[1792,192]{0,1:T(8,128)(2,1)} %param.12) | copy-start | bytes 2064388
  29.9 3.9 %collective-permute-start.9 = (bf16[2,128,2048]{2,1,0:T(8,128)(2,1)S(1)}, bf16[2,128,2048]{2,1,0:T(8,128)(2,1)S(1)}, u32[]{:S(2)}, u32[]{:S(2)}) collective-permute-start(bf16[2,128,2048]{2,1,0:T(8,128)(2,1)S(1)} %collective-permute-done.refs_2_), channel_id=1, source_target_pairs={{0,4},{1,5},{2,6},{3,7},{4,0},{5,1},{6,2},{7,3},{8,12},{9,13},{10,... | collective-permute-start | bytes 3145736 | tf_op jit(solution)/shard_map/ppermute | solution.py:85
  29.9 32.4 %collective-permute-start.6 = (bf16[2,128,2048]{2,1,0:T(8,128)(2,1)S(1)}, bf16[2,128,2048]{2,1,0:T(8,128)(2,1)S(1)}, u32[]{:S(2)}, u32[]{:S(2)}) collective-permute-start(bf16[2,128,2048]{2,1,0:T(8,128)(2,1)S(1)} %collective-permute-done.refs_2_), channel_id=1, source_target_pairs={{1,2},{2,1},{5,6},{6,5},{9,10},{10,9},{13,14},{14,13},{17,18},{18,... | collective-permute-start | bytes 3145736 | tf_op jit(solution)/shard_map/ppermute | solution.py:85
  30.8 31.5 %collective-permute-start.7 = (bf16[2,128,2048]{2,1,0:T(8,128)(2,1)S(1)}, bf16[2,128,2048]{2,1,0:T(8,128)(2,1)S(1)}, u32[]{:S(2)}, u32[]{:S(2)}) collective-permute-start(bf16[2,128,2048]{2,1,0:T(8,128)(2,1)S(1)} %collective-permute-done.refs_2_), channel_id=1, source_target_pairs={{0,8},{1,9},{2,10},{3,11},{4,12},{5,13},{6,14},{7,15},{8,0},{9,1},... | collective-permute-start | bytes 3145736 | tf_op jit(solution)/shard_map/ppermute | solution.py:85
  32.4 29.9 %collective-permute-start.5 = (bf16[2,128,2048]{2,1,0:T(8,128)(2,1)S(1)}, bf16[2,128,2048]{2,1,0:T(8,128)(2,1)S(1)}, u32[]{:S(2)}, u32[]{:S(2)}) collective-permute-start(bf16[2,128,2048]{2,1,0:T(8,128)(2,1)S(1)} %collective-permute-done.1), channel_id=1, source_target_pairs={{1,0},{2,3},{5,4},{6,7},{9,8},{10,11},{13,12},{14,15},{17,16},{18,... | collective-permute-start | bytes 3145736 | tf_op jit(solution)/shard_map/ppermute | solution.py:85
  33.6 28.6 %collective-permute-start.8 = (bf16[2,128,2048]{2,1,0:T(8,128)(2,1)S(1)}, bf16[2,128,2048]{2,1,0:T(8,128)(2,1)S(1)}, u32[]{:S(2)}, u32[]{:S(2)}) collective-permute-start(bf16[2,128,2048]{2,1,0:T(8,128)(2,1)S(1)} %collective-permute-done.2.refs_1_), channel_id=1, source_target_pairs={{0,4},{1,5},{2,6},{3,7},{4,0},{5,1},{6,2},{7,3},{8,12},{9,13},{10,... | collective-permute-start | bytes 3145736 | tf_op jit(solution)/shard_map/ppermute | solution.py:85
  62.3 4.0 %collective-permute-start.13 = (bf16[2,128,2048]{2,1,0:T(8,128)(2,1)S(1)}, bf16[2,128,2048]{2,1,0:T(8,128)(2,1)S(1)}, u32[]{:S(2)}, u32[]{:S(2)}) collective-permute-start(bf16[2,128,2048]{2,1,0:T(8,128)(2,1)S(1)} %collective-permute-done.7.refs_2_), channel_id=1, source_target_pairs={{0,4},{1,5},{2,6},{3,7},{4,0},{5,1},{6,2},{7,3},{8,12},{9,13},{10,... | collective-permute-start | bytes 3145736 | tf_op jit(solution)/shard_map/ppermute | solution.py:85
  62.5 27.7 %collective-permute-start.11 = (bf16[2,128,2048]{2,1,0:T(8,128)(2,1)S(1)}, bf16[2,128,2048]{2,1,0:T(8,128)(2,1)S(1)}, u32[]{:S(2)}, u32[]{:S(2)}) collective-permute-start(bf16[2,128,2048]{2,1,0:T(8,128)(2,1)S(1)} %broadcast_select_fusion.1.refs_1_), channel_id=1, source_target_pairs={{0,8},{1,9},{2,10},{3,11},{4,12},{5,13},{6,14},{7,15},{8,0},{9,1},... | collective-permute-start | bytes 3145736 | tf_op jit(solution)/shard_map/ppermute | solution.py:85
  63.0 27.2 %collective-permute-start.12 = (bf16[2,128,2048]{2,1,0:T(8,128)(2,1)S(1)}, bf16[2,128,2048]{2,1,0:T(8,128)(2,1)S(1)}, u32[]{:S(2)}, u32[]{:S(2)}) collective-permute-start(bf16[2,128,2048]{2,1,0:T(8,128)(2,1)S(1)} %broadcast_select_fusion.1.refs_1_), channel_id=1, source_target_pairs={{0,4},{1,5},{2,6},{3,7},{4,0},{5,1},{6,2},{7,3},{8,12},{9,13},{10,... | collective-permute-start | bytes 3145736 | tf_op jit(solution)/shard_map/ppermute | solution.py:85
  63.2 27.2 %collective-permute-start.10 = (bf16[2,128,2048]{2,1,0:T(8,128)(2,1)S(1)}, bf16[2,128,2048]{2,1,0:T(8,128)(2,1)S(1)}, u32[]{:S(2)}, u32[]{:S(2)}) collective-permute-start(bf16[2,128,2048]{2,1,0:T(8,128)(2,1)S(1)} %collective-permute-done.6), channel_id=1, source_target_pairs={{1,0},{2,3},{5,4},{6,7},{9,8},{10,11},{13,12},{14,15},{17,16},{18,... | collective-permute-start | bytes 3145736 | tf_op jit(solution)/shard_map/ppermute | solution.py:85
  64.7 25.5 %collective-permute-start.14 = (f32[192,128]{1,0:T(8,128)S(1)}, f32[192,128]{1,0:T(8,128)S(1)}, u32[]{:S(2)}, u32[]{:S(2)}) collective-permute-start(f32[192,128]{1,0:T(8,128)S(1)} %fusion.4), channel_id=1, source_target_pairs={{0,8},{1,9},{2,10},{3,11},{4,12},{5,13},{6,14},{7,15},{8,0},{9,1},... | collective-permute-start | bytes 294920 | tf_op jit(solution)/shard_map/ppermute | solution.py:85
  90.6 2.7 %collective-permute-start.18 = (bf16[2,128,2048]{2,1,0:T(8,128)(2,1)S(1)}, bf16[2,128,2048]{2,1,0:T(8,128)(2,1)S(1)}, u32[]{:S(2)}, u32[]{:S(2)}) collective-permute-start(bf16[2,128,2048]{2,1,0:T(8,128)(2,1)S(1)} %broadcast_select_fusion.refs_2_), channel_id=1, source_target_pairs={{0,4},{1,5},{2,6},{3,7},{4,0},{5,1},{6,2},{7,3},{8,12},{9,13},{10,... | collective-permute-start | bytes 3145736 | tf_op jit(solution)/shard_map/ppermute | solution.py:85
  90.7 25.6 %collective-permute-start.15 = (bf16[2,128,2048]{2,1,0:T(8,128)(2,1)S(1)}, bf16[2,128,2048]{2,1,0:T(8,128)(2,1)S(1)}, u32[]{:S(2)}, u32[]{:S(2)}) collective-permute-start(bf16[2,128,2048]{2,1,0:T(8,128)(2,1)S(1)} %broadcast_select_fusion.refs_2_), channel_id=1, source_target_pairs={{0,8},{1,9},{2,10},{3,11},{4,12},{5,13},{6,14},{7,15},{8,0},{9,1},... | collective-permute-start | bytes 3145736 | tf_op jit(solution)/shard_map/ppermute | solution.py:85
  92.3 24.0 %collective-permute-start.16 = (bf16[2,128,2048]{2,1,0:T(8,128)(2,1)S(1)}, bf16[2,128,2048]{2,1,0:T(8,128)(2,1)S(1)}, u32[]{:S(2)}, u32[]{:S(2)}) collective-permute-start(bf16[2,128,2048]{2,1,0:T(8,128)(2,1)S(1)} %collective-permute-done.11.refs_1_), channel_id=1, source_target_pairs={{0,4},{1,5},{2,6},{3,7},{4,0},{5,1},{6,2},{7,3},{8,12},{9,13},{10,... | collective-permute-start | bytes 3145736 | tf_op jit(solution)/shard_map/ppermute | solution.py:85
  92.5 20.9 %collective-permute-start.17 = (f32[96,256]{1,0:T(8,128)S(1)}, f32[96,256]{1,0:T(8,128)S(1)}, u32[]{:S(2)}, u32[]{:S(2)}) collective-permute-start(f32[96,256]{1,0:T(8,128)S(1)} %get-tuple-element.67), channel_id=1, source_target_pairs={{0,4},{1,5},{2,6},{3,7},{4,0},{5,1},{6,2},{7,3},{8,12},{9,13},{10,... | collective-permute-start | bytes 294920 | tf_op jit(solution)/shard_map/ppermute | solution.py:85
  116.3 2.7 %collective-permute-start.20 = (bf16[2,128,2048]{2,1,0:T(8,128)(2,1)S(1)}, bf16[2,128,2048]{2,1,0:T(8,128)(2,1)S(1)}, u32[]{:S(2)}, u32[]{:S(2)}) collective-permute-start(bf16[2,128,2048]{2,1,0:T(8,128)(2,1)S(1)} %collective-permute-done.15.refs_2_), channel_id=1, source_target_pairs={{0,4},{1,5},{2,6},{3,7},{4,0},{5,1},{6,2},{7,3},{8,12},{9,13},{10,... | collective-permute-start | bytes 3145736 | tf_op jit(solution)/shard_map/ppermute | solution.py:85
  116.3 48.2 %slice-start = ((s8[12582912]{0:T(1024)(128)(4,1)}), s8[4194304]{0:T(1024)(128)(4,1)S(1)}, s32[]{:S(2)}) async-start(s8[12582912]{0:T(1024)(128)(4,1)} %bitcast.14), calls=%async_computation | async-start | bytes 8388608
  116.3 48.2 %slice-start.1 = ((s8[12582912]{0:T(1024)(128)(4,1)}), s8[4194304]{0:T(1024)(128)(4,1)S(1)}, s32[]{:S(2)}) async-start(s8[12582912]{0:T(1024)(128)(4,1)} %bitcast.14), calls=%async_computation.1 | async-start | bytes 8388608
  116.3 48.2 %slice-start.2 = ((s8[12582912]{0:T(1024)(128)(4,1)}), s8[4194304]{0:T(1024)(128)(4,1)S(1)}, s32[]{:S(2)}) async-start(s8[12582912]{0:T(1024)(128)(4,1)} %bitcast.14), calls=%async_computation.2 | async-start | bytes 8388608
  116.3 26.5 %collective-permute-start.19 = (f32[96,128]{1,0:T(8,128)S(1)}, f32[96,128]{1,0:T(8,128)S(1)}, u32[]{:S(2)}, u32[]{:S(2)}) collective-permute-start(f32[96,128]{1,0:T(8,128)S(1)} %slice.25), channel_id=1, source_target_pairs={{0,1},{1,0},{2,3},{3,2},{4,5},{5,4},{6,7},{7,6},{8,9},{9,8},{10,11... | collective-permute-start | bytes 147464 | tf_op jit(solution)/shard_map/ppermute | solution.py:85
  142.9 1.5 collective-permute-start.21
  144.4 6.8 %collective-permute-start.22 = (f32[96,128]{1,0:T(8,128)S(1)}, f32[96,128]{1,0:T(8,128)S(1)}, u32[]{:S(2)}, u32[]{:S(2)}) collective-permute-start(f32[96,128]{1,0:T(8,128)S(1)} %get-tuple-element.85), channel_id=1, source_target_pairs={{0,2},{1,3},{2,0},{3,1},{4,6},{5,7},{6,4},{7,5},{8,10},{9,11},{10,... | collective-permute-start | bytes 147464 | tf_op jit(solution)/shard_map/ppermute | solution.py:85
  147.7 5.9 %collective-permute-start.23 = (f32[96,128]{1,0:T(8,128)S(1)}, f32[96,128]{1,0:T(8,128)S(1)}, u32[]{:S(2)}, u32[]{:S(2)}) collective-permute-start(f32[96,128]{1,0:T(8,128)S(1)} %get-tuple-element.86), channel_id=1, source_target_pairs={{0,3},{1,2},{2,1},{3,0},{4,7},{5,6},{6,5},{7,4},{8,11},{9,10},{10,... | collective-permute-start | bytes 147464 | tf_op jit(solution)/shard_map/ppermute | solution.py:85
  153.6 4.2 %collective-permute-start.24 = (f32[96,128]{1,0:T(8,128)S(1)}, f32[96,128]{1,0:T(8,128)S(1)}, u32[]{:S(2)}, u32[]{:S(2)}) collective-permute-start(f32[96,128]{1,0:T(8,128)S(1)} %fusion.3), channel_id=1, source_target_pairs={{0,8},{1,9},{2,10},{3,11},{4,12},{5,13},{6,14},{7,15},{8,0},{9,1},... | collective-permute-start | bytes 147464 | tf_op jit(solution)/shard_map/ppermute | solution.py:85
  157.8 1.3 collective-permute-start.25
  160.1 6.2 %collective-permute-start.26 = (f32[3,32,128]{2,1,0:T(8,128)S(1)}, f32[3,32,128]{2,1,0:T(8,128)S(1)}, u32[]{:S(2)}, u32[]{:S(2)}) collective-permute-start(f32[3,32,128]{2,1,0:T(8,128)S(1)} %sketch.1.refs_0_), channel_id=1, source_target_pairs={{0,1},{1,0},{2,3},{3,2},{4,5},{5,4},{6,7},{7,6},{8,9},{9,8},{10,11... | collective-permute-start | bytes 147464 | tf_op jit(solution)/shard_map/ppermute | solution.py:85
  160.1 7.0 %collective-permute-start.27 = (f32[3,32,128]{2,1,0:T(8,128)S(1)}, f32[3,32,128]{2,1,0:T(8,128)S(1)}, u32[]{:S(2)}, u32[]{:S(2)}) collective-permute-start(f32[3,32,128]{2,1,0:T(8,128)S(1)} %sketch.1.refs_0_), channel_id=1, source_target_pairs={{0,2},{1,3},{2,0},{3,1},{4,6},{5,7},{6,4},{7,5},{8,10},{9,11},{10,... | collective-permute-start | bytes 147464 | tf_op jit(solution)/shard_map/ppermute | solution.py:85
  161.9 5.9 %collective-permute-start.28 = (f32[3,32,128]{2,1,0:T(8,128)S(1)}, f32[3,32,128]{2,1,0:T(8,128)S(1)}, u32[]{:S(2)}, u32[]{:S(2)}) collective-permute-start(f32[3,32,128]{2,1,0:T(8,128)S(1)} %sketch.1.refs_0_), channel_id=1, source_target_pairs={{0,3},{1,2},{2,1},{3,0},{4,7},{5,6},{6,5},{7,4},{8,11},{9,10},{10,... | collective-permute-start | bytes 147464 | tf_op jit(solution)/shard_map/ppermute | solution.py:85
